TPU v7x, 256 devices: a whole 4x4x8 slice. The times are simulated.
256 devices in a mesh: rows: 32 (over z_hi, y, core), rep: 8 (over z_lo, x).
Axes of the slice: x: 4, y: 4, z: 8 (z_hi: 4, z_lo: 2; z = z_hi * 2 + z_lo), core: 2. Of those that a mesh axis runs over, the one named last changes fastest.
Arguments:
- features: bfloat16 [32768, 256], P('rows'), may hold values from -6 to 6
- inv_sqrt_degree: bfloat16 [32768], P('rows'), may hold values from 0.25 to 1
- weight: bfloat16 [256, 256], replicated, may hold values from -0.375 to 0.375
- tile_vals: bfloat16 [32, 1024, 128, 128], P('rows', 'rep'), may hold values from -0.046875 to 0.046875
- tile_row: int32 [32, 1024], P('rows', 'rep'), may hold values from 0 to 7, as said below
- tile_col: int32 [32, 1024], P('rows', 'rep'), may hold values from 0 to 31, as said below
- tile_count: int32 [32, 32], P('rows', 'rep'), may hold values from 0 to 64, as said below
- cotangent: bfloat16 [32768, 256], P('rows'), may hold values from -6 to 6
Outputs:
- activated: bfloat16 [32768, 256], P(('rows', 'rep'))
- weight_grad: float32 [256, 256], replicated
- feature_grad: bfloat16 [32768, 256], P(('rep', 'rows'))
Inputs may be any that keep to these rules, and one draw needn't show every extreme that they name: `tile_count`: each count is at most 64; the 4 counts of row block i and columns r * 4 .. r * 4 + 3 sum to at most 128. Some pair holds exactly 64 tiles and some block row and replica exactly 128, in every draw. `tile_row`: the valid slots of a block row and replica are ordered by column block, and inside one block pair their positions are distinct. A valid slot counted for column block r * 4 + s has tile_col between s * 8 and s * 8 + 7.
All inputs are finite; a program needn't handle non-finite values.
Results may differ from a plain program's by a relative error of at most 0.015.
Values may be sent and summed in bfloat16 or wider, within the bound.
No kernel may reach another device: no remote copies, remote signals or barrier semaphores. Data moves between devices by JAX's collectives and lax.ppermute only.
A program may use at most 128 MiB of HBM per device.

v0:
```python
import jax
import jax.numpy as jnp
from jax import lax
from jax.sharding import PartitionSpec as P


def from_root(shard, axis, root):
    mine = lax.axis_index(axis) == root
    return lax.psum(jnp.where(mine, shard, jnp.zeros_like(shard)), axis)


def tile_products(values, out_index, in_index, keep, source, out_tiles, flipped):
    count = values.shape[0]
    block_size = 32
    turns = count // block_size
    width = source.shape[-1]
    tile = values.shape[-1]

    def advance(carry, block):
        vals_block, out_block, in_block, keep_block = block
        picked = source[in_block]
        if flipped:
            prod = jnp.einsum(
                "kji,kjf->kif", vals_block, picked, preferred_element_type=jnp.float32
            )
        else:
            prod = jnp.einsum(
                "kij,kjf->kif", vals_block, picked, preferred_element_type=jnp.float32
            )
        prod = jnp.where(keep_block[:, None, None], prod, jnp.float32(0.0))
        return (carry.at[out_block].add(prod), None)

    blocks = (
        values.reshape(turns, block_size, tile, tile),
        out_index.reshape(turns, block_size),
        in_index.reshape(turns, block_size),
        keep.reshape(turns, block_size),
    )
    initial = jnp.zeros((out_tiles, tile, width), jnp.float32)
    result, _ = lax.scan(advance, initial, blocks)
    return result


def section_window(values, out_rows, in_cols, starts, ends, section, per_block):
    slots = values.shape[0]
    pair_slots = per_block * per_block
    first = jnp.clip(starts[section], 0, slots - pair_slots)
    index = first + jnp.arange(pair_slots, dtype=jnp.int32)
    keep = (index >= starts[section]) & (index < ends[section])
    vals_window = lax.dynamic_slice_in_dim(values, first, pair_slots, 0)
    rows_window = lax.dynamic_slice_in_dim(out_rows, first, pair_slots, 0)
    cols_window = lax.dynamic_slice_in_dim(in_cols, first, pair_slots, 0)
    cols_window = jnp.clip(cols_window - section * per_block, 0, per_block - 1)
    return (vals_window, rows_window, cols_window, keep)


def shards(features, inv_sqrt_degree, weight, tile_vals, tile_row, tile_col, tile_count, cotangent):
    rows_count = lax.axis_size("rows")
    rep_count = lax.axis_size("rep")
    sections = rows_count // rep_count
    replica = lax.axis_index("rep")
    block_row = lax.axis_index("rows")
    nodes_block, width = features.shape
    tile = tile_vals.shape[-1]
    per_block = nodes_block // tile
    share = nodes_block // rep_count
    values = tile_vals[0]
    out_rows = tile_row[0]
    in_cols = tile_col[0]
    counts = tile_count[0]
    degree = inv_sqrt_degree.astype(jnp.float32)[:, None]
    scaled = (degree * features.astype(jnp.float32)).astype(jnp.bfloat16)
    ends = jnp.cumsum(counts)
    starts = ends - counts
    grad_factor = float(nodes_block * rows_count) ** (-0.5)
    arrived = []
    forward_sum = jnp.zeros((per_block, tile, width), jnp.float32)
    for section in range(sections):
        root = replica * sections + section
        block_feats, block_degree = (
            from_root(scaled, "rows", root),
            from_root(inv_sqrt_degree, "rows", root),
        )
        arrived.append((block_feats, block_degree))
        vals_window, rows_window, cols_window, keep = section_window(
            values, out_rows, in_cols, starts, ends, section, per_block
        )
        source = block_feats.reshape(per_block, tile, width)
        forward_sum = forward_sum + tile_products(
            vals_window, rows_window, cols_window, keep, source, per_block, False
        )
    partial_rows = forward_sum.reshape(nodes_block, width)
    summed = lax.psum(partial_rows, "rep")
    propagated = (degree * (summed + scaled.astype(jnp.float32))).astype(jnp.bfloat16)
    preact = jnp.dot(propagated, weight, preferred_element_type=jnp.float32)
    gate = jax.nn.sigmoid(preact)
    activated_block = (preact * gate).astype(jnp.bfloat16)
    grad_pre = (cotangent.astype(jnp.float32) * gate * (1.0 + preact * (1.0 - gate))).astype(
        jnp.bfloat16
    )
    back = (degree * jnp.dot(grad_pre, weight.T, preferred_element_type=jnp.float32)).astype(
        jnp.bfloat16
    )
    activated = lax.dynamic_slice_in_dim(activated_block, replica * share, share, 0)
    prop_share = lax.dynamic_slice_in_dim(propagated, replica * share, share, 0)
    grad_share = lax.dynamic_slice_in_dim(grad_pre, replica * share, share, 0)
    local_grad = lax.dot_general(
        prop_share, grad_share, (((0,), (0,)), ((), ())), preferred_element_type=jnp.float32
    )
    weight_grad = lax.psum(local_grad * grad_factor, ("rows", "rep"))
    back_tiles = back.reshape(per_block, tile, width)
    pieces = []
    for section in range(sections):
        vals_window, rows_window, cols_window, keep = section_window(
            values, out_rows, in_cols, starts, ends, section, per_block
        )
        pieces.append(
            tile_products(vals_window, cols_window, rows_window, keep, back_tiles, per_block, True)
        )
    terms = jnp.stack(pieces).reshape(sections, nodes_block, width)
    own_section = block_row - replica * sections
    section_ids = jnp.arange(sections, dtype=jnp.int32)
    self_part = jnp.where(
        (section_ids == own_section)[:, None, None],
        back.astype(jnp.float32)[None, :, :],
        jnp.float32(0.0),
    )
    degrees = jnp.stack([pair[1] for pair in arrived]).astype(jnp.float32)
    terms = (terms + self_part) * degrees[:, :, None]
    feature_grad = lax.psum_scatter(
        terms.reshape(sections * nodes_block, width), "rows", scatter_dimension=0, tiled=True
    ).astype(jnp.bfloat16)
    return (activated, weight_grad, feature_grad)


def solution(mesh):
    placed = (
        P("rows", None),
        P("rows"),
        P(),
        P("rows", "rep", None, None),
        P("rows", "rep"),
        P("rows", "rep"),
        P("rows", "rep"),
        P("rows", None),
    )
    return jax.shard_map(
        shards,
        mesh=mesh,
        in_specs=placed,
        out_specs=(P(("rows", "rep"), None), P(), P(("rep", "rows"), None)),
        check_vma=False,
    )
```

profile of v0, /device:TPU:2, one launch (start us, length us, event | category | flops | bytes accessed | tf_op | source)
XLA Modules:
  0.0 1060.4 jit_solution(3447704333140686903)
XLA Ops:
  8.0 2.7 broadcast_select_fusion.2
  20.7 9.3 constant_dynamic-slice_fusion.23
  30.0 276.2 %all-reduce.10.cloned.1.call-done = (bf16[8,128,256]{2,1,0:T(8,128)(2,1)}, bf16[8,128,256]{2,1,0:T(8,128)(2,1)}, bf16[8,128,256]{2,1,0:T(8,128)(2,1)}, bf16[8,128,256]{2,1,0:T(8,128)(2,1)}) async-done(((bf16[8,128,256]{2,1,0:T(8,128)(2,1)}, bf16[8,128,256]{2,1,0:T(8,128)(2,1)}, bf16[8,128,256]{2,1,0:T(8,128)(2,1)}, bf16[8,128,256]{2,1,0:T(8,128)(2,1)}), (bf16[8,128,256]{2,1,0:T(8,128)(2,1)}, ...) | async-done | bytes 2097168 | tf_op jit(solution)/shard_map/psum | solution.py:9
  306.3 28.3 %while.83 = (s32[]{:T(128)}, f32[8,128,256]{2,1,0:T(8,128)S(1)}, s32[2,32]{1,0:T(2,128)S(1)}, pred[2,32]{1,0:T(4,128)(4,1)S(1)}, bf16[2,32,128,128]{3,2,1,0:T(8,...) while((s32[]{:T(128)}, f32[8,128,256]{2,1,0:T(8,128)S(1)}, ...), condition=%wide.region_16.17_spmd, body=%wide.region_14.16_spmd.sunk | while | flops 270533824 | bytes 24122440 | solution.py:40
  306.4 3.1 gather_fusion.3
  309.5 4.5 convolution_select_fusion.19
  314.0 6.5 scatter_fusion.3
  320.5 3.1 gather_fusion.3
  323.6 4.5 convolution_select_fusion.19
  328.2 6.5 scatter_fusion.3
  334.7 26.2 %while.82 = (s32[]{:T(128)}, f32[8,128,256]{2,1,0:T(8,128)S(1)}, s32[2,32]{1,0:T(2,128)S(1)}, pred[2,32]{1,0:T(4,128)(4,1)S(1)}, bf16[2,32,128,128]{3,2,1,0:T(8,...) while((s32[]{:T(128)}, f32[8,128,256]{2,1,0:T(8,128)S(1)}, ...), condition=%wide.region_12.13_spmd, body=%wide.region_10.12_spmd.sunk | while | flops 270533824 | bytes 24122440 | solution.py:40
  334.8 2.0 gather_fusion.2
  336.8 4.5 convolution_select_fusion.18
  341.4 6.5 scatter_fusion.2
  347.9 2.0 gather_fusion.2
  349.9 4.5 convolution_select_fusion.18
  354.5 6.5 scatter_fusion.2
  361.0 28.3 %while.80 = (s32[]{:T(128)}, f32[8,128,256]{2,1,0:T(8,128)S(1)}, s32[2,32]{1,0:T(2,128)S(1)}, pred[2,32]{1,0:T(4,128)(4,1)S(1)}, bf16[2,32,128,128]{3,2,1,0:T(8,...) while((s32[]{:T(128)}, f32[8,128,256]{2,1,0:T(8,128)S(1)}, ...), condition=%wide.region_4.5_spmd, body=%wide.region_2.4_spmd.sunk | while | flops 270533824 | bytes 24122440 | solution.py:40
  361.1 3.1 gather_fusion
  364.2 4.5 convolution_select_fusion.16
  368.7 6.5 scatter_fusion
  375.2 3.1 gather_fusion
  378.3 4.5 convolution_select_fusion.16
  382.8 6.4 scatter_fusion
  390.4 34.1 %while.81 = (s32[]{:T(128)}, f32[8,128,256]{2,1,0:T(8,128)}, s32[2,32]{1,0:T(2,128)S(1)}, pred[2,32]{1,0:T(4,128)(4,1)S(1)}, bf16[2,32,128,128]{3,2,1,0:T(8,128)...) while((s32[]{:T(128)}, f32[8,128,256]{2,1,0:T(8,128)}, s32[2,32]{1,0:T(2,128)S(1)}, ...), condition=%wide.region_8.9_spmd, body=%wide.region_6.8_spmd.sunk | while | flops 270533824 | bytes 24122440 | solution.py:40
  390.4 3.1 gather_fusion.1
  393.5 4.5 convolution_select_fusion.17
  398.0 9.5 scatter_fusion.1
  407.5 3.1 gather_fusion.1
  410.6 4.5 convolution_select_fusion.17
  415.1 9.4 scatter_fusion.1
  424.5 2.5 add_add_fusion
  427.1 4.2 copy.25
  431.3 2.9 copy.23
  434.2 4.2 copy.21
  438.4 2.9 copy.19
  441.5 144.2 %all-reduce = (bf16[1,1024,1]{1,2,0:T(2,128)(2,1)S(1)}, bf16[1,1024,1]{1,2,0:T(2,128)(2,1)S(1)}, bf16[1,1024,1]{1,2,0:T(2,128)(2,1)S(1)}, bf16[1,1024,1]{1,2,0:T(2,128)(2,1)S(1)}) all-reduce(bf16[1,1024,1]{1,2,0:T(2,128)(2,1)S(1)} %stack.41, bf16[1,1024,1]{1,2,0:T(2,128)(2,1)S(1)} %stack.40, ...), channel_id=1, replica_groups=mesh['rows'=32,'rep'=8] {'rows'}, use_global_device_ids=true, to_apply=%region_34.35 | all-reduce | flops 4096 | bytes 16384 | tf_op jit(solution)/shard_map/psum | solution.py:9
  590.5 26.1 %while.87 = (s32[]{:T(128)}, f32[8,128,256]{2,1,0:T(8,128)S(1)}, s32[2,32]{1,0:T(2,128)S(1)}, pred[2,32]{1,0:T(4,128)(4,1)S(1)}, bf16[2,32,128,128]{2,3,1,0:T(8,...) while((s32[]{:T(128)}, f32[8,128,256]{2,1,0:T(8,128)S(1)}, ...), condition=%wide.region_30.31_spmd, body=%wide.region_28.30_spmd.sunk | while | flops 270533824 | bytes 24122440 | solution.py:40
  590.5 2.0 gather_fusion.7
  592.6 4.5 convolution_select_fusion.23
  597.1 6.5 scatter_fusion.7
  603.6 2.0 gather_fusion.7
  605.7 4.5 convolution_select_fusion.23
  610.2 6.4 scatter_fusion.7
  616.7 26.1 %while.86 = (s32[]{:T(128)}, f32[8,128,256]{2,1,0:T(8,128)S(1)}, s32[2,32]{1,0:T(2,128)S(1)}, pred[2,32]{1,0:T(4,128)(4,1)S(1)}, bf16[2,32,128,128]{2,3,1,0:T(8,...) while((s32[]{:T(128)}, f32[8,128,256]{2,1,0:T(8,128)S(1)}, ...), condition=%wide.region_27.28_spmd, body=%wide.region_25.27_spmd.sunk | while | flops 270533824 | bytes 24122440 | solution.py:40
  616.8 2.0 gather_fusion.6
  618.8 4.5 convolution_select_fusion.22
  623.3 6.4 scatter_fusion.6
  629.8 2.0 gather_fusion.6
  631.8 4.5 convolution_select_fusion.22
  636.4 6.4 scatter_fusion.6
  644.1 28.2 %while.85 = (s32[]{:T(128)}, f32[8,128,256]{2,1,0:T(8,128)}, s32[2,32]{1,0:T(2,128)S(1)}, pred[2,32]{1,0:T(4,128)(4,1)S(1)}, bf16[2,32,128,128]{2,3,1,0:T(8,128)...) while((s32[]{:T(128)}, f32[8,128,256]{2,1,0:T(8,128)}, ...), condition=%wide.region_24.25_spmd, body=%wide.region_22.24_spmd.sunk | while | flops 270533824 | bytes 32511104 | solution.py:40
  646.1 4.6 convolution_select_fusion.21
  650.8 6.4 scatter_fusion.5
  660.2 4.6 convolution_select_fusion.21
  664.8 6.4 scatter_fusion.5
  672.3 26.1 %while.84 = (s32[]{:T(128)}, f32[8,128,256]{2,1,0:T(8,128)S(1)}, s32[2,32]{1,0:T(2,128)S(1)}, pred[2,32]{1,0:T(4,128)(4,1)S(1)}, bf16[2,32,128,128]{2,3,1,0:T(8,...) while((s32[]{:T(128)}, f32[8,128,256]{2,1,0:T(8,128)S(1)}, ...), condition=%wide.region_21.22_spmd, body=%wide.region_19.21_spmd.sunk | while | flops 270533824 | bytes 24122440 | solution.py:40
  674.4 4.5 convolution_select_fusion.20
  679.0 6.4 scatter_fusion.4
  687.4 4.5 convolution_select_fusion.20
  692.0 6.4 scatter_fusion.4
  700.5 2.8 fusion.57
  706.8 92.0 %reduce-scatter.2.cloned.1.call-done = f32[128,256]{1,0:T(8,128)} async-done(((f32[4096,256]{1,0:T(8,128)}), f32[128,256]{1,0:T(8,128)}) %reduce-scatter.2.cloned.1.call-update) | async-done | bytes 131088 | tf_op jit(solution)/shard_map/reduce_scatter | solution.py:130
  800.3 251.9 %all-reduce.8.cloned.1.call-done = f32[256,256]{1,0:T(8,128)} async-done(((f32[256,256]{1,0:T(8,128)}), f32[256,256]{1,0:T(8,128)}) %all-reduce.8.cloned.1.call-update) | async-done | bytes 262160 | tf_op jit(solution)/shard_map/psum | solution.py:110
  (141 shorter events, 34.9 us)
Async XLA Ops:
  7.2 580.1 %copy-start = (bf16[256,256]{1,0:T(8,128)(2,1)S(1)}, bf16[256,256]{1,0:T(8,128)(2,1)}, u32[]{:S(2)}) copy-start(bf16[256,256]{1,0:T(8,128)(2,1)} %param.26) | copy-start | bytes 393220
  7.2 299.0 %all-reduce.10.cloned.1.call-start = ((), (), s32[]{:S(2)}) async-start(), calls=%async_computation.4 | async-start | bytes 4194304 | tf_op jit(solution)/shard_map/psum | solution.py:9
  8.0 2.8 copy-start.16
  8.0 6.2 copy-start.11
  8.0 6.2 copy-start.12
  10.7 575.0 %all-reduce.6.cloned.1.call-start = ((), (), s32[]{:S(2)}) async-start(), calls=%async_computation.1 | async-start | bytes 2097152 | tf_op jit(solution)/shard_map/psum | solution.py:93
  306.3 28.4 %copy-start.5 = (bf16[8,128,256]{2,1,0:T(8,128)(2,1)S(1)}, bf16[8,128,256]{2,1,0:T(8,128)(2,1)}, u32[]{:S(2)}) copy-start(bf16[8,128,256]{2,1,0:T(8,128)(2,1)} %get-tuple-element.943) | copy-start | bytes 1572868
  389.3 1.1 copy-start.13
  427.0 371.7 %reduce-scatter.2.cloned.1.call-start = ((), (), s32[]{:S(2)}) async-start(), calls=%async_computation.3 | async-start | bytes 4325376 | tf_op jit(solution)/shard_map/reduce_scatter | solution.py:130
  427.1 4.2 copy-start.7
  434.2 4.2 copy-start.6
  438.4 147.4 %copy-start.9 = (bf16[1024,256]{1,0:T(8,128)(2,1)S(1)}, bf16[1024,256]{1,0:T(8,128)(2,1)}, u32[]{:S(2)}) copy-start(bf16[1024,256]{1,0:T(8,128)(2,1)} %param.24) | copy-start | bytes 1572868
  441.3 145.9 %copy-start.15 = (bf16[1024,256]{1,0:T(8,128)(2,1)S(1)}, bf16[1024,256]{1,0:T(8,128)(2,1)}, u32[]{:S(2)}) copy-start(bf16[1024,256]{1,0:T(8,128)(2,1)} %param.31) | copy-start | bytes 1572868
  587.3 1.8 copy-start.10
  642.8 1.3 copy-start.2
  644.0 28.4 %copy-start.14 = (pred[2,32]{1,0:T(4,128)(4,1)S(1)}, pred[2,32]{1,0:T(4,128)(4,1)}, u32[]{:S(2)}) copy-start(pred[2,32]{1,0:T(4,128)(4,1)} %copy-done.13) | copy-start | bytes 196
  646.1 4.6 copy-start.3
  657.2 1.0 copy-start.4
  660.2 4.6 copy-start.3
  671.3 1.0 copy-start.4
  698.4 2.0 copy-start.8
  703.3 350.5 %copy-start.1 = (bf16[256,256]{1,0:T(8,128)(2,1)S(1)}, bf16[256,256]{1,0:T(8,128)(2,1)}, u32[]{:S(2)}) copy-start(bf16[256,256]{1,0:T(8,128)(2,1)} %param.26) | copy-start | bytes 393220
  703.3 348.8 %all-reduce.8.cloned.1.call-start = ((), (), s32[]{:S(2)}) async-start(), calls=%async_computation.2 | async-start | bytes 524288 | tf_op jit(solution)/shard_map/psum | solution.py:110
Sparse Core Ops, SparseCore 0:
  10.9 295.2 all-reduce.9
  427.1 79.2 all-reduce.5
  703.5 95.2 reduce-scatter.1
  804.6 247.4 all-reduce.7
where the time goes:
time: 1060 us
  waiting for transfers between devices  620 us (58%)
  blocking collectives  144 us (14%)
  other arithmetic  130 us (12%)
  matrix products  77.6 us (7%)
  local copies, waits for them, and re-layouts  71 us (7%)
  between operations  16.7 us (2%)
    psum x1, waiting for transfers between devices, from_root(): return lax.psum(jnp.where(mine, shard, jnp.zeros_like(shard)), axis)  276 us
    psum x1, waiting for transfers between devices, shards(): weight_grad = lax.psum(local_grad * grad_factor, ('rows', 'rep'))  252 us
    psum x1, blocking collectives, from_root(): return lax.psum(jnp.where(mine, shard, jnp.zeros_like(shard)), axis)  144 us
    scatter-add x16, other arithmetic, advance(): return (carry.at[out_block].add(prod), None)  109 us
    reduce_scatter x1, waiting for transfers between devices, shards(): lax.psum_scatter(terms.reshape(sections * nodes_block, width), 'rows', sc...  92 us
    gather x16, local copies, waits for them, and re-layouts, advance(): picked = source[in_block]  38.8 us
    dot_general x8, matrix products, advance(): jnp.einsum('kji,kjf->kif', vals_block, picked, preferred_element_type=jnp...  36.5 us
    dot_general x8, matrix products, advance(): jnp.einsum('kij,kjf->kif', vals_block, picked, preferred_element_type=jnp...  36.3 us
  transfers between devices with their start and end apart: 4, of which 3 were waited for; matrix products, arithmetic and copies ran while one was open for 3% of the time, Pallas kernels for 0%

commit v1 on v0

v1 whole, which is shorter than its diff:
```python
import jax
import jax.numpy as jnp
from jax import lax
from jax.experimental import pallas as pl
from jax.experimental.pallas import tpu as pltpu
from jax.sharding import Mesh, PartitionSpec as P

ZH, Y, C, ZL, X = 4, 4, 2, 2, 4
ROWS = ("zh", "y", "c")
REP = ("zl", "x")
ALL = ROWS + REP
TILE = 128


def flat(zh, y, c, zl, x):
    return (((zh * Y + y) * C + c) * ZL + zl) * X + x


def chunk_route(m):
    pairs = []
    for j in range(ZH * Y * C):
        for k in range(ZL * X):
            r = j // 4
            source = j * (ZL * X) + k
            target = flat((j % 4) ^ m, k // 2, k % 2, r // X, r % X)
            pairs.append((source, target))
    return pairs


def assemble_body(count, row, pos, vals, own, other, sem):
    own[...] = jnp.zeros_like(own)
    other[...] = jnp.zeros_like(other)
    total = count[0]

    def place(k, into):
        at = pos[k] % 16
        return pltpu.make_async_copy(
            vals.at[k],
            into.at[pl.ds(pl.multiple_of(row[k] * TILE, TILE), TILE),
                    pl.ds(pl.multiple_of(at * TILE, TILE), TILE)],
            sem.at[k],
        )

    @pl.loop(0, total)
    def _(k):
        @pl.when(pos[k] < 16)
        def _():
            place(k, own).start()

        @pl.when(pos[k] >= 16)
        def _():
            place(k, other).start()

    @pl.loop(0, total)
    def _(k):
        place(k, own).wait()


def assemble(count, row, pos, vals, rows, cols):
    half = jax.ShapeDtypeStruct((rows, cols), jnp.bfloat16)
    smem = pl.BlockSpec(memory_space=pltpu.SMEM)
    whole = pl.BlockSpec(memory_space=pltpu.VMEM)
    return pl.pallas_call(
        assemble_body,
        out_shape=(half, half),
        in_specs=[smem, smem, smem, pl.BlockSpec(memory_space=pltpu.HBM)],
        out_specs=(whole, whole),
        scratch_shapes=[pltpu.SemaphoreType.DMA((vals.shape[0],))],
        name="assemble",
    )(count, row, pos, vals)


def shards(features, inv_sqrt_degree, weight, tile_vals, tile_row, tile_col, tile_count, cotangent):
    bf16, f32 = jnp.bfloat16, jnp.float32
    nodes_block, width = features.shape
    zh, core = lax.axis_index("zh"), lax.axis_index("c")
    replica = lax.axis_index(REP)
    share = nodes_block // (ZL * X)
    nodes = nodes_block * ZH * Y * C
    start = replica * share
    deg_bf = lax.dynamic_slice_in_dim(inv_sqrt_degree, start, share, 0)
    deg = deg_bf.astype(f32)[:, None]
    feats = lax.dynamic_slice_in_dim(features, start, share, 0)
    cot = lax.dynamic_slice_in_dim(cotangent, start, share, 0).astype(f32)
    scaled = (deg * feats.astype(f32)).astype(bf16)
    deg_rows = jnp.pad(deg_bf[None, :], ((0, 15), (0, width - share)))
    sent = [jnp.concatenate([scaled, deg_rows], 0), scaled, scaled, scaled]
    got = [lax.ppermute(sent[m], ALL, chunk_route(m)) for m in range(4)]

    section, sub = tile_col[0] // 8, tile_col[0] % 8
    pos = ((sub % 2) ^ core) * 16 + (sub // 2) * 4 + (section ^ zh)
    total = jnp.sum(tile_count[0]).reshape(1)
    own_a, other_a = assemble(
        total.astype(jnp.int32), tile_row[0], pos.astype(jnp.int32), tile_vals[0], nodes_block, Y * 4 * TILE
    )

    chunk_deg = got[0][share, :share].astype(f32)[:, None]
    piece = jnp.concatenate([got[0][:share], got[1], got[2], got[3]], 0)
    gathered = lax.all_to_all(jnp.broadcast_to(piece[None], (Y, 4 * share, width)), "y", 0, 0)
    own_x = gathered.reshape(Y * 4 * share, width)
    swap = [(0, 1), (1, 0)]
    other_x = lax.ppermute(own_x, "c", swap)
    partial = jnp.dot(own_a, own_x, preferred_element_type=f32) + jnp.dot(
        other_a, other_x, preferred_element_type=f32
    )
    parts = lax.all_to_all(partial.astype(bf16).reshape(ZL * X, share, width), REP, 0, 0)
    summed = jnp.sum(parts.astype(f32), 0)

    propagated = (deg * (summed + scaled.astype(f32))).astype(bf16)
    preact = jnp.dot(propagated, weight, preferred_element_type=f32)
    gate = jax.nn.sigmoid(preact)
    activated = (preact * gate).astype(bf16)
    grad_pre = (cot * gate * (1.0 + preact * (1.0 - gate))).astype(bf16)
    back = (
        deg * lax.dot_general(grad_pre, weight, (((1,), (1,)), ((), ())), preferred_element_type=f32)
    ).astype(bf16)
    local_grad = lax.dot_general(
        propagated, grad_pre, (((0,), (0,)), ((), ())), preferred_element_type=f32
    ) * (float(nodes) ** -0.5)

    slices = local_grad.astype(bf16).reshape(ZL * X, width // (ZL * X), width)
    both = jnp.concatenate([jnp.broadcast_to(back[None], (ZL * X, share, width)), slices], 1)
    both = lax.all_to_all(both, REP, 0, 0)
    back_block = both[:, :share].reshape(nodes_block, width)
    w_slice = jnp.sum(both[:, share:].astype(f32), 0)
    w_slice = w_slice + lax.ppermute(w_slice, "c", swap)

    def pull(a):
        return lax.dot_general(a, back_block, (((0,), (0,)), ((), ())), preferred_element_type=f32)

    other_g = lax.ppermute(pull(other_a).astype(bf16), "c", swap)
    col_sum = (pull(own_a) + other_g.astype(f32)).astype(bf16).reshape(Y, 4 * share, width)
    w_rows = w_slice.astype(bf16)
    both = lax.all_to_all(
        jnp.concatenate([col_sum, jnp.broadcast_to(w_rows[None], (Y,) + w_rows.shape)], 1), "y", 0, 0
    )
    both = jnp.sum(both.astype(f32), 0)
    chunks, w_rows = both[: 4 * share].reshape(4, share, width), both[4 * share :]
    w_sum = w_rows
    grad = chunks[0]
    for m in range(1, 4):
        pairs = [(i, i ^ m) for i in range(ZH)]
        payload = jnp.concatenate([chunks[m], w_rows], 0).astype(bf16)
        came = lax.ppermute(payload, "zh", pairs).astype(f32)
        grad = grad + came[:share]
        w_sum = w_sum + came[share:]
    own_back = lax.ppermute(back, ALL, chunk_route(0)).astype(f32)
    feature_grad = (chunk_deg * (grad + own_back)).astype(bf16)
    weight_grad = lax.all_to_all(jnp.broadcast_to(w_sum[None], (ZL * X,) + w_sum.shape), REP, 0, 0)
    return (activated, weight_grad.reshape(width, width), feature_grad)


def solution(mesh):
    fine = Mesh(mesh.devices.reshape(ZH, Y, C, ZL, X), ALL)
    placed = (
        P(ROWS, None),
        P(ROWS),
        P(),
        P(ROWS, REP, None, None),
        P(ROWS, REP),
        P(ROWS, REP),
        P(ROWS, REP),
        P(ROWS, None),
    )
    return jax.shard_map(
        shards,
        mesh=fine,
        in_specs=placed,
        out_specs=(P(ALL, None), P(), P(REP + ROWS, None)),
        check_vma=False,
    )
```

time: 1060 us -> 151 us (0.14)
  waiting for transfers between devices: 620 us -> 12.9 us
  other arithmetic: 130 us -> 5.02 us
  blocking collectives: 144 us -> 73.5 us
  local copies, waits for them, and re-layouts: 71 us -> 1.63 us
  matrix products: 77.6 us -> 9.65 us
  starting transfers between devices: 0.16 us -> 36.6 us
  between operations: 16.7 us -> 0.97 us
    psum x3 -> x0, waiting for transfers between devices: 528 us -> none  [the longest x1 276 us: from_root(): return lax.psum(jnp.where(mine, shard, jnp.zeros_like(shard)), axis)]
    psum x1 -> x0, blocking collectives: 144 us -> none  [from_root(): return lax.psum(jnp.where(mine, shard, jnp.zeros_like(shard)), axis)]
    scatter-add x16 -> x0, other arithmetic: 109 us -> none  [advance(): return (carry.at[out_block].add(prod), None)]
    reduce_scatter x1 -> x0, waiting for transfers between devices: 92 us -> none  [shards(): lax.psum_scatter(terms.reshape(sections * nodes_block, width), 'rows', sc...]
    all_to_all x0 -> x4, blocking collectives: none -> 73.5 us  [the longest x1 21.7 us: shards(): lax.all_to_all(partial.astype(bf16).reshape(ZL * X, share, width), REP, 0...]
    dot_general x19 -> x7, matrix products: 77.6 us -> 9.65 us  [the longest x1 3.59 us: shards(): jnp.dot(own_a, own_x, preferred_element_type=f32)]
    gather x16 -> x0, local copies, waits for them, and re-layouts: 38.8 us -> none  [advance(): picked = source[in_block]]
    ppermute x0 -> x11, starting transfers between devices: none -> 29.4 us  [the longest x4 19.9 us: shards(): got = [lax.ppermute(sent[m], ALL, chunk_route(m)) for m in range(4)]]
  transfers between devices with their start and end apart: 4 -> 12, of which waited for: 3 -> 6; matrix products, arithmetic and copies ran while one was open for 3% -> 4% of each run, Pallas kernels for 0% -> 5%
where the time goes in v1:
time: 151 us; the launch traced here: 148 us
  blocking collectives  73.5 us (49%)
  starting transfers between devices  36.6 us (24%)
  waiting for transfers between devices  12.9 us (9%)
  matrix products  9.65 us (6%)
  Pallas kernels  8.02 us (5%)
  other arithmetic  5.02 us (3%)
  local copies, waits for them, and re-layouts  1.63 us (1%)
    all_to_all x1, blocking collectives, shards(): lax.all_to_all(partial.astype(bf16).reshape(ZL * X, share, width), REP, 0...  21.7 us
    ppermute x4, starting transfers between devices, shards(): got = [lax.ppermute(sent[m], ALL, chunk_route(m)) for m in range(4)]  19.9 us
    all_to_all x1, blocking collectives, shards(): lax.all_to_all(jnp.concatenate([col_sum, jnp.broadcast_to(w_rows[None], (...  18.8 us
    all_to_all x1, blocking collectives, shards(): lax.all_to_all(jnp.broadcast_to(piece[None], (Y, 4 * share, width)), 'y',...  18.2 us
    all_to_all x1, blocking collectives, shards(): both = lax.all_to_all(both, REP, 0, 0)  14.8 us
    pallas_call x1, Pallas kernels, assemble(): pl.pallas_call(assemble_body, out_shape=(half, half), in_specs=[smem, sme...  8.02 us
    all_to_all x1, starting transfers between devices, shards(): lax.all_to_all(jnp.broadcast_to(w_sum[None], (ZL * X,) + w_sum.shape), RE...  7.17 us
    ppermute x3, starting transfers between devices, shards(): came = lax.ppermute(payload, 'zh', pairs).astype(f32)  6.89 us
  transfers between devices with their start and end apart: 12, of which 6 were waited for; matrix products, arithmetic and copies ran while one was open for 4% of the time, Pallas kernels for 5%

profile of v1, /device:TPU:2, one launch (start us, length us, event | category | flops | bytes accessed | tf_op | source)
XLA Modules:
  0.0 148.2 jit_solution(18332469933410856048)
XLA Ops:
  0.6 0.0 copy-start
  0.6 0.0 copy-start.4
  0.7 0.0 copy-start.1
  0.7 0.8 dynamic-slice_bitcast_fusion
  1.5 0.9 multiply_convert_fusion.3
  2.4 1.9 %collective-permute-start = (bf16[144,256]{1,0:T(8,128)(2,1)S(1)}, bf16[144,256]{1,0:T(8,128)(2,1)S(1)}, u32[]{:S(2)}, u32[]{:S(2)}) collective-permute-start(bf16[144,256]{1,0:T(8,128)(2,1)S(1)} %fusion.7), channel_id=1, source_target_pairs={{0,0},{1,8},{2,16},{3,24},{4,32},{5,40},{6,48},{7,56},{8,64},{9,72... | collective-permute-start | bytes 221192 | tf_op jit(solution)/shard_map/ppermute | solution.py:88
  4.3 11.3 %collective-permute-start.3 = (bf16[128,256]{1,0:T(8,128)(2,1)S(1)}, bf16[128,256]{1,0:T(8,128)(2,1)S(1)}, u32[]{:S(2)}, u32[]{:S(2)}) collective-permute-start(bf16[128,256]{1,0:T(8,128)(2,1)S(1)} %multiply_convert_fusion.3), channel_id=1, source_target_pairs={{0,192},{1,200},{2,208},{3,216},{4,224},{5,232},{6,240},{7,248},{8... | collective-permute-start | bytes 196616 | tf_op jit(solution)/shard_map/ppermute | solution.py:88
  15.7 0.8 collective-permute-start.2
  16.5 5.9 %collective-permute-start.1 = (bf16[128,256]{1,0:T(8,128)(2,1)S(1)}, bf16[128,256]{1,0:T(8,128)(2,1)S(1)}, u32[]{:S(2)}, u32[]{:S(2)}) collective-permute-start(bf16[128,256]{1,0:T(8,128)(2,1)S(1)} %multiply_convert_fusion.3), channel_id=1, source_target_pairs={{0,64},{1,72},{2,80},{3,88},{4,96},{5,104},{6,112},{7,120},{8,0},{... | collective-permute-start | bytes 196616 | tf_op jit(solution)/shard_map/ppermute | solution.py:88
  22.4 0.0 collective-permute-done
  22.4 0.0 collective-permute-done.3
  22.4 0.2 collective-permute-done.2
  22.6 1.7 %collective-permute-done.1 = bf16[128,256]{1,0:T(8,128)(2,1)S(1)} collective-permute-done((bf16[128,256]{1,0:T(8,128)(2,1)S(1)}, bf16[128,256]{1,0:T(8,128)(2,1)S(1)}, u32[]{:S(2)}, u32[]{:S(2)}) %collective-permute-start.1) | collective-permute-done | bytes 65568 | tf_op jit(solution)/shard_map/ppermute | solution.py:88
  24.3 0.1 broadcast_in_dim.11
  24.4 18.2 %all_to_all.25 = bf16[4,512,256]{2,1,0:T(8,128)(2,1)S(1)} all-to-all(bf16[4,512,256]{2,1,0:T(8,128)(2,1)S(1)} %broadcast_in_dim.11), channel_id=1, replica_groups=mesh['zh'=4,'y'=4,'c'=2,'zl'=2,'x'=4] {'y'}, dimensions={0} | all-to-all | bytes 2097152 | tf_op jit(solution)/shard_map/all_to_all | solution.py:99
  42.6 0.0 collective-permute-start.4
  42.6 0.0 copy-done.4
  42.6 0.6 reduce_sum.36
  43.2 0.0 copy-done.1
  43.2 0.5 fusion.11.pos
  43.8 8.0 %assemble.1 = (bf16[1024,2048]{1,0:T(8,128)(2,1)}, bf16[1024,2048]{1,0:T(8,128)(2,1)}) custom-call(s32[1]{0:T(128)} %bitcast.count, s32[128]{0:T(128)} %bitcast.52, s32[128]{0:T(128)} %fusion.11.pos, bf16[128,128,128]{2,1,0:T(8,128)(2,1)} %bitcast.43), custom_call_target="tpu_custom_call" | custom-call | tf_op jit(solution)/shard_map/assemble/pallas_call | solution.py:63
  51.8 0.0 copy-start.3
  51.8 3.6 %fusion.14 = f32[1024,256]{1,0:T(8,128)S(1)} fusion(bf16[1024,2048]{1,0:T(8,128)(2,1)} %get-tuple-element.5, bf16[2048,256]{1,0:T(8,128)(2,1)S(1)} %bitcast.45), kind=kOutput, calls=%fused_computation.55 | convolution fusion | flops 1073741824 | bytes 6291456 | tf_op jit(solution)/shard_map/dot_general | solution.py:103
  55.4 0.0 collective-permute-done.4
  55.4 0.0 copy-done.3
  55.4 1.3 fusion
  56.7 21.7 %all_to_all.26 = bf16[8,128,256]{2,1,0:T(8,128)(2,1)S(1)} all-to-all(bf16[8,128,256]{2,1,0:T(8,128)(2,1)S(1)} %bitcast.51), channel_id=1, replica_groups=mesh['zh'=4,'y'=4,'c'=2,'zl'=2,'x'=4] {'zl','x'}, dimensions={0} | all-to-all | bytes 1048576 | tf_op jit(solution)/shard_map/all_to_all | solution.py:106
  78.4 0.1 convert_reduce_fusion.1
  78.5 0.9 multiply_convert_fusion.2
  79.4 0.0 copy-done
  79.4 1.7 %multiply_convert_fusion = (bf16[128,256]{1,0:T(8,128)(2,1)S(1)}, bf16[128,256]{1,0:T(8,128)(2,1)}) fusion(bf16[1024,256]{1,0:T(8,128)(2,1)} %param.15, s32[]{:T(128)S(6)} %select_n.24, bf16[128,256]{1,0:T(8,128)(2,1)S(1)} %multiply_convert_fusion.2, bf16[256,256]{1,0:T(8,128)(2,1)S(1)} %copy-done), kind=kOutput, calls=%fused_computation.22 | convolution fusion | flops 17170432 | bytes 393220 | tf_op jit(solution)/shard_map/dot_general | solution.py:110
  81.1 0.2 fusion.2
  81.3 0.2 fusion.1
  81.6 14.8 %all_to_all.27 = bf16[8,160,256]{2,1,0:T(8,128)(2,1)S(1)} all-to-all(bf16[8,160,256]{2,1,0:T(8,128)(2,1)S(1)} %pad_maximum_fusion.1), channel_id=1, replica_groups=mesh['zh'=4,'y'=4,'c'=2,'zl'=2,'x'=4] {'zl','x'}, dimensions={0} | all-to-all | bytes 1310720 | tf_op jit(solution)/shard_map/all_to_all | solution.py:123
  96.5 0.0 copy-start.2
  96.5 1.3 convolution_convert_fusion
  97.8 0.1 collective-permute-start.5
  98.0 0.6 collective-permute-start.6
  98.5 2.1 %collective-permute-done.6 = f32[32,256]{1,0:T(8,128)S(1)} collective-permute-done((f32[32,256]{1,0:T(8,128)S(1)}, f32[32,256]{1,0:T(8,128)S(1)}, u32[]{:S(2)}, u32[]{:S(2)}) %collective-permute-start.6) | collective-permute-done | bytes 32800 | tf_op jit(solution)/shard_map/ppermute | solution.py:126
  100.6 0.0 collective-permute-done.5
  100.6 0.0 copy-done.2
  100.6 1.4 add_convert_fusion
  102.0 0.1 pad_maximum_fusion
  102.1 18.8 %all_to_all.28 = bf16[4,544,256]{2,1,0:T(8,128)(2,1)S(1)} all-to-all(bf16[4,544,256]{2,1,0:T(8,128)(2,1)S(1)} %pad_maximum_fusion), channel_id=1, replica_groups=mesh['zh'=4,'y'=4,'c'=2,'zl'=2,'x'=4] {'y'}, dimensions={0} | all-to-all | bytes 2228224 | tf_op jit(solution)/shard_map/all_to_all | solution.py:134
  120.9 0.2 convert_reduce_fusion
  121.1 3.2 %collective-permute-start.7 = (bf16[160,256]{1,0:T(8,128)(2,1)S(1)}, bf16[160,256]{1,0:T(8,128)(2,1)S(1)}, u32[]{:S(2)}, u32[]{:S(2)}) collective-permute-start(bf16[160,256]{1,0:T(8,128)(2,1)S(1)} %get-tuple-element.11), channel_id=1, source_target_pairs={{0,64},{64,0},{128,192},{192,128},{1,65},{65,1},{129,193},{193,129... | collective-permute-start | bytes 245768 | tf_op jit(solution)/shard_map/ppermute | solution.py:144
  124.3 2.7 %collective-permute-start.8 = (bf16[160,256]{1,0:T(8,128)(2,1)S(1)}, bf16[160,256]{1,0:T(8,128)(2,1)S(1)}, u32[]{:S(2)}, u32[]{:S(2)}) collective-permute-start(bf16[160,256]{1,0:T(8,128)(2,1)S(1)} %get-tuple-element.12), channel_id=1, source_target_pairs={{0,128},{64,192},{128,0},{192,64},{1,129},{65,193},{129,1},{193,65... | collective-permute-start | bytes 245768 | tf_op jit(solution)/shard_map/ppermute | solution.py:144
  127.0 1.0 collective-permute-start.9
  128.0 1.9 %collective-permute-start.10 = (bf16[128,256]{1,0:T(8,128)(2,1)S(1)}, bf16[128,256]{1,0:T(8,128)(2,1)S(1)}, u32[]{:S(2)}, u32[]{:S(2)}) collective-permute-start(bf16[128,256]{1,0:T(8,128)(2,1)S(1)} %fusion.2), channel_id=1, source_target_pairs={{0,0},{1,8},{2,16},{3,24},{4,32},{5,40},{6,48},{7,56},{8,64},{9,72... | collective-permute-start | bytes 196616 | tf_op jit(solution)/shard_map/ppermute | solution.py:147
  129.9 0.0 collective-permute-done.7
  130.0 3.5 %collective-permute-done.8 = bf16[160,256]{1,0:T(8,128)(2,1)S(1)} collective-permute-done((bf16[160,256]{1,0:T(8,128)(2,1)S(1)}, bf16[160,256]{1,0:T(8,128)(2,1)S(1)}, u32[]{:S(2)}, u32[]{:S(2)}) %collective-permute-start.8) | collective-permute-done | bytes 81952 | tf_op jit(solution)/shard_map/ppermute | solution.py:144
  133.5 0.7 collective-permute-done.9
  134.2 0.7 broadcast_in_dim.14
  134.9 7.2 %all-to-all-start.4 = ((f32[8,32,256]{2,1,0:T(8,128)}), f32[8,32,256]{2,1,0:T(8,128)S(1)}, u32[]{:S(2)}, u32[]{:S(2)}) async-start(f32[8,32,256]{2,1,0:T(8,128)} %broadcast_in_dim.14), calls=%async_computation.4 | async-start | bytes 524288 | tf_op jit(solution)/shard_map/all_to_all | solution.py:149
  142.1 0.0 collective-permute-done.10
  142.1 0.7 fusion.6
  142.8 4.7 %all-to-all-done.4 = f32[8,32,256]{2,1,0:T(8,128)S(1)} async-done(((f32[8,32,256]{2,1,0:T(8,128)}), f32[8,32,256]{2,1,0:T(8,128)S(1)}, u32[]{:S(2)}, u32[]{:S(2)}) %all-to-all-start.4) | async-done | bytes 262176 | tf_op jit(solution)/shard_map/all_to_all | solution.py:149
  147.5 0.7 copy.12
  (19 shorter events, 0.3 us)
Async XLA Ops:
  0.6 78.8 %copy-start = (bf16[256,256]{1,0:T(8,128)(2,1)S(1)}, bf16[256,256]{1,0:T(8,128)(2,1)}, u32[]{:S(2)}) copy-start(bf16[256,256]{1,0:T(8,128)(2,1)} %param.10) | copy-start | bytes 393220
  0.6 42.0 %copy-start.4 = (s32[1,4]{1,0:T(1,128)S(1)}, s32[1,4]{1,0:T(1,128)}, u32[]{:S(2)}) copy-start(s32[1,4]{1,0:T(1,128)} %param.14) | copy-start | bytes 52
  0.7 42.6 %copy-start.1 = (s32[1,128]{1,0:T(1,128)S(1)}, s32[1,128]{1,0:T(1,128)}, u32[]{:S(2)}) copy-start(s32[1,128]{1,0:T(1,128)} %param.13) | copy-start | bytes 1540
  2.4 19.9 %collective-permute-start = (bf16[144,256]{1,0:T(8,128)(2,1)S(1)}, bf16[144,256]{1,0:T(8,128)(2,1)S(1)}, u32[]{:S(2)}, u32[]{:S(2)}) collective-permute-start(bf16[144,256]{1,0:T(8,128)(2,1)S(1)} %fusion.7), channel_id=1, source_target_pairs={{0,0},{1,8},{2,16},{3,24},{4,32},{5,40},{6,48},{7,56},{8,64},{9,72... | collective-permute-start | bytes 221192 | tf_op jit(solution)/shard_map/ppermute | solution.py:88
  4.3 18.0 %collective-permute-start.3 = (bf16[128,256]{1,0:T(8,128)(2,1)S(1)}, bf16[128,256]{1,0:T(8,128)(2,1)S(1)}, u32[]{:S(2)}, u32[]{:S(2)}) collective-permute-start(bf16[128,256]{1,0:T(8,128)(2,1)S(1)} %multiply_convert_fusion.3), channel_id=1, source_target_pairs={{0,192},{1,200},{2,208},{3,216},{4,224},{5,232},{6,240},{7,248},{8... | collective-permute-start | bytes 196616 | tf_op jit(solution)/shard_map/ppermute | solution.py:88
  15.7 6.9 %collective-permute-start.2 = (bf16[128,256]{1,0:T(8,128)(2,1)S(1)}, bf16[128,256]{1,0:T(8,128)(2,1)S(1)}, u32[]{:S(2)}, u32[]{:S(2)}) collective-permute-start(bf16[128,256]{1,0:T(8,128)(2,1)S(1)} %multiply_convert_fusion.3), channel_id=1, source_target_pairs={{0,128},{1,136},{2,144},{3,152},{4,160},{5,168},{6,176},{7,184},{8... | collective-permute-start | bytes 196616 | tf_op jit(solution)/shard_map/ppermute | solution.py:88
  16.5 7.8 %collective-permute-start.1 = (bf16[128,256]{1,0:T(8,128)(2,1)S(1)}, bf16[128,256]{1,0:T(8,128)(2,1)S(1)}, u32[]{:S(2)}, u32[]{:S(2)}) collective-permute-start(bf16[128,256]{1,0:T(8,128)(2,1)S(1)} %multiply_convert_fusion.3), channel_id=1, source_target_pairs={{0,64},{1,72},{2,80},{3,88},{4,96},{5,104},{6,112},{7,120},{8,0},{... | collective-permute-start | bytes 196616 | tf_op jit(solution)/shard_map/ppermute | solution.py:88
  42.6 12.8 %collective-permute-start.4 = (bf16[2048,256]{1,0:T(8,128)(2,1)S(1)}, bf16[2048,256]{1,0:T(8,128)(2,1)S(1)}, u32[]{:S(2)}, u32[]{:S(2)}) collective-permute-start(bf16[2048,256]{1,0:T(8,128)(2,1)S(1)} %bitcast.44), channel_id=1, source_target_pairs={{0,8},{8,0},{1,9},{9,1},{2,10},{10,2},{3,11},{11,3},{4,12},{12,4},... | collective-permute-start | bytes 3145736 | tf_op jit(solution)/shard_map/ppermute | solution.py:102
  51.8 3.6 %copy-start.3 = (bf16[1024,2048]{1,0:T(8,128)(2,1)S(1)}, bf16[1024,2048]{1,0:T(8,128)(2,1)}, u32[]{:S(2)}) copy-start(bf16[1024,2048]{1,0:T(8,128)(2,1)} %get-tuple-element.6) | copy-start | bytes 12582916
  96.5 4.2 %copy-start.2 = (bf16[1024,2048]{1,0:T(8,128)(2,1)S(1)}, bf16[1024,2048]{1,0:T(8,128)(2,1)}, u32[]{:S(2)}) copy-start(bf16[1024,2048]{1,0:T(8,128)(2,1)} %get-tuple-element.5) | copy-start | bytes 12582916
  97.8 2.8 %collective-permute-start.5 = (bf16[2048,256]{1,0:T(8,128)(2,1)S(1)}, bf16[2048,256]{1,0:T(8,128)(2,1)S(1)}, u32[]{:S(2)}, u32[]{:S(2)}) collective-permute-start(bf16[2048,256]{1,0:T(8,128)(2,1)S(1)} %convolution_convert_fusion), channel_id=1, source_target_pairs={{0,8},{8,0},{1,9},{9,1},{2,10},{10,2},{3,11},{11,3},{4,12},{12,4},... | collective-permute-start | bytes 3145736 | tf_op jit(solution)/shard_map/ppermute | solution.py:131
  98.0 2.7 %collective-permute-start.6 = (f32[32,256]{1,0:T(8,128)S(1)}, f32[32,256]{1,0:T(8,128)S(1)}, u32[]{:S(2)}, u32[]{:S(2)}) collective-permute-start(f32[32,256]{1,0:T(8,128)S(1)} %convert_reduce_fusion.2), channel_id=1, source_target_pairs={{0,8},{8,0},{1,9},{9,1},{2,10},{10,2},{3,11},{11,3},{4,12},{12,4},... | collective-permute-start | bytes 98312 | tf_op jit(solution)/shard_map/ppermute | solution.py:126
  121.1 8.8 %collective-permute-start.7 = (bf16[160,256]{1,0:T(8,128)(2,1)S(1)}, bf16[160,256]{1,0:T(8,128)(2,1)S(1)}, u32[]{:S(2)}, u32[]{:S(2)}) collective-permute-start(bf16[160,256]{1,0:T(8,128)(2,1)S(1)} %get-tuple-element.11), channel_id=1, source_target_pairs={{0,64},{64,0},{128,192},{192,128},{1,65},{65,1},{129,193},{193,129... | collective-permute-start | bytes 245768 | tf_op jit(solution)/shard_map/ppermute | solution.py:144
  124.3 9.1 %collective-permute-start.8 = (bf16[160,256]{1,0:T(8,128)(2,1)S(1)}, bf16[160,256]{1,0:T(8,128)(2,1)S(1)}, u32[]{:S(2)}, u32[]{:S(2)}) collective-permute-start(bf16[160,256]{1,0:T(8,128)(2,1)S(1)} %get-tuple-element.12), channel_id=1, source_target_pairs={{0,128},{64,192},{128,0},{192,64},{1,129},{65,193},{129,1},{193,65... | collective-permute-start | bytes 245768 | tf_op jit(solution)/shard_map/ppermute | solution.py:144
  127.0 7.2 %collective-permute-start.9 = (bf16[160,256]{1,0:T(8,128)(2,1)S(1)}, bf16[160,256]{1,0:T(8,128)(2,1)S(1)}, u32[]{:S(2)}, u32[]{:S(2)}) collective-permute-start(bf16[160,256]{1,0:T(8,128)(2,1)S(1)} %concatenate.30), channel_id=1, source_target_pairs={{0,192},{64,128},{128,64},{192,0},{1,193},{65,129},{129,65},{193,1... | collective-permute-start | bytes 245768 | tf_op jit(solution)/shard_map/ppermute | solution.py:144
  128.0 14.1 %collective-permute-start.10 = (bf16[128,256]{1,0:T(8,128)(2,1)S(1)}, bf16[128,256]{1,0:T(8,128)(2,1)S(1)}, u32[]{:S(2)}, u32[]{:S(2)}) collective-permute-start(bf16[128,256]{1,0:T(8,128)(2,1)S(1)} %fusion.2), channel_id=1, source_target_pairs={{0,0},{1,8},{2,16},{3,24},{4,32},{5,40},{6,48},{7,56},{8,64},{9,72... | collective-permute-start | bytes 196616 | tf_op jit(solution)/shard_map/ppermute | solution.py:147
  134.9 12.6 %all-to-all-start.4 = ((f32[8,32,256]{2,1,0:T(8,128)}), f32[8,32,256]{2,1,0:T(8,128)S(1)}, u32[]{:S(2)}, u32[]{:S(2)}) async-start(f32[8,32,256]{2,1,0:T(8,128)} %broadcast_in_dim.14), calls=%async_computation.4 | async-start | bytes 524288 | tf_op jit(solution)/shard_map/all_to_all | solution.py:149

commit v2 on v1

v2 whole, which is shorter than its diff:
```python
import jax
import jax.numpy as jnp
from jax import lax
from jax.experimental import pallas as pl
from jax.experimental.pallas import tpu as pltpu
from jax.sharding import Mesh, PartitionSpec as P

ZH, Y, C, ZL, X = 4, 4, 2, 2, 4
ROWS = ("zh", "y", "c")
REP = ("zl", "x")
ALL = ROWS + REP
TILE = 128


def flat(zh, y, c, zl, x):
    return (((zh * Y + y) * C + c) * ZL + zl) * X + x


def piece_route():
    pairs = []
    for j in range(ZH * Y * C):
        for k in range(ZL * X):
            zl, x = k // X, k % X
            r = j // 4
            pairs.append((j * (ZL * X) + k, flat(zl * 2 + x % 2, j % 4, x // 2, r // X, r % X)))
    return pairs


def share_route():
    pairs = []
    for j in range(ZH * Y * C):
        for k in range(ZL * X):
            r = j // 4
            pairs.append((j * (ZL * X) + k, flat(j % 4, k // 2, k % 2, r // X, r % X)))
    return pairs


def assemble_body(count, core, row, col, vals, own, other, sem):
    own[...] = jnp.zeros_like(own)
    other[...] = jnp.zeros_like(other)
    total = count[0, 0] + count[0, 1] + count[0, 2] + count[0, 3]

    @pl.loop(0, total)
    def _(k):
        at = col[0, k]
        sub = at % 8
        slot = (sub % 2) ^ core[0]
        place = (at // 8) * 4 + sub // 2
        down = pl.ds(pl.multiple_of(row[0, k] * TILE, TILE), TILE)
        across = pl.ds(pl.multiple_of(place * TILE, TILE), TILE)

        @pl.when(slot == 0)
        def _():
            pltpu.make_async_copy(vals.at[0, k], own.at[down, across], sem.at[k]).start()

        @pl.when(slot != 0)
        def _():
            pltpu.make_async_copy(vals.at[0, k], other.at[down, across], sem.at[k]).start()

    @pl.loop(0, total)
    def _(k):
        pltpu.make_async_copy(vals.at[0, k], own.at[pl.ds(0, TILE), pl.ds(0, TILE)], sem.at[k]).wait()


def assemble(count, core, row, col, vals, rows, cols):
    half = jax.ShapeDtypeStruct((rows, cols), jnp.bfloat16)
    smem = pl.BlockSpec(memory_space=pltpu.SMEM)
    whole = pl.BlockSpec(memory_space=pltpu.VMEM)
    return pl.pallas_call(
        assemble_body,
        out_shape=(half, half),
        in_specs=[smem, smem, smem, smem, pl.BlockSpec(memory_space=pltpu.HBM)],
        out_specs=(whole, whole),
        scratch_shapes=[pltpu.SemaphoreType.DMA((vals.shape[1],))],
        name="assemble",
    )(count, core, row, col, vals)


def shards(features, inv_sqrt_degree, weight, tile_vals, tile_row, tile_col, tile_count, cotangent):
    bf16, f32 = jnp.bfloat16, jnp.float32
    nodes_block, width = features.shape
    zh, core = lax.axis_index("zh"), lax.axis_index("c")
    replica = lax.axis_index(REP)
    reps = ZL * X
    share = nodes_block // reps
    nodes = nodes_block * ZH * Y * C
    half = lax.axis_index("x") // 2
    piece_rows = 4 * share
    feats = lax.dynamic_index_in_dim(features.reshape(4, 2, share, width), half, 1, False)
    degs = lax.dynamic_index_in_dim(inv_sqrt_degree.reshape(4, 2, share), half, 1, False)
    piece = (feats.astype(f32) * degs.astype(f32)[:, :, None]).astype(bf16).reshape(piece_rows, width)
    piece = lax.ppermute(piece, ALL, piece_route())

    own_a, other_a = assemble(
        tile_count, core.reshape(1), tile_row, tile_col, tile_vals, nodes_block, Y * piece_rows
    )
    start = replica * share
    deg_bf = lax.dynamic_slice_in_dim(inv_sqrt_degree, start, share, 0)
    deg_rows = jnp.pad(deg_bf[None, :], ((0, 15), (0, width - share)))
    deg = deg_bf.astype(f32)[:, None]
    scaled = (deg * lax.dynamic_slice_in_dim(features, start, share, 0).astype(f32)).astype(bf16)
    cot = lax.dynamic_slice_in_dim(cotangent, start, share, 0).astype(f32)
    piece, own_a, other_a, scaled, cot, deg_rows = lax.optimization_barrier(
        (piece, own_a, other_a, scaled, cot, deg_rows)
    )

    gathered = lax.all_to_all(jnp.broadcast_to(piece[None], (Y,) + piece.shape), "y", 0, 0)
    own_x = gathered.reshape(Y * piece_rows, width)
    swap = [(0, 1), (1, 0)]
    other_x = lax.ppermute(own_x, "c", swap)
    partial = jnp.dot(own_a, own_x, preferred_element_type=f32) + jnp.dot(
        other_a, other_x, preferred_element_type=f32
    )
    parts = lax.all_to_all(partial.astype(bf16).reshape(reps, share, width), REP, 0, 0)
    summed = jnp.sum(parts.astype(f32), 0)

    propagated = (deg * (summed + scaled.astype(f32))).astype(bf16)
    preact = jnp.dot(propagated, weight, preferred_element_type=f32)
    gate = jax.nn.sigmoid(preact)
    activated = (preact * gate).astype(bf16)
    grad_pre = (cot * gate * (1.0 + preact * (1.0 - gate))).astype(bf16)
    back = (
        deg * lax.dot_general(grad_pre, weight, (((1,), (1,)), ((), ())), preferred_element_type=f32)
    ).astype(bf16)
    local_grad = lax.dot_general(
        propagated, grad_pre, (((0,), (0,)), ((), ())), preferred_element_type=f32
    ) * (float(nodes) ** -0.5)

    back_sent = lax.ppermute(jnp.concatenate([back, deg_rows], 0), ALL, share_route())

    slices = local_grad.astype(bf16).reshape(reps, width // reps, width)
    both = jnp.concatenate([jnp.broadcast_to(back[None], (reps, share, width)), slices], 1)
    both = lax.all_to_all(both, REP, 0, 0)
    back_block = both[:, :share].reshape(nodes_block, width)
    w_slice = jnp.sum(both[:, share:].astype(f32), 0)
    w_slice = w_slice + lax.ppermute(w_slice, "c", swap)

    def pull(a):
        return lax.dot_general(a, back_block, (((0,), (0,)), ((), ())), preferred_element_type=f32)

    other_g = lax.ppermute(pull(other_a).astype(bf16), "c", swap)
    col_sum = (pull(own_a) + other_g.astype(f32)).astype(bf16)
    col_sum, back_sent = lax.optimization_barrier((col_sum, back_sent))
    col_sum = col_sum.reshape(4, 4, share, width).transpose(1, 0, 2, 3).reshape(Y, piece_rows, width)
    w_rows = w_slice.astype(bf16)
    both = lax.all_to_all(
        jnp.concatenate([col_sum, jnp.broadcast_to(w_rows[None], (Y,) + w_rows.shape)], 1), "y", 0, 0
    )
    both = jnp.sum(both.astype(f32), 0)
    chunks, w_rows = both[:piece_rows].reshape(4, share, width), both[piece_rows:]
    w_sum = w_rows
    grad = lax.dynamic_index_in_dim(chunks, zh, 0, False)
    for m in range(1, 4):
        pairs = [(i, i ^ m) for i in range(ZH)]
        chunk = lax.dynamic_index_in_dim(chunks, zh ^ m, 0, False)
        payload = jnp.concatenate([chunk, w_rows], 0).astype(bf16)
        came = lax.ppermute(payload, "zh", pairs).astype(f32)
        grad = grad + came[:share]
        w_sum = w_sum + came[share:]
    own_back = back_sent[:share].astype(f32)
    chunk_deg = back_sent[share, :share].astype(f32)[:, None]
    feature_grad = (chunk_deg * (grad + own_back)).astype(bf16)
    weight_grad = lax.all_to_all(jnp.broadcast_to(w_sum[None], (reps,) + w_sum.shape), REP, 0, 0)
    return (activated, weight_grad.reshape(width, width), feature_grad)


def solution(mesh):
    fine = Mesh(mesh.devices.reshape(ZH, Y, C, ZL, X), ALL)
    placed = (
        P(ROWS, None),
        P(ROWS),
        P(),
        P(ROWS, REP, None, None),
        P(ROWS, REP),
        P(ROWS, REP),
        P(ROWS, REP),
        P(ROWS, None),
    )
    return jax.shard_map(
        shards,
        mesh=fine,
        in_specs=placed,
        out_specs=(P(ALL, None), P(), P(REP + ROWS, None)),
        check_vma=False,
    )
```

time: 151 us -> 142 us (0.940); the launches traced: 148 us -> 141 us
  blocking collectives: 73.5 us -> 51.2 us
  waiting for transfers between devices: 12.9 us -> 33.6 us
  starting transfers between devices: 36.6 us -> 29.6 us
    all_to_all x3 -> x2, blocking collectives: 58.7 us -> 37 us  [the longest x1 19.9 us: shards(): lax.all_to_all(jnp.broadcast_to(piece[None], (Y,) + piece.shape), 'y', 0, 0)]
    all_to_all x1 -> x2, waiting for transfers between devices: 4.69 us -> 20.3 us  [the longest x1 15.6 us: shards(): lax.all_to_all(jnp.concatenate([col_sum, jnp.broadcast_to(w_rows[None], (...]
    ppermute x5 -> x2, starting transfers between devices: 21.8 us -> 8.21 us  [the longest x1 5.15 us: shards(): piece = lax.ppermute(piece, ALL, piece_route())]
    all_to_all x1 -> x2, starting transfers between devices: 7.17 us -> 10.8 us  [the longest x1 7.3 us: shards(): lax.all_to_all(jnp.broadcast_to(w_sum[None], (reps,) + w_sum.shape), REP,...]
    ppermute x3, starting transfers between devices: 6.89 us -> 9.79 us  [shards(): came = lax.ppermute(payload, 'zh', pairs).astype(f32)]
    ppermute x5 -> x2, waiting for transfers between devices: 1.89 us -> 4.72 us  [the longest x1 4.72 us: shards(): lax.ppermute(jnp.concatenate([back, deg_rows], 0), ALL, share_route())]
    ppermute x1, waiting for transfers between devices: 0.01 us -> 2.54 us  [shards(): other_x = lax.ppermute(own_x, 'c', swap)]
    dot_general x1, matrix products: 3.59 us -> 1.25 us  [shards(): jnp.dot(own_a, own_x, preferred_element_type=f32)]
  transfers between devices with their start and end apart: 12 -> 10, of which waited for: 6 -> 6; matrix products, arithmetic and copies ran while one was open for 4% -> 3% of each run, Pallas kernels for 5% -> 6%
where the time goes in v2:
time: 142 us; the launch traced here: 141 us
  blocking collectives  51.2 us (36%)
  waiting for transfers between devices  33.6 us (24%)
  starting transfers between devices  29.6 us (21%)
  Pallas kernels  8.8 us (6%)
  matrix products  8.71 us (6%)
  other arithmetic  5.63 us (4%)
  local copies, waits for them, and re-layouts  2.75 us (2%)
    all_to_all x1, blocking collectives, shards(): lax.all_to_all(jnp.broadcast_to(piece[None], (Y,) + piece.shape), 'y', 0, 0)  19.9 us
    all_to_all x1, blocking collectives, shards(): lax.all_to_all(partial.astype(bf16).reshape(reps, share, width), REP, 0, 0)  17 us
    all_to_all x1, waiting for transfers between devices, shards(): lax.all_to_all(jnp.concatenate([col_sum, jnp.broadcast_to(w_rows[None], (...  15.6 us
    all_to_all x1, blocking collectives, shards(): both = lax.all_to_all(both, REP, 0, 0)  14.2 us
    ppermute x3, starting transfers between devices, shards(): came = lax.ppermute(payload, 'zh', pairs).astype(f32)  9.79 us
    pallas_call x1, Pallas kernels, assemble(): pl.pallas_call(assemble_body, out_shape=(half, half), in_specs=[smem, sme...  8.8 us
    all_to_all x1, starting transfers between devices, shards(): lax.all_to_all(jnp.broadcast_to(w_sum[None], (reps,) + w_sum.shape), REP,...  7.3 us
    ppermute x3, waiting for transfers between devices, shards(): came = lax.ppermute(payload, 'zh', pairs).astype(f32)  6.06 us
  transfers between devices with their start and end apart: 10, of which 6 were waited for; matrix products, arithmetic and copies ran while one was open for 3% of the time, Pallas kernels for 6%

profile of v2, /device:TPU:2, one launch (start us, length us, event | category | flops | bytes accessed | tf_op | source)
XLA Modules:
  0.0 141.2 jit_solution(10311523503063390265)
XLA Ops:
  0.6 0.0 copy-start
  0.7 1.0 constant_dynamic-slice_fusion
  1.7 0.7 dynamic-slice_convert_fusion.4
  2.4 0.1 fusion.4
  2.5 5.2 %collective-permute-start = (bf16[512,256]{1,0:T(8,128)(2,1)S(1)}, bf16[512,256]{1,0:T(8,128)(2,1)S(1)}, u32[]{:S(2)}, u32[]{:S(2)}) collective-permute-start(bf16[512,256]{1,0:T(8,128)(2,1)S(1)} %fusion.4), channel_id=1, source_target_pairs={{0,0},{1,64},{2,8},{3,72},{4,128},{5,192},{6,136},{7,200},{8,16},{... | collective-permute-start | bytes 786440 | tf_op jit(solution)/shard_map/ppermute | solution.py:92
  7.7 0.9 dynamic-slice_convert_fusion.3
  8.5 0.8 dynamic-slice_bitcast_fusion
  9.3 8.8 %assemble.1 = (bf16[1024,2048]{1,0:T(8,128)(2,1)}, bf16[1024,2048]{1,0:T(8,128)(2,1)}) custom-call(s32[1,4]{1,0:T(1,128)} %count.1, s32[1]{0:T(128)} %bitcast.4.core, s32[1,128]{1,0:T(1,128)} %row.1, s32[1,128]{1,0:T(1,128)} %col.1, bf16[1,128,128,128]{3,2,1,0:T(8,128)(2,1)} %vals.1), custom_call_target="tpu_custom_call" | custom-call | tf_op jit(solution)/shard_map/assemble/pallas_call | solution.py:69
  18.1 0.9 multiply_convert_fusion.3
  19.1 0.0 collective-permute-done
  19.1 0.1 broadcast_in_dim.11
  19.1 19.9 %all_to_all.25 = bf16[4,512,256]{2,1,0:T(8,128)(2,1)S(1)} all-to-all(bf16[4,512,256]{2,1,0:T(8,128)(2,1)S(1)} %broadcast_in_dim.11), channel_id=1, replica_groups=mesh['zh'=4,'y'=4,'c'=2,'zl'=2,'x'=4] {'y'}, dimensions={0} | all-to-all | bytes 2097152 | tf_op jit(solution)/shard_map/all_to_all | solution.py:107
  39.1 0.0 copy-start.1
  39.1 0.1 collective-permute-start.1
  39.2 2.5 %collective-permute-done.1 = bf16[2048,256]{1,0:T(8,128)(2,1)S(1)} collective-permute-done((bf16[2048,256]{1,0:T(8,128)(2,1)S(1)}, bf16[2048,256]{1,0:T(8,128)(2,1)S(1)}, u32[]{:S(2)}, u32[]{:S(2)}) %collective-permute-start.1) | collective-permute-done | bytes 1048608 | tf_op jit(solution)/shard_map/ppermute | solution.py:110
  41.7 3.4 %fusion.11 = f32[1024,256]{1,0:T(8,128)S(1)} fusion(bf16[1024,2048]{1,0:T(8,128)(2,1)} %get-tuple-element.17, bf16[2048,256]{1,0:T(8,128)(2,1)S(1)} %collective-permute-done.1), kind=kOutput, calls=%fused_computation.48 | convolution fusion | flops 1073741824 | bytes 6291456 | tf_op jit(solution)/shard_map/dot_general | solution.py:111
  45.2 0.0 copy-done.1
  45.2 1.3 fusion.1
  46.4 17.0 %all_to_all.26 = bf16[8,128,256]{2,1,0:T(8,128)(2,1)S(1)} all-to-all(bf16[8,128,256]{2,1,0:T(8,128)(2,1)S(1)} %bitcast.54), channel_id=1, replica_groups=mesh['zh'=4,'y'=4,'c'=2,'zl'=2,'x'=4] {'zl','x'}, dimensions={0} | all-to-all | bytes 1048576 | tf_op jit(solution)/shard_map/all_to_all | solution.py:114
  63.5 0.1 convert_reduce_fusion.1
  63.5 0.1 multiply_convert_fusion.2
  63.6 0.0 copy-done
  63.7 0.8 multiply_convert_fusion
  64.5 0.2 fusion.3
  64.7 0.0 copy-start.2
  64.7 0.2 fusion.2
  65.0 14.2 %all_to_all.27 = bf16[8,160,256]{2,1,0:T(8,128)(2,1)S(1)} all-to-all(bf16[8,160,256]{2,1,0:T(8,128)(2,1)S(1)} %pad_maximum_fusion.1), channel_id=1, replica_groups=mesh['zh'=4,'y'=4,'c'=2,'zl'=2,'x'=4] {'zl','x'}, dimensions={0} | all-to-all | bytes 1310720 | tf_op jit(solution)/shard_map/all_to_all | solution.py:133
  79.3 0.0 copy-done.2
  79.3 1.4 convolution_convert_fusion
  80.7 0.1 collective-permute-start.2
  80.8 0.6 collective-permute-start.4
  81.4 3.1 %collective-permute-start.3 = (bf16[144,256]{1,0:T(8,128)(2,1)S(1)}, bf16[144,256]{1,0:T(8,128)(2,1)S(1)}, u32[]{:S(2)}, u32[]{:S(2)}) collective-permute-start(bf16[144,256]{1,0:T(8,128)(2,1)S(1)} %pad_maximum_fusion.5), channel_id=1, source_target_pairs={{0,0},{1,8},{2,16},{3,24},{4,32},{5,40},{6,48},{7,56},{8,64},{9,72... | collective-permute-start | bytes 221192 | tf_op jit(solution)/shard_map/ppermute | solution.py:129
  84.4 0.0 collective-permute-done.4
  84.5 0.0 collective-permute-done.2
  84.5 1.4 %fusion = bf16[2048,256]{1,0:T(8,128)(2,1)S(1)} fusion(bf16[1024,2048]{1,0:T(8,128)(2,1)S(1)} %copy-done.1, bf16[1024,256]{1,0:T(8,128)(2,1)S(1)} %bitcast.53, bf16[2048,256]{1,0:T(8,128)(2,1)S(1)} %collective-permute-done.2), kind=kOutput, calls=%fused_computation.1 | convolution fusion | flops 1075314688 | bytes 6815744 | tf_op jit(solution)/shard_map/dot_general | solution.py:139
  85.9 4.7 %collective-permute-done.3 = bf16[144,256]{1,0:T(8,128)(2,1)S(1)} collective-permute-done((bf16[144,256]{1,0:T(8,128)(2,1)S(1)}, bf16[144,256]{1,0:T(8,128)(2,1)S(1)}, u32[]{:S(2)}, u32[]{:S(2)}) %collective-permute-start.3) | collective-permute-done | bytes 73760 | tf_op jit(solution)/shard_map/ppermute | solution.py:129
  90.6 0.1 copy.12
  90.7 1.1 pad_maximum_fusion
  91.8 3.5 %all-to-all-start.3 = ((bf16[4,544,256]{2,1,0:T(8,128)(2,1)}), bf16[4,544,256]{2,1,0:T(8,128)(2,1)S(1)}, u32[]{:S(2)}, u32[]{:S(2)}) async-start(bf16[4,544,256]{2,1,0:T(8,128)(2,1)} %pad_maximum_fusion), calls=%async_computation.3 | async-start | bytes 2228224 | tf_op jit(solution)/shard_map/all_to_all | solution.py:146
  95.3 15.6 %all-to-all-done.3 = bf16[4,544,256]{2,1,0:T(8,128)(2,1)S(1)} async-done(((bf16[4,544,256]{2,1,0:T(8,128)(2,1)}), bf16[4,544,256]{2,1,0:T(8,128)(2,1)S(1)}, u32[]{:S(2)}, u32[]{:S(2)}) %all-to-all-start.3) | async-done | bytes 1114144 | tf_op jit(solution)/shard_map/all_to_all | solution.py:146
  110.9 0.2 convert_reduce_fusion
  111.2 3.4 %collective-permute-start.5 = (bf16[160,256]{1,0:T(8,128)(2,1)S(1)}, bf16[160,256]{1,0:T(8,128)(2,1)S(1)}, u32[]{:S(2)}, u32[]{:S(2)}) collective-permute-start(bf16[160,256]{1,0:T(8,128)(2,1)S(1)} %get-tuple-element.28), channel_id=1, source_target_pairs={{0,64},{64,0},{128,192},{192,128},{1,65},{65,1},{129,193},{193,129... | collective-permute-start | bytes 245768 | tf_op jit(solution)/shard_map/ppermute | solution.py:157
  114.5 6.0 %collective-permute-start.6 = (bf16[160,256]{1,0:T(8,128)(2,1)S(1)}, bf16[160,256]{1,0:T(8,128)(2,1)S(1)}, u32[]{:S(2)}, u32[]{:S(2)}) collective-permute-start(bf16[160,256]{1,0:T(8,128)(2,1)S(1)} %get-tuple-element.29), channel_id=1, source_target_pairs={{0,128},{64,192},{128,0},{192,64},{1,129},{65,193},{129,1},{193,65... | collective-permute-start | bytes 245768 | tf_op jit(solution)/shard_map/ppermute | solution.py:157
  120.5 0.5 collective-permute-start.7
  121.0 0.0 collective-permute-done.5
  121.0 2.9 %collective-permute-done.6 = bf16[160,256]{1,0:T(8,128)(2,1)S(1)} collective-permute-done((bf16[160,256]{1,0:T(8,128)(2,1)S(1)}, bf16[160,256]{1,0:T(8,128)(2,1)S(1)}, u32[]{:S(2)}, u32[]{:S(2)}) %collective-permute-start.6) | collective-permute-done | bytes 81952 | tf_op jit(solution)/shard_map/ppermute | solution.py:157
  123.9 3.1 %collective-permute-done.7 = bf16[160,256]{1,0:T(8,128)(2,1)S(1)} collective-permute-done((bf16[160,256]{1,0:T(8,128)(2,1)S(1)}, bf16[160,256]{1,0:T(8,128)(2,1)S(1)}, u32[]{:S(2)}, u32[]{:S(2)}) %collective-permute-start.7) | collective-permute-done | bytes 81952 | tf_op jit(solution)/shard_map/ppermute | solution.py:157
  127.1 0.7 broadcast_in_dim.14
  127.8 7.3 %all-to-all-start.4 = ((f32[8,32,256]{2,1,0:T(8,128)}), f32[8,32,256]{2,1,0:T(8,128)S(1)}, u32[]{:S(2)}, u32[]{:S(2)}) async-start(f32[8,32,256]{2,1,0:T(8,128)} %broadcast_in_dim.14), calls=%async_computation.4 | async-start | bytes 524288 | tf_op jit(solution)/shard_map/all_to_all | solution.py:163
  135.1 0.7 fusion.7
  135.8 4.7 %all-to-all-done.4 = f32[8,32,256]{2,1,0:T(8,128)S(1)} async-done(((f32[8,32,256]{2,1,0:T(8,128)}), f32[8,32,256]{2,1,0:T(8,128)S(1)}, u32[]{:S(2)}, u32[]{:S(2)}) %all-to-all-start.4) | async-done | bytes 262176 | tf_op jit(solution)/shard_map/all_to_all | solution.py:163
  140.5 0.7 copy.14
  (17 shorter events, 0.3 us)
Async XLA Ops:
  0.6 63.0 %copy-start = (bf16[256,256]{1,0:T(8,128)(2,1)S(1)}, bf16[256,256]{1,0:T(8,128)(2,1)}, u32[]{:S(2)}) copy-start(bf16[256,256]{1,0:T(8,128)(2,1)} %param.10) | copy-start | bytes 393220
  2.5 16.5 %collective-permute-start = (bf16[512,256]{1,0:T(8,128)(2,1)S(1)}, bf16[512,256]{1,0:T(8,128)(2,1)S(1)}, u32[]{:S(2)}, u32[]{:S(2)}) collective-permute-start(bf16[512,256]{1,0:T(8,128)(2,1)S(1)} %fusion.4), channel_id=1, source_target_pairs={{0,0},{1,64},{2,8},{3,72},{4,128},{5,192},{6,136},{7,200},{8,16},{... | collective-permute-start | bytes 786440 | tf_op jit(solution)/shard_map/ppermute | solution.py:92
  39.1 6.1 %copy-start.1 = (bf16[1024,2048]{1,0:T(8,128)(2,1)S(1)}, bf16[1024,2048]{1,0:T(8,128)(2,1)}, u32[]{:S(2)}) copy-start(bf16[1024,2048]{1,0:T(8,128)(2,1)} %get-tuple-element.15) | copy-start | bytes 12582916
  39.1 2.7 %collective-permute-start.1 = (bf16[2048,256]{1,0:T(8,128)(2,1)S(1)}, bf16[2048,256]{1,0:T(8,128)(2,1)S(1)}, u32[]{:S(2)}, u32[]{:S(2)}) collective-permute-start(bf16[2048,256]{1,0:T(8,128)(2,1)S(1)} %bitcast.47), channel_id=1, source_target_pairs={{0,8},{8,0},{1,9},{9,1},{2,10},{10,2},{3,11},{11,3},{4,12},{12,4},... | collective-permute-start | bytes 3145736 | tf_op jit(solution)/shard_map/ppermute | solution.py:110
  64.7 14.6 %copy-start.2 = (bf16[1024,2048]{1,0:T(8,128)(2,1)S(1)}, bf16[1024,2048]{1,0:T(8,128)(2,1)}, u32[]{:S(2)}) copy-start(bf16[1024,2048]{1,0:T(8,128)(2,1)} %get-tuple-element.17) | copy-start | bytes 12582916
  80.7 3.8 %collective-permute-start.2 = (bf16[2048,256]{1,0:T(8,128)(2,1)S(1)}, bf16[2048,256]{1,0:T(8,128)(2,1)S(1)}, u32[]{:S(2)}, u32[]{:S(2)}) collective-permute-start(bf16[2048,256]{1,0:T(8,128)(2,1)S(1)} %convolution_convert_fusion), channel_id=1, source_target_pairs={{0,8},{8,0},{1,9},{9,1},{2,10},{10,2},{3,11},{11,3},{4,12},{12,4},... | collective-permute-start | bytes 3145736 | tf_op jit(solution)/shard_map/ppermute | solution.py:141
  80.8 3.7 %collective-permute-start.4 = (f32[32,256]{1,0:T(8,128)S(1)}, f32[32,256]{1,0:T(8,128)S(1)}, u32[]{:S(2)}, u32[]{:S(2)}) collective-permute-start(f32[32,256]{1,0:T(8,128)S(1)} %convert_reduce_fusion.2), channel_id=1, source_target_pairs={{0,8},{8,0},{1,9},{9,1},{2,10},{10,2},{3,11},{11,3},{4,12},{12,4},... | collective-permute-start | bytes 98312 | tf_op jit(solution)/shard_map/ppermute | solution.py:136
  81.4 9.2 %collective-permute-start.3 = (bf16[144,256]{1,0:T(8,128)(2,1)S(1)}, bf16[144,256]{1,0:T(8,128)(2,1)S(1)}, u32[]{:S(2)}, u32[]{:S(2)}) collective-permute-start(bf16[144,256]{1,0:T(8,128)(2,1)S(1)} %pad_maximum_fusion.5), channel_id=1, source_target_pairs={{0,0},{1,8},{2,16},{3,24},{4,32},{5,40},{6,48},{7,56},{8,64},{9,72... | collective-permute-start | bytes 221192 | tf_op jit(solution)/shard_map/ppermute | solution.py:129
  91.8 19.1 %all-to-all-start.3 = ((bf16[4,544,256]{2,1,0:T(8,128)(2,1)}), bf16[4,544,256]{2,1,0:T(8,128)(2,1)S(1)}, u32[]{:S(2)}, u32[]{:S(2)}) async-start(bf16[4,544,256]{2,1,0:T(8,128)(2,1)} %pad_maximum_fusion), calls=%async_computation.3 | async-start | bytes 2228224 | tf_op jit(solution)/shard_map/all_to_all | solution.py:146
  111.2 9.8 %collective-permute-start.5 = (bf16[160,256]{1,0:T(8,128)(2,1)S(1)}, bf16[160,256]{1,0:T(8,128)(2,1)S(1)}, u32[]{:S(2)}, u32[]{:S(2)}) collective-permute-start(bf16[160,256]{1,0:T(8,128)(2,1)S(1)} %get-tuple-element.28), channel_id=1, source_target_pairs={{0,64},{64,0},{128,192},{192,128},{1,65},{65,1},{129,193},{193,129... | collective-permute-start | bytes 245768 | tf_op jit(solution)/shard_map/ppermute | solution.py:157
  114.5 9.4 %collective-permute-start.6 = (bf16[160,256]{1,0:T(8,128)(2,1)S(1)}, bf16[160,256]{1,0:T(8,128)(2,1)S(1)}, u32[]{:S(2)}, u32[]{:S(2)}) collective-permute-start(bf16[160,256]{1,0:T(8,128)(2,1)S(1)} %get-tuple-element.29), channel_id=1, source_target_pairs={{0,128},{64,192},{128,0},{192,64},{1,129},{65,193},{129,1},{193,65... | collective-permute-start | bytes 245768 | tf_op jit(solution)/shard_map/ppermute | solution.py:157
  120.5 6.6 %collective-permute-start.7 = (bf16[160,256]{1,0:T(8,128)(2,1)S(1)}, bf16[160,256]{1,0:T(8,128)(2,1)S(1)}, u32[]{:S(2)}, u32[]{:S(2)}) collective-permute-start(bf16[160,256]{1,0:T(8,128)(2,1)S(1)} %get-tuple-element.30), channel_id=1, source_target_pairs={{0,192},{64,128},{128,64},{192,0},{1,193},{65,129},{129,65},{193,1... | collective-permute-start | bytes 245768 | tf_op jit(solution)/shard_map/ppermute | solution.py:157
  127.8 12.7 %all-to-all-start.4 = ((f32[8,32,256]{2,1,0:T(8,128)}), f32[8,32,256]{2,1,0:T(8,128)S(1)}, u32[]{:S(2)}, u32[]{:S(2)}) async-start(f32[8,32,256]{2,1,0:T(8,128)} %broadcast_in_dim.14), calls=%async_computation.4 | async-start | bytes 524288 | tf_op jit(solution)/shard_map/all_to_all | solution.py:163

commit v3 on v2

--- a/solution.py
+++ b/solution.py
@@ -16,13 +16,42 @@
     return (((zh * Y + y) * C + c) * ZL + zl) * X + x
 
 
+def place_of(q, r):
+    return (2 * (r % 2) + q // 2 + (q % 2) * (2 * (q // 2) - 1)) % Y
+
+
 def piece_route():
     pairs = []
     for j in range(ZH * Y * C):
         for k in range(ZL * X):
-            zl, x = k // X, k % X
             r = j // 4
-            pairs.append((j * (ZL * X) + k, flat(zl * 2 + x % 2, j % 4, x // 2, r // X, r % X)))
+            dx = (k % X - r % X) % X
+            if k // X == r // X:
+                near, far = 0, 3 if r // X == 0 else 1
+            else:
+                near, far = 1 if r // X == 0 else 3, 2
+            zh = (j // (Y * C) + (far if dx < 2 else near)) % ZH
+            pairs.append((j * (ZL * X) + k, flat(zh, place_of(j % 4, r), dx % 2, r // X, r % X)))
+    return pairs
+
+
+def return_route(m):
+    pairs = []
+    for zh in range(ZH):
+        for q in range(4):
+            for c in range(C):
+                for r in range(ZL * X):
+                    source = flat(zh, place_of(q, r), c, r // X, r % X)
+                    pairs.append((source, flat(q, zh ^ m, c, r // X, r % X)))
+    return pairs
+
+
+def ring_route(back):
+    pairs = []
+    for y in range(Y):
+        for c in range(C):
+            step = 1 if (c == 0) != back else -1
+            pairs.append((y * C + c, (y + step) % Y * C + c))
     return pairs
 
 
@@ -35,7 +64,7 @@
     return pairs
 
 
-def assemble_body(count, core, row, col, vals, own, other, sem):
+def assemble_body(count, here, row, col, vals, own, other, sem):
     own[...] = jnp.zeros_like(own)
     other[...] = jnp.zeros_like(other)
     total = count[0, 0] + count[0, 1] + count[0, 2] + count[0, 3]
@@ -43,9 +72,13 @@
     @pl.loop(0, total)
     def _(k):
         at = col[0, k]
-        sub = at % 8
-        slot = (sub % 2) ^ core[0]
-        place = (at // 8) * 4 + sub // 2
+        q, sub = at >> 3, at & 7
+        parity = sub & 1
+        slot = parity ^ here[0]
+        high, low = q >> 1, q & 1
+        apart = (2 * here[2] + high + low * (2 * high - 1) - here[1]) & 3
+        order = jnp.where((apart & 1) == 0, 3 * (apart >> 1), 1 + (((3 - apart) >> 1) ^ parity))
+        place = order * 4 + (sub >> 1)
         down = pl.ds(pl.multiple_of(row[0, k] * TILE, TILE), TILE)
         across = pl.ds(pl.multiple_of(place * TILE, TILE), TILE)
 
@@ -62,7 +95,7 @@
         pltpu.make_async_copy(vals.at[0, k], own.at[pl.ds(0, TILE), pl.ds(0, TILE)], sem.at[k]).wait()
 
 
-def assemble(count, core, row, col, vals, rows, cols):
+def assemble(count, here, row, col, vals, rows, cols):
     half = jax.ShapeDtypeStruct((rows, cols), jnp.bfloat16)
     smem = pl.BlockSpec(memory_space=pltpu.SMEM)
     whole = pl.BlockSpec(memory_space=pltpu.VMEM)
@@ -73,18 +106,18 @@
         out_specs=(whole, whole),
         scratch_shapes=[pltpu.SemaphoreType.DMA((vals.shape[1],))],
         name="assemble",
-    )(count, core, row, col, vals)
+    )(count, here, row, col, vals)
 
 
 def shards(features, inv_sqrt_degree, weight, tile_vals, tile_row, tile_col, tile_count, cotangent):
     bf16, f32 = jnp.bfloat16, jnp.float32
     nodes_block, width = features.shape
-    zh, core = lax.axis_index("zh"), lax.axis_index("c")
+    zh, y, core = lax.axis_index("zh"), lax.axis_index("y"), lax.axis_index("c")
     replica = lax.axis_index(REP)
     reps = ZL * X
     share = nodes_block // reps
     nodes = nodes_block * ZH * Y * C
-    half = lax.axis_index("x") // 2
+    half = (lax.axis_index("x") + y // 2) % 2
     piece_rows = 4 * share
     feats = lax.dynamic_index_in_dim(features.reshape(4, 2, share, width), half, 1, False)
     degs = lax.dynamic_index_in_dim(inv_sqrt_degree.reshape(4, 2, share), half, 1, False)
@@ -92,7 +125,7 @@
     piece = lax.ppermute(piece, ALL, piece_route())
 
     own_a, other_a = assemble(
-        tile_count, core.reshape(1), tile_row, tile_col, tile_vals, nodes_block, Y * piece_rows
+        tile_count, jnp.stack([core, y, replica % 2]), tile_row, tile_col, tile_vals, nodes_block, Y * piece_rows
     )
     start = replica * share
     deg_bf = lax.dynamic_slice_in_dim(inv_sqrt_degree, start, share, 0)
@@ -104,13 +137,17 @@
         (piece, own_a, other_a, scaled, cot, deg_rows)
     )
 
-    gathered = lax.all_to_all(jnp.broadcast_to(piece[None], (Y,) + piece.shape), "y", 0, 0)
-    own_x = gathered.reshape(Y * piece_rows, width)
     swap = [(0, 1), (1, 0)]
-    other_x = lax.ppermute(own_x, "c", swap)
-    partial = jnp.dot(own_a, own_x, preferred_element_type=f32) + jnp.dot(
-        other_a, other_x, preferred_element_type=f32
-    )
+    ahead, behind = ring_route(False), ring_route(True)
+    first = lax.ppermute(piece, ("y", "c"), ahead)
+    second = lax.ppermute(piece, ("y", "c"), behind)
+    third = lax.ppermute(first, ("y", "c"), ahead)
+    partial = jnp.zeros((nodes_block, width), f32)
+    for i, own_x in enumerate((piece, first, second, third)):
+        other_x = lax.ppermute(own_x, "c", swap)
+        at = slice(i * piece_rows, (i + 1) * piece_rows)
+        partial = partial + jnp.dot(own_a[:, at], own_x, preferred_element_type=f32)
+        partial = partial + jnp.dot(other_a[:, at], other_x, preferred_element_type=f32)
     parts = lax.all_to_all(partial.astype(bf16).reshape(reps, share, width), REP, 0, 0)
     summed = jnp.sum(parts.astype(f32), 0)
 
@@ -135,26 +172,35 @@
     w_slice = jnp.sum(both[:, share:].astype(f32), 0)
     w_slice = w_slice + lax.ppermute(w_slice, "c", swap)
 
-    def pull(a):
-        return lax.dot_general(a, back_block, (((0,), (0,)), ((), ())), preferred_element_type=f32)
-
-    other_g = lax.ppermute(pull(other_a).astype(bf16), "c", swap)
-    col_sum = (pull(own_a) + other_g.astype(f32)).astype(bf16)
-    col_sum, back_sent = lax.optimization_barrier((col_sum, back_sent))
-    col_sum = col_sum.reshape(4, 4, share, width).transpose(1, 0, 2, 3).reshape(Y, piece_rows, width)
     w_rows = w_slice.astype(bf16)
-    both = lax.all_to_all(
-        jnp.concatenate([col_sum, jnp.broadcast_to(w_rows[None], (Y,) + w_rows.shape)], 1), "y", 0, 0
-    )
-    both = jnp.sum(both.astype(f32), 0)
-    chunks, w_rows = both[:piece_rows].reshape(4, share, width), both[piece_rows:]
-    w_sum = w_rows
-    grad = lax.dynamic_index_in_dim(chunks, zh, 0, False)
-    for m in range(1, 4):
-        pairs = [(i, i ^ m) for i in range(ZH)]
+
+    def pull(a, i):
+        return lax.dot_general(
+            a[:, i * piece_rows : (i + 1) * piece_rows],
+            back_block,
+            (((0,), (0,)), ((), ())),
+            preferred_element_type=f32,
+        )
+
+    def both_rows(i):
+        other_g = lax.ppermute(pull(other_a, i).astype(bf16), "c", swap)
+        return pull(own_a, i) + other_g.astype(f32)
+
+    def send(grad_rows, w_part, route):
+        came = lax.ppermute(jnp.concatenate([grad_rows.astype(bf16), w_part], 0), ("y", "c"), route)
+        return came[:piece_rows].astype(f32), came[piece_rows:]
+
+    relayed, w_first = send(both_rows(3), w_rows, ahead)
+    direct, w_second = send(both_rows(1), w_rows, behind)
+    relayed, back_sent = lax.optimization_barrier((relayed, back_sent))
+    relayed, w_third = send(both_rows(2) + relayed, w_first, ahead)
+    chunks = (both_rows(0) + direct + relayed).astype(bf16).reshape(4, share, width)
+    w_rows = sum(w.astype(f32) for w in (w_rows, w_first, w_second, w_third)).astype(bf16)
+    grad = jnp.zeros((share, width), f32)
+    w_sum = jnp.zeros(w_rows.shape, f32)
+    for m in range(4):
         chunk = lax.dynamic_index_in_dim(chunks, zh ^ m, 0, False)
-        payload = jnp.concatenate([chunk, w_rows], 0).astype(bf16)
-        came = lax.ppermute(payload, "zh", pairs).astype(f32)
+        came = lax.ppermute(jnp.concatenate([chunk, w_rows], 0), ALL, return_route(m)).astype(f32)
         grad = grad + came[:share]
         w_sum = w_sum + came[share:]
     own_back = back_sent[:share].astype(f32)

time: 142 us -> 142 us (level)
  starting transfers between devices: 29.6 us -> 65.8 us
  blocking collectives: 51.2 us -> 27 us
  waiting for transfers between devices: 33.6 us -> 19.2 us
  matrix products: 8.71 us -> 12.5 us
  Pallas kernels: 8.8 us -> 7.14 us
    ppermute x4 -> x14, starting transfers between devices: 9.89 us -> 45.3 us  [the longest x4 25.6 us: shards(): lax.ppermute(jnp.concatenate([chunk, w_rows], 0), ALL, return_route(m))]
    all_to_all x1 -> x0, blocking collectives: 19.9 us -> none  [shards(): lax.all_to_all(jnp.broadcast_to(piece[None], (Y,) + piece.shape), 'y', 0, 0)]
    all_to_all x1 -> x0, waiting for transfers between devices: 15.6 us -> none  [shards(): lax.all_to_all(jnp.concatenate([col_sum, jnp.broadcast_to(w_rows[None], (...]
    ppermute x4 -> x14, waiting for transfers between devices: 6.06 us -> 14 us  [the longest x1 4.5 us: shards(): first = lax.ppermute(piece, ('y', 'c'), ahead)]
    ppermute x1 -> x4, starting transfers between devices: 0.12 us -> 5.44 us  [shards(): other_x = lax.ppermute(own_x, 'c', swap)]
    ppermute x1, waiting for transfers between devices: 4.72 us -> 0.01 us  [shards(): lax.ppermute(jnp.concatenate([back, deg_rows], 0), ALL, share_route())]
    all_to_all x1, blocking collectives: 17 us -> 12.5 us  [shards(): lax.all_to_all(partial.astype(bf16).reshape(reps, share, width), REP, 0, 0)]
    dot_general x4 -> x16, matrix products: 7.46 us -> 11.2 us  [the longest x8 5.13 us: pull(): lax.dot_general(a[:, i * piece_rows:(i + 1) * piece_rows], back_block, ((...]
  transfers between devices with their start and end apart: 10 -> 22, of which waited for: 6 -> 10; matrix products, arithmetic and copies ran while one was open for 3% -> 9% of each run, Pallas kernels for 6% -> 5%
where the time goes in v3:
time: 142 us; the launch traced here: 141 us
  starting transfers between devices  65.8 us (46%)
  blocking collectives  27 us (19%)
  waiting for transfers between devices  19.2 us (14%)
  matrix products  12.5 us (9%)
  Pallas kernels  7.14 us (5%)
  other arithmetic  5.34 us (4%)
  local copies, waits for them, and re-layouts  2.56 us (2%)
    ppermute x4, starting transfers between devices, shards(): lax.ppermute(jnp.concatenate([chunk, w_rows], 0), ALL, return_route(m))  25.6 us
    ppermute x3, starting transfers between devices, send(): lax.ppermute(jnp.concatenate([grad_rows.astype(bf16), w_part], 0), ('y',...  15.1 us
    all_to_all x1, blocking collectives, shards(): both = lax.all_to_all(both, REP, 0, 0)  14.5 us
    all_to_all x1, blocking collectives, shards(): lax.all_to_all(partial.astype(bf16).reshape(reps, share, width), REP, 0, 0)  12.5 us
    pallas_call x1, Pallas kernels, assemble(): pl.pallas_call(assemble_body, out_shape=(half, half), in_specs=[smem, sme...  7.14 us
    ppermute x1, starting transfers between devices, shards(): piece = lax.ppermute(piece, ALL, piece_route())  5.79 us
    all_to_all x1, starting transfers between devices, shards(): lax.all_to_all(jnp.broadcast_to(w_sum[None], (reps,) + w_sum.shape), REP,...  5.51 us
    ppermute x4, starting transfers between devices, shards(): other_x = lax.ppermute(own_x, 'c', swap)  5.44 us
  transfers between devices with their start and end apart: 22, of which 10 were waited for; matrix products, arithmetic and copies ran while one was open for 9% of the time, Pallas kernels for 5%

profile of v3, /device:TPU:2, one launch (start us, length us, event | category | flops | bytes accessed | tf_op | source)
XLA Modules:
  0.0 140.6 jit_solution(3239779108185376083)
XLA Ops:
  0.7 1.0 constant_dynamic-slice_fusion
  1.7 0.7 dynamic-slice_convert_fusion.1
  2.4 0.1 fusion.33
  2.5 5.8 %collective-permute-start = (bf16[512,256]{1,0:T(8,128)(2,1)S(1)}, bf16[512,256]{1,0:T(8,128)(2,1)S(1)}, u32[]{:S(2)}, u32[]{:S(2)}) collective-permute-start(bf16[512,256]{1,0:T(8,128)(2,1)S(1)} %fusion.33), channel_id=1, source_target_pairs={{0,192},{1,200},{2,0},{3,8},{4,128},{5,136},{6,64},{7,72},{8,240},... | collective-permute-start | bytes 786440 | tf_op jit(solution)/shard_map/ppermute | solution.py:125
  8.3 0.8 dynamic-slice_bitcast_fusion.4
  9.1 0.8 dynamic-slice_convert_fusion
  9.9 0.7 pad_add_fusion.here
  10.6 7.1 %assemble.1 = (bf16[1024,2048]{1,0:T(8,128)(2,1)}, bf16[1024,2048]{1,0:T(8,128)(2,1)}) custom-call(s32[1,4]{1,0:T(1,128)} %count.1, s32[3]{0:T(128)} %pad_add_fusion.here, s32[1,128]{1,0:T(1,128)} %row.1, s32[1,128]{1,0:T(1,128)} %col.1, bf16[1,128,128,128]{3,2,1,0:T(8,128)(2,1)} %vals.1), custom_call_target="tpu_custom_call" | custom-call | tf_op jit(solution)/shard_map/assemble/pallas_call | solution.py:102
  17.8 1.1 multiply_convert_fusion.3
  18.9 2.6 %collective-permute-start.2 = (bf16[512,256]{1,0:T(8,128)(2,1)S(1)}, bf16[512,256]{1,0:T(8,128)(2,1)S(1)}, u32[]{:S(2)}, u32[]{:S(2)}) collective-permute-start(bf16[512,256]{1,0:T(8,128)(2,1)S(1)} %collective-permute-done), channel_id=1, source_target_pairs={{0,16},{8,56},{16,32},{24,8},{32,48},{40,24},{48,0},{56,40},{1,17}... | collective-permute-start | bytes 786440 | tf_op jit(solution)/shard_map/ppermute | solution.py:142
  21.5 1.0 collective-permute-start.1
  22.5 0.6 collective-permute-start.4
  23.1 4.5 %collective-permute-done.2 = bf16[512,256]{1,0:T(8,128)(2,1)S(1)} collective-permute-done((bf16[512,256]{1,0:T(8,128)(2,1)S(1)}, bf16[512,256]{1,0:T(8,128)(2,1)S(1)}, u32[]{:S(2)}, u32[]{:S(2)}) %collective-permute-start.2) | collective-permute-done | bytes 262176 | tf_op jit(solution)/shard_map/ppermute | solution.py:142
  27.6 2.1 %collective-permute-start.3 = (bf16[512,256]{1,0:T(8,128)(2,1)S(1)}, bf16[512,256]{1,0:T(8,128)(2,1)S(1)}, u32[]{:S(2)}, u32[]{:S(2)}) collective-permute-start(bf16[512,256]{1,0:T(8,128)(2,1)S(1)} %collective-permute-done.2), channel_id=1, source_target_pairs={{0,8},{8,0},{1,9},{9,1},{2,10},{10,2},{3,11},{11,3},{4,12},{12,4},... | collective-permute-start | bytes 786440 | tf_op jit(solution)/shard_map/ppermute | solution.py:147
  29.7 1.7 %fusion.26 = f32[1024,256]{1,0:T(8,128)S(1)} fusion(bf16[512,256]{1,0:T(8,128)(2,1)S(1)} %collective-permute-done.2, bf16[1024,2048]{1,0:T(8,128)(2,1)} %get-tuple-element.15), kind=kOutput, calls=%fused_computation.41 | convolution fusion | flops 268435456 | bytes 2359296 | tf_op jit(solution)/shard_map/dot_general | solution.py:149
  31.3 1.8 %fusion.29 = f32[1024,256]{1,0:T(8,128)S(1)} fusion(bf16[512,256]{1,0:T(8,128)(2,1)S(1)} %collective-permute-done.1, bf16[1024,2048]{1,0:T(8,128)(2,1)} %get-tuple-element.17), kind=kOutput, calls=%fused_computation.44 | convolution fusion | flops 268435456 | bytes 2359296 | tf_op jit(solution)/shard_map/dot_general | solution.py:150
  33.2 0.4 fusion.2
  33.6 2.3 %collective-permute-start.5 = (bf16[512,256]{1,0:T(8,128)(2,1)S(1)}, bf16[512,256]{1,0:T(8,128)(2,1)S(1)}, u32[]{:S(2)}, u32[]{:S(2)}) collective-permute-start(bf16[512,256]{1,0:T(8,128)(2,1)S(1)} %collective-permute-done.4), channel_id=1, source_target_pairs={{0,8},{8,0},{1,9},{9,1},{2,10},{10,2},{3,11},{11,3},{4,12},{12,4},... | collective-permute-start | bytes 786440 | tf_op jit(solution)/shard_map/ppermute | solution.py:147
  36.0 0.4 fusion.21
  36.4 0.8 collective-permute-done.6
  37.3 0.4 fusion.1
  37.7 0.4 fusion.16
  38.2 0.4 fusion
  38.6 0.2 collective-permute-done.7
  38.8 0.4 fusion.3
  39.2 12.5 %all_to_all.15 = bf16[8,128,256]{2,1,0:T(8,128)(2,1)S(1)} all-to-all(bf16[8,128,256]{2,1,0:T(8,128)(2,1)S(1)} %bitcast.49), channel_id=1, replica_groups=mesh['zh'=4,'y'=4,'c'=2,'zl'=2,'x'=4] {'zl','x'}, dimensions={0} | all-to-all | bytes 1048576 | tf_op jit(solution)/shard_map/all_to_all | solution.py:151
  51.7 0.1 convert_reduce_fusion
  51.8 0.1 multiply_convert_fusion.2
  51.9 0.8 multiply_convert_fusion
  52.7 0.2 fusion.12
  52.9 0.2 fusion.11
  53.2 14.5 %all_to_all.16 = bf16[8,160,256]{2,1,0:T(8,128)(2,1)S(1)} all-to-all(bf16[8,160,256]{2,1,0:T(8,128)(2,1)S(1)} %pad_maximum_fusion), channel_id=1, replica_groups=mesh['zh'=4,'y'=4,'c'=2,'zl'=2,'x'=4] {'zl','x'}, dimensions={0} | all-to-all | bytes 1310720 | tf_op jit(solution)/shard_map/all_to_all | solution.py:170
  67.7 0.5 convolution_convert_fusion
  68.2 0.1 collective-permute-start.13
  68.4 0.8 collective-permute-start.10
  69.1 0.5 convolution_convert_fusion.2
  69.6 0.1 collective-permute-start.9
  69.7 0.3 collective-permute-done.10
  70.0 0.5 fusion.8
  70.5 0.7 collective-permute-done.9
  71.2 0.5 fusion.7
  71.8 0.3 collective-permute-start.14
  72.1 0.5 convolution_convert_fusion.1
  72.5 1.1 collective-permute-start.12
  73.6 3.0 %collective-permute-start.15 = (bf16[144,256]{1,0:T(8,128)(2,1)S(1)}, bf16[144,256]{1,0:T(8,128)(2,1)S(1)}, u32[]{:S(2)}, u32[]{:S(2)}) collective-permute-start(bf16[144,256]{1,0:T(8,128)(2,1)S(1)} %pad_maximum_fusion.8), channel_id=1, source_target_pairs={{0,0},{1,8},{2,16},{3,24},{4,32},{5,40},{6,48},{7,56},{8,64},{9,72... | collective-permute-start | bytes 221192 | tf_op jit(solution)/shard_map/ppermute | solution.py:166
  76.7 13.2 %collective-permute-start.11 = (bf16[544,256]{1,0:T(8,128)(2,1)S(1)}, bf16[544,256]{1,0:T(8,128)(2,1)S(1)}, u32[]{:S(2)}, u32[]{:S(2)}) collective-permute-start(bf16[544,256]{1,0:T(8,128)(2,1)S(1)} %get-tuple-element.33), channel_id=1, source_target_pairs={{0,48},{8,24},{16,0},{24,40},{32,16},{40,56},{48,32},{56,8},{1,49}... | collective-permute-start | bytes 835592 | tf_op jit(solution)/shard_map/ppermute | solution.py:190
  89.9 0.5 fusion.10
  90.5 1.6 %collective-permute-start.16 = (bf16[544,256]{1,0:T(8,128)(2,1)S(1)}, bf16[544,256]{1,0:T(8,128)(2,1)S(1)}, u32[]{:S(2)}, u32[]{:S(2)}) collective-permute-start(bf16[544,256]{1,0:T(8,128)(2,1)S(1)} %pad_maximum_fusion.3), channel_id=1, source_target_pairs={{0,16},{8,56},{16,32},{24,8},{32,48},{40,24},{48,0},{56,40},{1,17}... | collective-permute-start | bytes 835592 | tf_op jit(solution)/shard_map/ppermute | solution.py:190
  92.1 0.5 convolution_convert_fusion.3
  92.6 0.1 collective-permute-start.8
  92.7 1.5 %collective-permute-done.8 = bf16[512,256]{1,0:T(8,128)(2,1)S(1)} collective-permute-done((bf16[512,256]{1,0:T(8,128)(2,1)S(1)}, bf16[512,256]{1,0:T(8,128)(2,1)S(1)}, u32[]{:S(2)}, u32[]{:S(2)}) %collective-permute-start.8) | collective-permute-done | bytes 262176 | tf_op jit(solution)/shard_map/ppermute | solution.py:186
  94.2 4.1 %collective-permute-done.16 = bf16[544,256]{1,0:T(8,128)(2,1)S(1)} collective-permute-done((bf16[544,256]{1,0:T(8,128)(2,1)S(1)}, bf16[544,256]{1,0:T(8,128)(2,1)S(1)}, u32[]{:S(2)}, u32[]{:S(2)}) %collective-permute-start.16) | collective-permute-done | bytes 278560 | tf_op jit(solution)/shard_map/ppermute | solution.py:190
  98.3 1.7 %fusion.9 = bf16[512,256]{1,0:T(8,128)(2,1)S(1)} fusion(bf16[1024,256]{1,0:T(8,128)(2,1)S(1)} %bitcast.59, bf16[1024,2048]{1,0:T(8,128)(2,1)} %get-tuple-element.15, bf16[512,256]{1,0:T(8,128)(2,1)S(1)} %collective-permute-done.8, bf16[544,256]{1,0:T(8,128)(2,1)S(1)} %collective-permute-done.16, bf16[544,256]{1,0:T(8,128)(2,1)S(1)} %collective-permute-done.11), kind=kOutput, calls=%fused_computation.17 | convolution fusion | flops 269352960 | bytes 2621440 | tf_op jit(solution)/shard_map/dot_general | solution.py:178
  100.1 2.8 %collective-permute-start.17 = (bf16[160,256]{1,0:T(8,128)(2,1)S(1)}, bf16[160,256]{1,0:T(8,128)(2,1)S(1)}, u32[]{:S(2)}, u32[]{:S(2)}) collective-permute-start(bf16[160,256]{1,0:T(8,128)(2,1)S(1)} %get-tuple-element.29), channel_id=1, source_target_pairs={{0,0},{33,1},{2,2},{35,3},{4,4},{37,5},{6,6},{39,7},{8,8},{41,9},{... | collective-permute-start | bytes 245768 | tf_op jit(solution)/shard_map/ppermute | solution.py:203
  102.9 7.8 %collective-permute-start.18 = (bf16[160,256]{1,0:T(8,128)(2,1)S(1)}, bf16[160,256]{1,0:T(8,128)(2,1)S(1)}, u32[]{:S(2)}, u32[]{:S(2)}) collective-permute-start(bf16[160,256]{1,0:T(8,128)(2,1)S(1)} %get-tuple-element.30), channel_id=1, source_target_pairs={{0,16},{33,17},{2,18},{35,19},{4,20},{37,21},{6,22},{39,23},{8,24}... | collective-permute-start | bytes 245768 | tf_op jit(solution)/shard_map/ppermute | solution.py:203
  110.7 2.2 %collective-permute-start.19 = (bf16[160,256]{1,0:T(8,128)(2,1)S(1)}, bf16[160,256]{1,0:T(8,128)(2,1)S(1)}, u32[]{:S(2)}, u32[]{:S(2)}) collective-permute-start(bf16[160,256]{1,0:T(8,128)(2,1)S(1)} %get-tuple-element.31), channel_id=1, source_target_pairs={{0,32},{33,33},{2,34},{35,35},{4,36},{37,37},{6,38},{39,39},{8,40}... | collective-permute-start | bytes 245768 | tf_op jit(solution)/shard_map/ppermute | solution.py:203
  112.9 12.8 %collective-permute-start.20 = (bf16[160,256]{1,0:T(8,128)(2,1)S(1)}, bf16[160,256]{1,0:T(8,128)(2,1)S(1)}, u32[]{:S(2)}, u32[]{:S(2)}) collective-permute-start(bf16[160,256]{1,0:T(8,128)(2,1)S(1)} %get-tuple-element.32), channel_id=1, source_target_pairs={{0,48},{33,49},{2,50},{35,51},{4,52},{37,53},{6,54},{39,55},{8,56}... | collective-permute-start | bytes 245768 | tf_op jit(solution)/shard_map/ppermute | solution.py:203
  125.8 0.9 collective-permute-done.19
  126.8 1.4 collective-permute-done.20
  128.2 0.7 broadcast_in_dim.8
  128.9 5.5 %all-to-all-start.2 = ((f32[8,32,256]{2,1,0:T(8,128)}), f32[8,32,256]{2,1,0:T(8,128)S(1)}, u32[]{:S(2)}, u32[]{:S(2)}) async-start(f32[8,32,256]{2,1,0:T(8,128)} %broadcast_in_dim.8), calls=%async_computation.2 | async-start | bytes 524288 | tf_op jit(solution)/shard_map/all_to_all | solution.py:209
  134.4 0.7 fusion.36
  135.1 4.8 %all-to-all-done.2 = f32[8,32,256]{2,1,0:T(8,128)S(1)} async-done(((f32[8,32,256]{2,1,0:T(8,128)}), f32[8,32,256]{2,1,0:T(8,128)S(1)}, u32[]{:S(2)}, u32[]{:S(2)}) %all-to-all-start.2) | async-done | bytes 262176 | tf_op jit(solution)/shard_map/all_to_all | solution.py:209
  139.9 0.7 copy.12
  (40 shorter events, 0.4 us)
Async XLA Ops:
  0.6 51.2 %copy-start = (bf16[256,256]{1,0:T(8,128)(2,1)S(1)}, bf16[256,256]{1,0:T(8,128)(2,1)}, u32[]{:S(2)}) copy-start(bf16[256,256]{1,0:T(8,128)(2,1)} %param.10) | copy-start | bytes 393220
  2.5 16.3 %collective-permute-start = (bf16[512,256]{1,0:T(8,128)(2,1)S(1)}, bf16[512,256]{1,0:T(8,128)(2,1)S(1)}, u32[]{:S(2)}, u32[]{:S(2)}) collective-permute-start(bf16[512,256]{1,0:T(8,128)(2,1)S(1)} %fusion.33), channel_id=1, source_target_pairs={{0,192},{1,200},{2,0},{3,8},{4,128},{5,136},{6,64},{7,72},{8,240},... | collective-permute-start | bytes 786440 | tf_op jit(solution)/shard_map/ppermute | solution.py:125
  17.8 15.4 %copy-start.1 = (bf16[1024,2048]{1,0:T(8,128)(2,1)S(1)}, bf16[1024,2048]{1,0:T(8,128)(2,1)}, u32[]{:S(2)}) copy-start(bf16[1024,2048]{1,0:T(8,128)(2,1)} %get-tuple-element.15) | copy-start | bytes 12582916
  18.9 8.7 %collective-permute-start.2 = (bf16[512,256]{1,0:T(8,128)(2,1)S(1)}, bf16[512,256]{1,0:T(8,128)(2,1)S(1)}, u32[]{:S(2)}, u32[]{:S(2)}) collective-permute-start(bf16[512,256]{1,0:T(8,128)(2,1)S(1)} %collective-permute-done), channel_id=1, source_target_pairs={{0,16},{8,56},{16,32},{24,8},{32,48},{40,24},{48,0},{56,40},{1,17}... | collective-permute-start | bytes 786440 | tf_op jit(solution)/shard_map/ppermute | solution.py:142
  21.5 9.8 %collective-permute-start.1 = (bf16[512,256]{1,0:T(8,128)(2,1)S(1)}, bf16[512,256]{1,0:T(8,128)(2,1)S(1)}, u32[]{:S(2)}, u32[]{:S(2)}) collective-permute-start(bf16[512,256]{1,0:T(8,128)(2,1)S(1)} %collective-permute-done), channel_id=1, source_target_pairs={{0,8},{8,0},{1,9},{9,1},{2,10},{10,2},{3,11},{11,3},{4,12},{12,4},... | collective-permute-start | bytes 786440 | tf_op jit(solution)/shard_map/ppermute | solution.py:147
  22.5 11.1 %collective-permute-start.4 = (bf16[512,256]{1,0:T(8,128)(2,1)S(1)}, bf16[512,256]{1,0:T(8,128)(2,1)S(1)}, u32[]{:S(2)}, u32[]{:S(2)}) collective-permute-start(bf16[512,256]{1,0:T(8,128)(2,1)S(1)} %collective-permute-done), channel_id=1, source_target_pairs={{0,48},{8,24},{16,0},{24,40},{32,16},{40,56},{48,32},{56,8},{1,49}... | collective-permute-start | bytes 786440 | tf_op jit(solution)/shard_map/ppermute | solution.py:143
  27.6 9.7 %collective-permute-start.3 = (bf16[512,256]{1,0:T(8,128)(2,1)S(1)}, bf16[512,256]{1,0:T(8,128)(2,1)S(1)}, u32[]{:S(2)}, u32[]{:S(2)}) collective-permute-start(bf16[512,256]{1,0:T(8,128)(2,1)S(1)} %collective-permute-done.2), channel_id=1, source_target_pairs={{0,8},{8,0},{1,9},{9,1},{2,10},{10,2},{3,11},{11,3},{4,12},{12,4},... | collective-permute-start | bytes 786440 | tf_op jit(solution)/shard_map/ppermute | solution.py:147
  29.7 7.6 %collective-permute-start.6 = (bf16[512,256]{1,0:T(8,128)(2,1)S(1)}, bf16[512,256]{1,0:T(8,128)(2,1)S(1)}, u32[]{:S(2)}, u32[]{:S(2)}) collective-permute-start(bf16[512,256]{1,0:T(8,128)(2,1)S(1)} %collective-permute-done.2), channel_id=1, source_target_pairs={{0,16},{8,56},{16,32},{24,8},{32,48},{40,24},{48,0},{56,40},{1,17}... | collective-permute-start | bytes 786440 | tf_op jit(solution)/shard_map/ppermute | solution.py:144
  31.3 5.9 %copy-start.2 = (bf16[1024,2048]{1,0:T(8,128)(2,1)S(1)}, bf16[1024,2048]{1,0:T(8,128)(2,1)}, u32[]{:S(2)}) copy-start(bf16[1024,2048]{1,0:T(8,128)(2,1)} %get-tuple-element.17) | copy-start | bytes 12582916
  33.6 4.5 %collective-permute-start.5 = (bf16[512,256]{1,0:T(8,128)(2,1)S(1)}, bf16[512,256]{1,0:T(8,128)(2,1)S(1)}, u32[]{:S(2)}, u32[]{:S(2)}) collective-permute-start(bf16[512,256]{1,0:T(8,128)(2,1)S(1)} %collective-permute-done.4), channel_id=1, source_target_pairs={{0,8},{8,0},{1,9},{9,1},{2,10},{10,2},{3,11},{11,3},{4,12},{12,4},... | collective-permute-start | bytes 786440 | tf_op jit(solution)/shard_map/ppermute | solution.py:147
  37.2 1.5 %collective-permute-start.7 = (bf16[512,256]{1,0:T(8,128)(2,1)S(1)}, bf16[512,256]{1,0:T(8,128)(2,1)S(1)}, u32[]{:S(2)}, u32[]{:S(2)}) collective-permute-start(bf16[512,256]{1,0:T(8,128)(2,1)S(1)} %collective-permute-done.6), channel_id=1, source_target_pairs={{0,8},{8,0},{1,9},{9,1},{2,10},{10,2},{3,11},{11,3},{4,12},{12,4},... | collective-permute-start | bytes 786440 | tf_op jit(solution)/shard_map/ppermute | solution.py:147
  68.2 1.8 %collective-permute-start.13 = (bf16[512,256]{1,0:T(8,128)(2,1)S(1)}, bf16[512,256]{1,0:T(8,128)(2,1)S(1)}, u32[]{:S(2)}, u32[]{:S(2)}) collective-permute-start(bf16[512,256]{1,0:T(8,128)(2,1)S(1)} %convolution_convert_fusion), channel_id=1, source_target_pairs={{0,8},{8,0},{1,9},{9,1},{2,10},{10,2},{3,11},{11,3},{4,12},{12,4},... | collective-permute-start | bytes 786440 | tf_op jit(solution)/shard_map/ppermute | solution.py:186
  68.4 1.6 %collective-permute-start.10 = (f32[32,256]{1,0:T(8,128)S(1)}, f32[32,256]{1,0:T(8,128)S(1)}, u32[]{:S(2)}, u32[]{:S(2)}) collective-permute-start(f32[32,256]{1,0:T(8,128)S(1)} %convert_reduce_fusion.1), channel_id=1, source_target_pairs={{0,8},{8,0},{1,9},{9,1},{2,10},{10,2},{3,11},{11,3},{4,12},{12,4},... | collective-permute-start | bytes 98312 | tf_op jit(solution)/shard_map/ppermute | solution.py:173
  69.6 1.6 %collective-permute-start.9 = (bf16[512,256]{1,0:T(8,128)(2,1)S(1)}, bf16[512,256]{1,0:T(8,128)(2,1)S(1)}, u32[]{:S(2)}, u32[]{:S(2)}) collective-permute-start(bf16[512,256]{1,0:T(8,128)(2,1)S(1)} %convolution_convert_fusion.2), channel_id=1, source_target_pairs={{0,8},{8,0},{1,9},{9,1},{2,10},{10,2},{3,11},{11,3},{4,12},{12,4},... | collective-permute-start | bytes 786440 | tf_op jit(solution)/shard_map/ppermute | solution.py:186
  71.8 18.1 %collective-permute-start.14 = (bf16[544,256]{1,0:T(8,128)(2,1)S(1)}, bf16[544,256]{1,0:T(8,128)(2,1)S(1)}, u32[]{:S(2)}, u32[]{:S(2)}) collective-permute-start(bf16[544,256]{1,0:T(8,128)(2,1)S(1)} %get-tuple-element.34), channel_id=1, source_target_pairs={{0,16},{8,56},{16,32},{24,8},{32,48},{40,24},{48,0},{56,40},{1,17}... | collective-permute-start | bytes 835592 | tf_op jit(solution)/shard_map/ppermute | solution.py:190
  72.5 17.4 %collective-permute-start.12 = (bf16[512,256]{1,0:T(8,128)(2,1)S(1)}, bf16[512,256]{1,0:T(8,128)(2,1)S(1)}, u32[]{:S(2)}, u32[]{:S(2)}) collective-permute-start(bf16[512,256]{1,0:T(8,128)(2,1)S(1)} %convolution_convert_fusion.1), channel_id=1, source_target_pairs={{0,8},{8,0},{1,9},{9,1},{2,10},{10,2},{3,11},{11,3},{4,12},{12,4},... | collective-permute-start | bytes 786440 | tf_op jit(solution)/shard_map/ppermute | solution.py:186
  73.6 16.3 %collective-permute-start.15 = (bf16[144,256]{1,0:T(8,128)(2,1)S(1)}, bf16[144,256]{1,0:T(8,128)(2,1)S(1)}, u32[]{:S(2)}, u32[]{:S(2)}) collective-permute-start(bf16[144,256]{1,0:T(8,128)(2,1)S(1)} %pad_maximum_fusion.8), channel_id=1, source_target_pairs={{0,0},{1,8},{2,16},{3,24},{4,32},{5,40},{6,48},{7,56},{8,64},{9,72... | collective-permute-start | bytes 221192 | tf_op jit(solution)/shard_map/ppermute | solution.py:166
  76.7 17.5 %collective-permute-start.11 = (bf16[544,256]{1,0:T(8,128)(2,1)S(1)}, bf16[544,256]{1,0:T(8,128)(2,1)S(1)}, u32[]{:S(2)}, u32[]{:S(2)}) collective-permute-start(bf16[544,256]{1,0:T(8,128)(2,1)S(1)} %get-tuple-element.33), channel_id=1, source_target_pairs={{0,48},{8,24},{16,0},{24,40},{32,16},{40,56},{48,32},{56,8},{1,49}... | collective-permute-start | bytes 835592 | tf_op jit(solution)/shard_map/ppermute | solution.py:190
  90.5 7.8 %collective-permute-start.16 = (bf16[544,256]{1,0:T(8,128)(2,1)S(1)}, bf16[544,256]{1,0:T(8,128)(2,1)S(1)}, u32[]{:S(2)}, u32[]{:S(2)}) collective-permute-start(bf16[544,256]{1,0:T(8,128)(2,1)S(1)} %pad_maximum_fusion.3), channel_id=1, source_target_pairs={{0,16},{8,56},{16,32},{24,8},{32,48},{40,24},{48,0},{56,40},{1,17}... | collective-permute-start | bytes 835592 | tf_op jit(solution)/shard_map/ppermute | solution.py:190
  92.6 1.6 %collective-permute-start.8 = (bf16[512,256]{1,0:T(8,128)(2,1)S(1)}, bf16[512,256]{1,0:T(8,128)(2,1)S(1)}, u32[]{:S(2)}, u32[]{:S(2)}) collective-permute-start(bf16[512,256]{1,0:T(8,128)(2,1)S(1)} %convolution_convert_fusion.3), channel_id=1, source_target_pairs={{0,8},{8,0},{1,9},{9,1},{2,10},{10,2},{3,11},{11,3},{4,12},{12,4},... | collective-permute-start | bytes 786440 | tf_op jit(solution)/shard_map/ppermute | solution.py:186
  100.1 25.7 %collective-permute-start.17 = (bf16[160,256]{1,0:T(8,128)(2,1)S(1)}, bf16[160,256]{1,0:T(8,128)(2,1)S(1)}, u32[]{:S(2)}, u32[]{:S(2)}) collective-permute-start(bf16[160,256]{1,0:T(8,128)(2,1)S(1)} %get-tuple-element.29), channel_id=1, source_target_pairs={{0,0},{33,1},{2,2},{35,3},{4,4},{37,5},{6,6},{39,7},{8,8},{41,9},{... | collective-permute-start | bytes 245768 | tf_op jit(solution)/shard_map/ppermute | solution.py:203
  102.9 22.9 %collective-permute-start.18 = (bf16[160,256]{1,0:T(8,128)(2,1)S(1)}, bf16[160,256]{1,0:T(8,128)(2,1)S(1)}, u32[]{:S(2)}, u32[]{:S(2)}) collective-permute-start(bf16[160,256]{1,0:T(8,128)(2,1)S(1)} %get-tuple-element.30), channel_id=1, source_target_pairs={{0,16},{33,17},{2,18},{35,19},{4,20},{37,21},{6,22},{39,23},{8,24}... | collective-permute-start | bytes 245768 | tf_op jit(solution)/shard_map/ppermute | solution.py:203
  110.7 16.0 %collective-permute-start.19 = (bf16[160,256]{1,0:T(8,128)(2,1)S(1)}, bf16[160,256]{1,0:T(8,128)(2,1)S(1)}, u32[]{:S(2)}, u32[]{:S(2)}) collective-permute-start(bf16[160,256]{1,0:T(8,128)(2,1)S(1)} %get-tuple-element.31), channel_id=1, source_target_pairs={{0,32},{33,33},{2,34},{35,35},{4,36},{37,37},{6,38},{39,39},{8,40}... | collective-permute-start | bytes 245768 | tf_op jit(solution)/shard_map/ppermute | solution.py:203
  112.9 15.2 %collective-permute-start.20 = (bf16[160,256]{1,0:T(8,128)(2,1)S(1)}, bf16[160,256]{1,0:T(8,128)(2,1)S(1)}, u32[]{:S(2)}, u32[]{:S(2)}) collective-permute-start(bf16[160,256]{1,0:T(8,128)(2,1)S(1)} %get-tuple-element.32), channel_id=1, source_target_pairs={{0,48},{33,49},{2,50},{35,51},{4,52},{37,53},{6,54},{39,55},{8,56}... | collective-permute-start | bytes 245768 | tf_op jit(solution)/shard_map/ppermute | solution.py:203
  128.9 11.0 %all-to-all-start.2 = ((f32[8,32,256]{2,1,0:T(8,128)}), f32[8,32,256]{2,1,0:T(8,128)S(1)}, u32[]{:S(2)}, u32[]{:S(2)}) async-start(f32[8,32,256]{2,1,0:T(8,128)} %broadcast_in_dim.8), calls=%async_computation.2 | async-start | bytes 524288 | tf_op jit(solution)/shard_map/all_to_all | solution.py:209

commit v4 on v3

v4 whole, which is shorter than its diff:
```python
import jax
import jax.numpy as jnp
from jax import lax
from jax.experimental import pallas as pl
from jax.experimental.pallas import tpu as pltpu
from jax.sharding import Mesh, PartitionSpec as P

ZH, Y, C, ZL, X = 4, 4, 2, 2, 4
ROWS = ("zh", "y", "c")
REP = ("zl", "x")
ALL = ROWS + REP
TILE = 128


def flat(zh, y, c, zl, x):
    return (((zh * Y + y) * C + c) * ZL + zl) * X + x


def place_of(q, r):
    return (2 * (r % 2) + q // 2 + (q % 2) * (2 * (q // 2) - 1)) % Y


def piece_route():
    pairs = []
    for j in range(ZH * Y * C):
        for k in range(ZL * X):
            r = j // 4
            dx = (k % X - r % X) % X
            if k // X == r // X:
                near, far = 0, 3 if r // X == 0 else 1
            else:
                near, far = 1 if r // X == 0 else 3, 2
            zh = (j // (Y * C) + (far if dx < 2 else near)) % ZH
            pairs.append((j * (ZL * X) + k, flat(zh, place_of(j % 4, r), dx % 2, r // X, r % X)))
    return pairs


def ring_route(back):
    pairs = []
    for y in range(Y):
        for c in range(C):
            step = 1 if (c == 0) != back else -1
            pairs.append((y * C + c, (y + step) % Y * C + c))
    return pairs


def order_of(apart, parity):
    return jnp.where((apart & 1) == 0, 3 * (apart >> 1), 1 + (((3 - apart) >> 1) ^ parity))


def apart_of(q, odd, y):
    high, low = q >> 1, q & 1
    return (2 * odd + high + low * (2 * high - 1) - y) & 3


def assemble_body(count, core, y, odd, row, col, vals, dense, sems):
    dense[...] = jnp.zeros_like(dense)
    total = count[0, 0] + count[0, 1] + count[0, 2] + count[0, 3]

    @pl.loop(0, total)
    def _(k):
        at = col[0, k]
        q, sub = at >> 3, at & 7
        parity, pair = sub & 1, sub >> 1
        place = (parity ^ core[0]) * 16 + order_of(apart_of(q, odd[0], y[0]), parity) * 4 + pair
        down = pl.ds(pl.multiple_of(row[0, k] * TILE, TILE), TILE)
        across = pl.ds(pl.multiple_of(place * TILE, TILE), TILE)
        pltpu.make_async_copy(vals.at[0, k], dense.at[down, across], sems.at[k]).start()

    @pl.loop(0, total)
    def _(k):
        corner = (pl.ds(0, TILE), pl.ds(0, TILE))
        pltpu.make_async_copy(vals.at[0, k], dense.at[corner], sems.at[k]).wait()


def assemble(count, core, y, odd, row, col, vals, rows, cols):
    smem = pl.BlockSpec(memory_space=pltpu.SMEM)
    return pl.pallas_call(
        assemble_body,
        out_shape=jax.ShapeDtypeStruct((rows, cols), jnp.bfloat16),
        in_specs=[smem] * 6 + [pl.BlockSpec(memory_space=pltpu.HBM)],
        out_specs=pl.BlockSpec(memory_space=pltpu.VMEM),
        scratch_shapes=[pltpu.SemaphoreType.DMA((vals.shape[1],))],
        name="assemble",
    )(count, core, y, odd, row, col, vals)


def regroup(ids, parity, rows, both, outs, others):
    y, odd, owner, q_own = ids
    for i, out in enumerate(outs):
        pair = (y + (0, 3 - 2 * parity, 1 + 2 * parity, 2)[i]) & 3

        def load(q, at):
            place = order_of(apart_of(q, odd, y), parity) * 4 + pair
            part = rows[pl.ds(pl.multiple_of(place * TILE, TILE), TILE), :]
            if others is None:
                return part
            return part + others[pl.ds(pl.multiple_of(i * 4 * TILE + at, TILE), TILE), :].astype(jnp.float32)

        for q in range(4):
            out[q * TILE : (q + 1) * TILE, :] = load(q, q * TILE).astype(out.dtype)

        @pl.when(owner != 0)
        def _():
            at = pl.multiple_of(q_own * TILE, TILE)
            mine = load(q_own, at) + both[2 * pair + parity, :TILE, :].astype(jnp.float32)
            out[pl.ds(at, TILE), :] = mine.astype(out.dtype)


def send_body(core, y, odd, owner, q_own, rows, both, out):
    outs = [out.at[i * 4 * TILE : (i + 1) * 4 * TILE] for i in range(4)]
    regroup((y[0], odd[0], owner[0], q_own[0]), 1 - core[0], rows, both, outs, None)


def keep_body(core, y, odd, owner, q_own, rows, both, others, out0, out1, out2, out3):
    ids = (y[0], odd[0], owner[0], q_own[0])
    regroup(ids, core[0], rows, both, (out0, out1, out2, out3), others)


def call_regroup(body, ids, arrays, outs, name):
    smem, whole = pl.BlockSpec(memory_space=pltpu.SMEM), pl.BlockSpec(memory_space=pltpu.VMEM)
    return pl.pallas_call(
        body,
        out_shape=outs,
        in_specs=[smem] * len(ids) + [whole] * len(arrays),
        out_specs=jax.tree.map(lambda _: whole, outs),
        compiler_params=pltpu.CompilerParams(vmem_limit_bytes=16 << 20),
        name=name,
    )(*ids, *arrays)


def shards(features, inv_sqrt_degree, weight, tile_vals, tile_row, tile_col, tile_count, cotangent):
    bf16, f32 = jnp.bfloat16, jnp.float32
    nodes_block, width = features.shape
    zh, y, core = lax.axis_index("zh"), lax.axis_index("y"), lax.axis_index("c")
    replica, block = lax.axis_index(REP), lax.axis_index(ROWS)
    reps = ZL * X
    share = nodes_block // reps
    nodes = nodes_block * ZH * Y * C
    half = (lax.axis_index("x") + y // 2) % 2
    piece_rows = 4 * share
    cols = 2 * Y * piece_rows
    feats = lax.dynamic_index_in_dim(features.reshape(4, 2, share, width), half, 1, False)
    degs = lax.dynamic_index_in_dim(inv_sqrt_degree.reshape(4, 2, share), half, 1, False)
    piece = (feats.astype(f32) * degs.astype(f32)[:, :, None]).astype(bf16).reshape(piece_rows, width)
    deg_rows = jnp.pad(degs.reshape(2, width), ((0, 14), (0, 0)))
    piece = lax.ppermute(jnp.concatenate([piece, deg_rows], 0), ALL, piece_route())

    ids = [core.reshape(1), y.reshape(1), (replica % 2).reshape(1)]
    dense = assemble(tile_count, *ids, tile_row, tile_col, tile_vals, nodes_block, cols)
    piece, dense = lax.optimization_barrier((piece, dense))

    swap = [(0, 1), (1, 0)]
    ahead, behind = ring_route(False), ring_route(True)
    first = lax.ppermute(piece, ("y", "c"), ahead)
    second = lax.ppermute(piece, ("y", "c"), behind)
    third = lax.ppermute(first, ("y", "c"), ahead)
    pieces = (piece, first, second, third)
    partial = jnp.zeros((nodes_block, width), f32)
    for i, own_x in enumerate(pieces):
        other_x = lax.ppermute(own_x[:piece_rows], "c", swap)
        at = slice(i * piece_rows, (i + 1) * piece_rows)
        partial = partial + jnp.dot(dense[:, at], own_x[:piece_rows], preferred_element_type=f32)
        at = slice((4 + i) * piece_rows, (5 + i) * piece_rows)
        partial = partial + jnp.dot(dense[:, at], other_x, preferred_element_type=f32)

    start = replica * share
    deg = lax.dynamic_slice_in_dim(inv_sqrt_degree, start, share, 0).astype(f32)[:, None]
    scaled = (deg * lax.dynamic_slice_in_dim(features, start, share, 0).astype(f32)).astype(bf16)
    cot = lax.dynamic_slice_in_dim(cotangent, start, share, 0).astype(f32)
    chunk_deg = lax.dynamic_slice(
        jnp.stack([p[piece_rows:] for p in pieces]),
        (order_of(apart_of(zh, replica % 2, y), core), y // 2, (y % 2) * share),
        (1, 1, share),
    ).reshape(share, 1).astype(f32)
    partial = partial.astype(bf16)
    partial, scaled, cot, chunk_deg = lax.optimization_barrier((partial, scaled, cot, chunk_deg))
    parts = lax.all_to_all(partial.reshape(reps, share, width), REP, 0, 0)
    summed = jnp.sum(parts.astype(f32), 0)

    propagated = (deg * (summed + scaled.astype(f32))).astype(bf16)
    preact = jnp.dot(propagated, weight, preferred_element_type=f32)
    gate = jax.nn.sigmoid(preact)
    activated = (preact * gate).astype(bf16)
    grad_pre = (cot * gate * (1.0 + preact * (1.0 - gate))).astype(bf16)
    back = (
        deg * lax.dot_general(grad_pre, weight, (((1,), (1,)), ((), ())), preferred_element_type=f32)
    ).astype(bf16)
    local_grad = lax.dot_general(
        propagated, grad_pre, (((0,), (0,)), ((), ())), preferred_element_type=f32
    ) * (float(nodes) ** -0.5)

    slices = local_grad.astype(bf16).reshape(reps, width // reps, width)
    both = jnp.concatenate([jnp.broadcast_to(back[None], (reps, share, width)), slices], 1)
    both = lax.all_to_all(both, REP, 0, 0)
    back_block = both[:, :share].reshape(nodes_block, width)
    w_sum = jnp.sum(both[:, share:].astype(f32), 0)
    ids = ids + [(replica == block // 4).astype(jnp.int32).reshape(1), (block % 4).reshape(1)]

    def pull(at):
        return lax.dot_general(
            dense[:, at], back_block, (((0,), (0,)), ((), ())), preferred_element_type=f32
        )

    other_g = call_regroup(
        send_body, ids, (pull(slice(cols // 2, cols)), both), pltpu.VMEM((cols // 2, width), bf16), "regroup_send"
    )
    other_g = lax.ppermute(other_g, "c", swap)
    own_rows = pull(slice(0, cols // 2))
    kinds = (f32, bf16, f32, bf16)
    keep, straight, aside, relay = call_regroup(
        keep_body,
        ids,
        (own_rows, both, other_g),
        tuple(pltpu.VMEM((piece_rows, width), kind) for kind in kinds),
        "regroup_keep",
    )
    relayed = lax.ppermute(relay, ("y", "c"), ahead).astype(f32)
    direct = lax.ppermute(straight, ("y", "c"), behind).astype(f32)
    w_sum = w_sum + lax.ppermute(w_sum, "c", swap)
    w_part = w_sum
    w_part, relay, straight = lax.optimization_barrier((w_part, relay, straight))
    for m in range(1, 4):
        w_sum = w_sum + lax.ppermute(w_part, "zh", [(i, i ^ m) for i in range(ZH)])
    w_part = w_sum
    relayed = lax.ppermute((aside + relayed).astype(bf16), ("y", "c"), ahead).astype(f32)
    for m in range(1, 4):
        w_sum = w_sum + lax.ppermute(w_part, "y", [(i, (i + m) % Y) for i in range(Y)])
    chunks = (keep + direct + relayed).reshape(4, share, width)
    grad = lax.dynamic_index_in_dim(chunks, zh, 0, False)
    for m in range(1, 4):
        chunk = lax.dynamic_index_in_dim(chunks, zh ^ m, 0, False).astype(bf16)
        grad = grad + lax.ppermute(chunk, "zh", [(i, i ^ m) for i in range(ZH)]).astype(f32)
    feature_grad = (chunk_deg * grad).astype(bf16)
    weight_grad = lax.all_to_all(jnp.broadcast_to(w_sum[None], (reps,) + w_sum.shape), REP, 0, 0)
    return (activated, weight_grad.reshape(width, width), feature_grad)


def solution(mesh):
    fine = Mesh(mesh.devices.reshape(ZH, Y, C, ZL, X), ALL)
    placed = (
        P(ROWS, None),
        P(ROWS),
        P(),
        P(ROWS, REP, None, None),
        P(ROWS, REP),
        P(ROWS, REP),
        P(ROWS, REP),
        P(ROWS, None),
    )
    return jax.shard_map(
        shards,
        mesh=fine,
        in_specs=placed,
        out_specs=(P(ALL, None), P(), P(REP + ROWS, None)),
        check_vma=False,
    )
```

time: 142 us -> 126 us (0.89)
  blocking collectives: 27 us -> 12.9 us
  starting transfers between devices: 65.8 us -> 52.9 us
  waiting for transfers between devices: 19.2 us -> 28.2 us
    ppermute x18 -> x19, starting transfers between devices: 57.1 us -> 39.3 us  [the longest x3 11.6 us: shards(): w_sum = w_sum + lax.ppermute(w_part, 'zh', [(i, i ^ m) for i in range(ZH)])]
    all_to_all x2 -> x1, blocking collectives: 27 us -> 12.9 us  [shards(): parts = lax.all_to_all(partial.reshape(reps, share, width), REP, 0, 0)]
    all_to_all x0 -> x1, waiting for transfers between devices: none -> 8.34 us  [shards(): both = lax.all_to_all(both, REP, 0, 0)]
    all_to_all x0 -> x1, starting transfers between devices: none -> 5.26 us  [shards(): both = lax.all_to_all(both, REP, 0, 0)]
    all_to_all x1, waiting for transfers between devices: 4.77 us -> 0.81 us  [shards(): lax.all_to_all(jnp.broadcast_to(w_sum[None], (reps,) + w_sum.shape), REP,...]
    ppermute x1, waiting for transfers between devices: 0.84 us -> 4.64 us  [shards(): third = lax.ppermute(first, ('y', 'c'), ahead)]
    ppermute x1, starting transfers between devices: 0.57 us -> 3.22 us  [shards(): second = lax.ppermute(piece, ('y', 'c'), behind)]
    ppermute x1, starting transfers between devices: 2.62 us -> 0.08 us  [shards(): first = lax.ppermute(piece, ('y', 'c'), ahead)]
  transfers between devices with their start and end apart: 22 -> 24, of which waited for: 10 -> 10; matrix products, arithmetic and copies ran while one was open for 9% -> 9% of each run, Pallas kernels for 5% -> 6%
where the time goes in v4:
time: 126 us; the launch traced here: 125 us
  starting transfers between devices  52.9 us (42%)
  waiting for transfers between devices  28.2 us (22%)
  blocking collectives  12.9 us (10%)
  matrix products  12.8 us (10%)
  Pallas kernels  8.23 us (7%)
  other arithmetic  6.21 us (5%)
  local copies, waits for them, and re-layouts  2.66 us (2%)
    all_to_all x1, blocking collectives, shards(): parts = lax.all_to_all(partial.reshape(reps, share, width), REP, 0, 0)  12.9 us
    ppermute x3, starting transfers between devices, shards(): w_sum = w_sum + lax.ppermute(w_part, 'zh', [(i, i ^ m) for i in range(ZH)])  11.6 us
    all_to_all x1, waiting for transfers between devices, shards(): both = lax.all_to_all(both, REP, 0, 0)  8.34 us
    pallas_call x1, Pallas kernels, assemble(): pl.pallas_call(assemble_body, out_shape=jax.ShapeDtypeStruct((rows, cols)...  7.73 us
    ppermute x3, starting transfers between devices, shards(): lax.ppermute(chunk, 'zh', [(i, i ^ m) for i in range(ZH)]).astype(f32)  6.58 us
    ppermute x3, starting transfers between devices, shards(): lax.ppermute(w_part, 'y', [(i, (i + m) % Y) for i in range(Y)])  6.29 us
    ppermute x1, starting transfers between devices, shards(): lax.ppermute(jnp.concatenate([piece, deg_rows], 0), ALL, piece_route())  5.79 us
    all_to_all x1, starting transfers between devices, shards(): both = lax.all_to_all(both, REP, 0, 0)  5.26 us
  transfers between devices with their start and end apart: 24, of which 10 were waited for; matrix products, arithmetic and copies ran while one was open for 9% of the time, Pallas kernels for 6%

profile of v4, /device:TPU:2, one launch (start us, length us, event | category | flops | bytes accessed | tf_op | source)
XLA Modules:
  0.0 125.0 jit_solution(3529812582136996275)
XLA Ops:
  0.7 1.0 constant_dynamic-slice_fusion.1
  1.7 0.7 fusion.35
  2.4 0.1 fusion.25
  2.6 5.8 %collective-permute-start = (bf16[528,256]{1,0:T(8,128)(2,1)S(1)}, bf16[528,256]{1,0:T(8,128)(2,1)S(1)}, u32[]{:S(2)}, u32[]{:S(2)}) collective-permute-start(bf16[528,256]{1,0:T(8,128)(2,1)S(1)} %fusion.26), channel_id=1, source_target_pairs={{0,192},{1,200},{2,0},{3,8},{4,128},{5,136},{6,64},{7,72},{8,240},... | collective-permute-start | bytes 811016 | tf_op jit(solution)/shard_map/ppermute | solution.py:147
  8.4 0.8 dynamic-slice_convert_fusion.4
  9.1 7.7 %assemble.1 = bf16[1024,4096]{1,0:T(8,128)(2,1)} custom-call(s32[1,4]{1,0:T(1,128)} %count.1, s32[1]{0:T(128)} %bitcast.4.core, s32[1]{0:T(128)} %bitcast.5.y, s32[1]{0:T(128)} %bitcast.6.odd, s32[1,128]{1,0:T(1,128)} %row.1, s32[1,128]{1,0:T(1,128)} %col.1, bf16[1,128,128,128]{3,2,1,0:T(8,128)(2,1)} %vals.1), custom_call_target="tpu_custom_call" | custom-call | tf_op jit(solution)/shard_map/assemble/pallas_call | solution.py:78
  16.9 0.9 multiply_convert_fusion.3
  17.8 3.7 %collective-permute-start.1 = (bf16[512,256]{1,0:T(8,128)(2,1)S(1)}, bf16[512,256]{1,0:T(8,128)(2,1)S(1)}, u32[]{:S(2)}, u32[]{:S(2)}) collective-permute-start(bf16[512,256]{1,0:T(8,128)(2,1)S(1)} %slice.65), channel_id=1, source_target_pairs={{0,8},{8,0},{1,9},{9,1},{2,10},{10,2},{3,11},{11,3},{4,12},{12,4},... | collective-permute-start | bytes 786440 | tf_op jit(solution)/shard_map/ppermute | solution.py:161
  21.6 0.8 dynamic-slice_convert_fusion.3
  22.5 0.1 collective-permute-start.2
  22.6 3.2 %collective-permute-start.4 = (bf16[528,256]{1,0:T(8,128)(2,1)S(1)}, bf16[528,256]{1,0:T(8,128)(2,1)S(1)}, u32[]{:S(2)}, u32[]{:S(2)}) collective-permute-start(bf16[528,256]{1,0:T(8,128)(2,1)S(1)} %collective-permute-done), channel_id=1, source_target_pairs={{0,48},{8,24},{16,0},{24,40},{32,16},{40,56},{48,32},{56,8},{1,49}... | collective-permute-start | bytes 811016 | tf_op jit(solution)/shard_map/ppermute | solution.py:156
  25.8 1.7 %fusion.21 = f32[1024,256]{1,0:T(8,128)S(1)} fusion(bf16[512,256]{1,0:T(8,128)(2,1)S(1)} %collective-permute-done.1, bf16[1024,4096]{1,0:T(8,128)(2,1)} %assemble.1), kind=kOutput, calls=%fused_computation.27 | convolution fusion | flops 268435456 | bytes 2359296 | tf_op jit(solution)/shard_map/dot_general | solution.py:165
  27.4 1.7 %convolution_add_fusion.2 = f32[1024,256]{1,0:T(8,128)S(1)} fusion(f32[1024,256]{1,0:T(8,128)S(1)} %fusion.21, bf16[1024,4096]{1,0:T(8,128)(2,1)} %assemble.1, bf16[528,256]{1,0:T(8,128)(2,1)S(1)} %collective-permute-done), kind=kOutput, calls=%fused_computation.10 | convolution fusion | flops 268697600 | bytes 3407872 | tf_op jit(solution)/shard_map/dot_general | solution.py:163
  29.1 3.1 %collective-permute-done.2 = bf16[528,256]{1,0:T(8,128)(2,1)S(1)} collective-permute-done((bf16[528,256]{1,0:T(8,128)(2,1)S(1)}, bf16[528,256]{1,0:T(8,128)(2,1)S(1)}, u32[]{:S(2)}, u32[]{:S(2)}) %collective-permute-start.2) | collective-permute-done | bytes 270368 | tf_op jit(solution)/shard_map/ppermute | solution.py:155
  32.3 0.1 collective-permute-start.3
  32.4 0.6 collective-permute-start.5
  33.0 1.7 %fusion.16 = f32[1024,256]{1,0:T(8,128)S(1)} fusion(bf16[1024,4096]{1,0:T(8,128)(2,1)} %assemble.1, bf16[528,256]{1,0:T(8,128)(2,1)S(1)} %collective-permute-done.4), kind=kOutput, calls=%fused_computation.22 | convolution fusion | flops 268435456 | bytes 2359296 | tf_op jit(solution)/shard_map/dot_general | solution.py:163
  34.7 0.4 fusion.18
  35.1 0.4 fusion.14
  35.6 0.4 fusion.7
  36.0 4.6 %collective-permute-done.6 = bf16[528,256]{1,0:T(8,128)(2,1)S(1)} collective-permute-done((bf16[528,256]{1,0:T(8,128)(2,1)S(1)}, bf16[528,256]{1,0:T(8,128)(2,1)S(1)}, u32[]{:S(2)}, u32[]{:S(2)}) %collective-permute-start.6) | collective-permute-done | bytes 270368 | tf_op jit(solution)/shard_map/ppermute | solution.py:157
  40.7 0.1 collective-permute-start.7
  40.8 0.1 fusion.36
  40.9 1.4 %collective-permute-done.7 = bf16[512,256]{1,0:T(8,128)(2,1)S(1)} collective-permute-done((bf16[512,256]{1,0:T(8,128)(2,1)S(1)}, bf16[512,256]{1,0:T(8,128)(2,1)S(1)}, u32[]{:S(2)}, u32[]{:S(2)}) %collective-permute-start.7) | collective-permute-done | bytes 262176 | tf_op jit(solution)/shard_map/ppermute | solution.py:161
  42.3 0.4 fusion.11
  42.7 0.5 fusion.8
  43.2 12.9 %all_to_all.15 = bf16[8,128,256]{2,1,0:T(8,128)(2,1)S(1)} all-to-all(bf16[8,128,256]{2,1,0:T(8,128)(2,1)S(1)} %bitcast.60), channel_id=1, replica_groups=mesh['zh'=4,'y'=4,'c'=2,'zl'=2,'x'=4] {'zl','x'}, dimensions={0} | all-to-all | bytes 1048576 | tf_op jit(solution)/shard_map/all_to_all | solution.py:178
  56.2 0.1 convert_reduce_fusion
  56.2 0.1 multiply_convert_fusion.2
  56.3 0.2 fusion.41
  56.5 0.7 multiply_convert_fusion
  57.2 0.2 fusion.10
  57.4 0.2 fusion.9
  57.7 1.0 pad_maximum_fusion
  58.6 5.3 %all-to-all-start.1 = ((bf16[8,160,256]{2,1,0:T(8,128)(2,1)}), bf16[8,160,256]{2,1,0:T(8,128)(2,1)S(1)}, u32[]{:S(2)}, u32[]{:S(2)}) async-start(bf16[8,160,256]{2,1,0:T(8,128)(2,1)} %pad_maximum_fusion), calls=%async_computation.1 | async-start | bytes 1310720 | tf_op jit(solution)/shard_map/all_to_all | solution.py:195
  63.9 8.3 %all-to-all-done.1.both = bf16[8,160,256]{2,1,0:T(8,128)(2,1)S(1)} async-done(((bf16[8,160,256]{2,1,0:T(8,128)(2,1)}), bf16[8,160,256]{2,1,0:T(8,128)(2,1)S(1)}, u32[]{:S(2)}, u32[]{:S(2)}) %all-to-all-start.1) | async-done | bytes 655392 | tf_op jit(solution)/shard_map/all_to_all | solution.py:195
  72.3 3.7 %fusion.rows = f32[2048,256]{1,0:T(8,128)S(1)} fusion(bf16[1024,256]{1,0:T(8,128)(2,1)S(1)} %bitcast.65, bf16[1024,4096]{1,0:T(8,128)(2,1)} %assemble.1), kind=kOutput, calls=%fused_computation | convolution fusion | flops 1073741824 | bytes 6815744 | tf_op jit(solution)/shard_map/dot_general | solution.py:201
  76.0 0.3 regroup_send.1
  76.3 0.1 collective-permute-start.9
  76.4 0.6 collective-permute-start.8
  77.0 1.3 %fusion.2.rows = f32[2048,256]{1,0:T(8,128)S(1)} fusion(bf16[1024,256]{1,0:T(8,128)(2,1)S(1)} %bitcast.66, bf16[1024,4096]{1,0:T(8,128)(2,1)S(1)} %bitcast.59), kind=kOutput, calls=%fused_computation.2 | convolution fusion | flops 1073741824 | bytes 6815744 | tf_op jit(solution)/shard_map/dot_general | solution.py:201
  78.4 0.7 collective-permute-done.9.others
  79.1 0.2 regroup_keep.1
  79.3 0.1 collective-permute-start.17
  79.4 5.5 %collective-permute-start.10 = (f32[32,256]{1,0:T(8,128)S(1)}, f32[32,256]{1,0:T(8,128)S(1)}, u32[]{:S(2)}, u32[]{:S(2)}) collective-permute-start(f32[32,256]{1,0:T(8,128)S(1)} %add.165), channel_id=1, source_target_pairs={{0,64},{64,0},{128,192},{192,128},{1,65},{65,1},{129,193},{193,129... | collective-permute-start | bytes 98312 | tf_op jit(solution)/shard_map/ppermute | solution.py:224
  84.9 5.7 %collective-permute-start.11 = (f32[32,256]{1,0:T(8,128)S(1)}, f32[32,256]{1,0:T(8,128)S(1)}, u32[]{:S(2)}, u32[]{:S(2)}) collective-permute-start(f32[32,256]{1,0:T(8,128)S(1)} %add.165), channel_id=1, source_target_pairs={{0,128},{64,192},{128,0},{192,64},{1,129},{65,193},{129,1},{193,65... | collective-permute-start | bytes 98312 | tf_op jit(solution)/shard_map/ppermute | solution.py:224
  90.5 0.5 collective-permute-start.12
  91.0 3.2 %collective-permute-start.16 = (bf16[512,256]{1,0:T(8,128)(2,1)S(1)}, bf16[512,256]{1,0:T(8,128)(2,1)S(1)}, u32[]{:S(2)}, u32[]{:S(2)}) collective-permute-start(bf16[512,256]{1,0:T(8,128)(2,1)S(1)} %get-tuple-element.20), channel_id=1, source_target_pairs={{0,48},{8,24},{16,0},{24,40},{32,16},{40,56},{48,32},{56,8},{1,49}... | collective-permute-start | bytes 786440 | tf_op jit(solution)/shard_map/ppermute | solution.py:219
  94.2 2.4 %collective-permute-done.12 = f32[32,256]{1,0:T(8,128)S(1)} collective-permute-done((f32[32,256]{1,0:T(8,128)S(1)}, f32[32,256]{1,0:T(8,128)S(1)}, u32[]{:S(2)}, u32[]{:S(2)}) %collective-permute-start.12) | collective-permute-done | bytes 32800 | tf_op jit(solution)/shard_map/ppermute | solution.py:224
  96.7 1.2 collective-permute-start.13
  97.9 3.5 %collective-permute-start.14 = (f32[32,256]{1,0:T(8,128)S(1)}, f32[32,256]{1,0:T(8,128)S(1)}, u32[]{:S(2)}, u32[]{:S(2)}) collective-permute-start(f32[32,256]{1,0:T(8,128)S(1)} %add_add_fusion.1), channel_id=1, source_target_pairs={{0,32},{16,48},{32,0},{48,16},{1,33},{17,49},{33,1},{49,17},{2,34}... | collective-permute-start | bytes 98312 | tf_op jit(solution)/shard_map/ppermute | solution.py:228
  101.4 1.5 %collective-permute-start.15 = (f32[32,256]{1,0:T(8,128)S(1)}, f32[32,256]{1,0:T(8,128)S(1)}, u32[]{:S(2)}, u32[]{:S(2)}) collective-permute-start(f32[32,256]{1,0:T(8,128)S(1)} %add_add_fusion.1), channel_id=1, source_target_pairs={{0,48},{16,0},{32,16},{48,32},{1,49},{17,1},{33,17},{49,33},{2,50}... | collective-permute-start | bytes 98312 | tf_op jit(solution)/shard_map/ppermute | solution.py:228
  103.0 0.6 collective-permute-start.18
  103.7 2.1 %collective-permute-done.15 = f32[32,256]{1,0:T(8,128)S(1)} collective-permute-done((f32[32,256]{1,0:T(8,128)S(1)}, f32[32,256]{1,0:T(8,128)S(1)}, u32[]{:S(2)}, u32[]{:S(2)}) %collective-permute-start.15) | collective-permute-done | bytes 32800 | tf_op jit(solution)/shard_map/ppermute | solution.py:228
  105.8 0.7 broadcast_in_dim.5
  106.5 5.0 %all-to-all-start.2 = ((f32[8,32,256]{2,1,0:T(8,128)}), f32[8,32,256]{2,1,0:T(8,128)S(1)}, u32[]{:S(2)}, u32[]{:S(2)}) async-start(f32[8,32,256]{2,1,0:T(8,128)} %broadcast_in_dim.5), calls=%async_computation.2 | async-start | bytes 524288 | tf_op jit(solution)/shard_map/all_to_all | solution.py:235
  111.6 0.1 convert_add_fusion
  111.7 2.6 %collective-permute-start.19 = (bf16[128,256]{1,0:T(8,128)(2,1)S(1)}, bf16[128,256]{1,0:T(8,128)(2,1)S(1)}, u32[]{:S(2)}, u32[]{:S(2)}) collective-permute-start(bf16[128,256]{1,0:T(8,128)(2,1)S(1)} %get-tuple-element.25), channel_id=1, source_target_pairs={{0,64},{64,0},{128,192},{192,128},{1,65},{65,1},{129,193},{193,129... | collective-permute-start | bytes 196616 | tf_op jit(solution)/shard_map/ppermute | solution.py:233
  114.2 1.8 %collective-permute-start.20 = (bf16[128,256]{1,0:T(8,128)(2,1)S(1)}, bf16[128,256]{1,0:T(8,128)(2,1)S(1)}, u32[]{:S(2)}, u32[]{:S(2)}) collective-permute-start(bf16[128,256]{1,0:T(8,128)(2,1)S(1)} %get-tuple-element.27), channel_id=1, source_target_pairs={{0,128},{64,192},{128,0},{192,64},{1,129},{65,193},{129,1},{193,65... | collective-permute-start | bytes 196616 | tf_op jit(solution)/shard_map/ppermute | solution.py:233
  116.1 2.2 %collective-permute-start.21 = (bf16[128,256]{1,0:T(8,128)(2,1)S(1)}, bf16[128,256]{1,0:T(8,128)(2,1)S(1)}, u32[]{:S(2)}, u32[]{:S(2)}) collective-permute-start(bf16[128,256]{1,0:T(8,128)(2,1)S(1)} %get-tuple-element.26), channel_id=1, source_target_pairs={{0,192},{64,128},{128,64},{192,0},{1,193},{65,129},{129,65},{193,1... | collective-permute-start | bytes 196616 | tf_op jit(solution)/shard_map/ppermute | solution.py:233
  118.3 0.8 all-to-all-done.2
  119.1 4.5 %collective-permute-done.20 = bf16[128,256]{1,0:T(8,128)(2,1)S(1)} collective-permute-done((bf16[128,256]{1,0:T(8,128)(2,1)S(1)}, bf16[128,256]{1,0:T(8,128)(2,1)S(1)}, u32[]{:S(2)}, u32[]{:S(2)}) %collective-permute-start.20) | collective-permute-done | bytes 65568 | tf_op jit(solution)/shard_map/ppermute | solution.py:233
  123.6 0.7 fusion.30
  124.3 0.7 copy.12
  (43 shorter events, 0.5 us)
Async XLA Ops:
  0.6 55.7 %copy-start = (bf16[256,256]{1,0:T(8,128)(2,1)S(1)}, bf16[256,256]{1,0:T(8,128)(2,1)}, u32[]{:S(2)}) copy-start(bf16[256,256]{1,0:T(8,128)(2,1)} %param.10) | copy-start | bytes 393220
  2.6 15.2 %collective-permute-start = (bf16[528,256]{1,0:T(8,128)(2,1)S(1)}, bf16[528,256]{1,0:T(8,128)(2,1)S(1)}, u32[]{:S(2)}, u32[]{:S(2)}) collective-permute-start(bf16[528,256]{1,0:T(8,128)(2,1)S(1)} %fusion.26), channel_id=1, source_target_pairs={{0,192},{1,200},{2,0},{3,8},{4,128},{5,136},{6,64},{7,72},{8,240},... | collective-permute-start | bytes 811016 | tf_op jit(solution)/shard_map/ppermute | solution.py:147
  17.8 7.9 %collective-permute-start.1 = (bf16[512,256]{1,0:T(8,128)(2,1)S(1)}, bf16[512,256]{1,0:T(8,128)(2,1)S(1)}, u32[]{:S(2)}, u32[]{:S(2)}) collective-permute-start(bf16[512,256]{1,0:T(8,128)(2,1)S(1)} %slice.65), channel_id=1, source_target_pairs={{0,8},{8,0},{1,9},{9,1},{2,10},{10,2},{3,11},{11,3},{4,12},{12,4},... | collective-permute-start | bytes 786440 | tf_op jit(solution)/shard_map/ppermute | solution.py:161
  22.5 12.2 %copy-start.1 = (bf16[1024,4096]{1,0:T(8,128)(2,1)S(1)}, bf16[1024,4096]{1,0:T(8,128)(2,1)}, u32[]{:S(2)}) copy-start(bf16[1024,4096]{1,0:T(8,128)(2,1)} %assemble.1) | copy-start | bytes 25165828
  22.5 9.8 %collective-permute-start.2 = (bf16[528,256]{1,0:T(8,128)(2,1)S(1)}, bf16[528,256]{1,0:T(8,128)(2,1)S(1)}, u32[]{:S(2)}, u32[]{:S(2)}) collective-permute-start(bf16[528,256]{1,0:T(8,128)(2,1)S(1)} %collective-permute-done), channel_id=1, source_target_pairs={{0,16},{8,56},{16,32},{24,8},{32,48},{40,24},{48,0},{56,40},{1,17}... | collective-permute-start | bytes 811016 | tf_op jit(solution)/shard_map/ppermute | solution.py:155
  22.6 9.8 %collective-permute-start.4 = (bf16[528,256]{1,0:T(8,128)(2,1)S(1)}, bf16[528,256]{1,0:T(8,128)(2,1)S(1)}, u32[]{:S(2)}, u32[]{:S(2)}) collective-permute-start(bf16[528,256]{1,0:T(8,128)(2,1)S(1)} %collective-permute-done), channel_id=1, source_target_pairs={{0,48},{8,24},{16,0},{24,40},{32,16},{40,56},{48,32},{56,8},{1,49}... | collective-permute-start | bytes 811016 | tf_op jit(solution)/shard_map/ppermute | solution.py:156
  32.3 2.4 %collective-permute-start.3 = (bf16[512,256]{1,0:T(8,128)(2,1)S(1)}, bf16[512,256]{1,0:T(8,128)(2,1)S(1)}, u32[]{:S(2)}, u32[]{:S(2)}) collective-permute-start(bf16[512,256]{1,0:T(8,128)(2,1)S(1)} %slice.84), channel_id=1, source_target_pairs={{0,8},{8,0},{1,9},{9,1},{2,10},{10,2},{3,11},{11,3},{4,12},{12,4},... | collective-permute-start | bytes 786440 | tf_op jit(solution)/shard_map/ppermute | solution.py:161
  32.4 2.7 %collective-permute-start.5 = (bf16[512,256]{1,0:T(8,128)(2,1)S(1)}, bf16[512,256]{1,0:T(8,128)(2,1)S(1)}, u32[]{:S(2)}, u32[]{:S(2)}) collective-permute-start(bf16[512,256]{1,0:T(8,128)(2,1)S(1)} %slice.85), channel_id=1, source_target_pairs={{0,8},{8,0},{1,9},{9,1},{2,10},{10,2},{3,11},{11,3},{4,12},{12,4},... | collective-permute-start | bytes 786440 | tf_op jit(solution)/shard_map/ppermute | solution.py:161
  33.0 7.7 %collective-permute-start.6 = (bf16[528,256]{1,0:T(8,128)(2,1)S(1)}, bf16[528,256]{1,0:T(8,128)(2,1)S(1)}, u32[]{:S(2)}, u32[]{:S(2)}) collective-permute-start(bf16[528,256]{1,0:T(8,128)(2,1)S(1)} %collective-permute-done.2), channel_id=1, source_target_pairs={{0,16},{8,56},{16,32},{24,8},{32,48},{40,24},{48,0},{56,40},{1,17}... | collective-permute-start | bytes 811016 | tf_op jit(solution)/shard_map/ppermute | solution.py:157
  40.7 1.6 %collective-permute-start.7 = (bf16[512,256]{1,0:T(8,128)(2,1)S(1)}, bf16[512,256]{1,0:T(8,128)(2,1)S(1)}, u32[]{:S(2)}, u32[]{:S(2)}) collective-permute-start(bf16[512,256]{1,0:T(8,128)(2,1)S(1)} %slice.86), channel_id=1, source_target_pairs={{0,8},{8,0},{1,9},{9,1},{2,10},{10,2},{3,11},{11,3},{4,12},{12,4},... | collective-permute-start | bytes 786440 | tf_op jit(solution)/shard_map/ppermute | solution.py:161
  58.6 13.6 %all-to-all-start.1 = ((bf16[8,160,256]{2,1,0:T(8,128)(2,1)}), bf16[8,160,256]{2,1,0:T(8,128)(2,1)S(1)}, u32[]{:S(2)}, u32[]{:S(2)}) async-start(bf16[8,160,256]{2,1,0:T(8,128)(2,1)} %pad_maximum_fusion), calls=%async_computation.1 | async-start | bytes 1310720 | tf_op jit(solution)/shard_map/all_to_all | solution.py:195
  72.2 4.8 %slice-start = ((s8[8388608]{0:T(1024)(128)(4,1)}), s8[4194304]{0:T(1024)(128)(4,1)S(1)}, s32[]{:S(2)}) async-start(s8[8388608]{0:T(1024)(128)(4,1)} %bitcast.58), calls=%async_computation.3 | async-start | bytes 8388608
  72.3 4.8 %slice-start.1 = ((s8[8388608]{0:T(1024)(128)(4,1)}), s8[4194304]{0:T(1024)(128)(4,1)S(1)}, s32[]{:S(2)}) async-start(s8[8388608]{0:T(1024)(128)(4,1)} %bitcast.58), calls=%async_computation.4 | async-start | bytes 8388608
  76.3 2.7 %collective-permute-start.9 = (bf16[2048,256]{1,0:T(8,128)(2,1)S(1)}, bf16[2048,256]{1,0:T(8,128)(2,1)S(1)}, u32[]{:S(2)}, u32[]{:S(2)}) collective-permute-start(bf16[2048,256]{1,0:T(8,128)(2,1)S(1)} %regroup_send.1), channel_id=1, source_target_pairs={{0,8},{8,0},{1,9},{9,1},{2,10},{10,2},{3,11},{11,3},{4,12},{12,4},... | collective-permute-start | bytes 3145736 | tf_op jit(solution)/shard_map/ppermute | solution.py:208
  76.4 2.9 %collective-permute-start.8 = (f32[32,256]{1,0:T(8,128)S(1)}, f32[32,256]{1,0:T(8,128)S(1)}, u32[]{:S(2)}, u32[]{:S(2)}) collective-permute-start(f32[32,256]{1,0:T(8,128)S(1)} %convert_reduce_fusion.1), channel_id=1, source_target_pairs={{0,8},{8,0},{1,9},{9,1},{2,10},{10,2},{3,11},{11,3},{4,12},{12,4},... | collective-permute-start | bytes 98312 | tf_op jit(solution)/shard_map/ppermute | solution.py:220
  79.3 23.7 %collective-permute-start.17 = (bf16[512,256]{1,0:T(8,128)(2,1)S(1)}, bf16[512,256]{1,0:T(8,128)(2,1)S(1)}, u32[]{:S(2)}, u32[]{:S(2)}) collective-permute-start(bf16[512,256]{1,0:T(8,128)(2,1)S(1)} %get-tuple-element.19), channel_id=1, source_target_pairs={{0,16},{8,56},{16,32},{24,8},{32,48},{40,24},{48,0},{56,40},{1,17}... | collective-permute-start | bytes 786440 | tf_op jit(solution)/shard_map/ppermute | solution.py:218
  79.4 14.9 %collective-permute-start.10 = (f32[32,256]{1,0:T(8,128)S(1)}, f32[32,256]{1,0:T(8,128)S(1)}, u32[]{:S(2)}, u32[]{:S(2)}) collective-permute-start(f32[32,256]{1,0:T(8,128)S(1)} %add.165), channel_id=1, source_target_pairs={{0,64},{64,0},{128,192},{192,128},{1,65},{65,1},{129,193},{193,129... | collective-permute-start | bytes 98312 | tf_op jit(solution)/shard_map/ppermute | solution.py:224
  84.9 9.4 %collective-permute-start.11 = (f32[32,256]{1,0:T(8,128)S(1)}, f32[32,256]{1,0:T(8,128)S(1)}, u32[]{:S(2)}, u32[]{:S(2)}) collective-permute-start(f32[32,256]{1,0:T(8,128)S(1)} %add.165), channel_id=1, source_target_pairs={{0,128},{64,192},{128,0},{192,64},{1,129},{65,193},{129,1},{193,65... | collective-permute-start | bytes 98312 | tf_op jit(solution)/shard_map/ppermute | solution.py:224
  90.5 6.1 %collective-permute-start.12 = (f32[32,256]{1,0:T(8,128)S(1)}, f32[32,256]{1,0:T(8,128)S(1)}, u32[]{:S(2)}, u32[]{:S(2)}) collective-permute-start(f32[32,256]{1,0:T(8,128)S(1)} %add.165), channel_id=1, source_target_pairs={{0,192},{64,128},{128,64},{192,0},{1,193},{65,129},{129,65},{193,1... | collective-permute-start | bytes 98312 | tf_op jit(solution)/shard_map/ppermute | solution.py:224
  91.0 20.5 %collective-permute-start.16 = (bf16[512,256]{1,0:T(8,128)(2,1)S(1)}, bf16[512,256]{1,0:T(8,128)(2,1)S(1)}, u32[]{:S(2)}, u32[]{:S(2)}) collective-permute-start(bf16[512,256]{1,0:T(8,128)(2,1)S(1)} %get-tuple-element.20), channel_id=1, source_target_pairs={{0,48},{8,24},{16,0},{24,40},{32,16},{40,56},{48,32},{56,8},{1,49}... | collective-permute-start | bytes 786440 | tf_op jit(solution)/shard_map/ppermute | solution.py:219
  96.7 6.9 %collective-permute-start.13 = (f32[32,256]{1,0:T(8,128)S(1)}, f32[32,256]{1,0:T(8,128)S(1)}, u32[]{:S(2)}, u32[]{:S(2)}) collective-permute-start(f32[32,256]{1,0:T(8,128)S(1)} %add_add_fusion.1), channel_id=1, source_target_pairs={{0,16},{16,32},{32,48},{48,0},{1,17},{17,33},{33,49},{49,1},{2,18}... | collective-permute-start | bytes 98312 | tf_op jit(solution)/shard_map/ppermute | solution.py:228
  97.9 5.8 %collective-permute-start.14 = (f32[32,256]{1,0:T(8,128)S(1)}, f32[32,256]{1,0:T(8,128)S(1)}, u32[]{:S(2)}, u32[]{:S(2)}) collective-permute-start(f32[32,256]{1,0:T(8,128)S(1)} %add_add_fusion.1), channel_id=1, source_target_pairs={{0,32},{16,48},{32,0},{48,16},{1,33},{17,49},{33,1},{49,17},{2,34}... | collective-permute-start | bytes 98312 | tf_op jit(solution)/shard_map/ppermute | solution.py:228
  101.4 4.3 %collective-permute-start.15 = (f32[32,256]{1,0:T(8,128)S(1)}, f32[32,256]{1,0:T(8,128)S(1)}, u32[]{:S(2)}, u32[]{:S(2)}) collective-permute-start(f32[32,256]{1,0:T(8,128)S(1)} %add_add_fusion.1), channel_id=1, source_target_pairs={{0,48},{16,0},{32,16},{48,32},{1,49},{17,1},{33,17},{49,33},{2,50}... | collective-permute-start | bytes 98312 | tf_op jit(solution)/shard_map/ppermute | solution.py:228
  103.0 8.5 %collective-permute-start.18 = (bf16[512,256]{1,0:T(8,128)(2,1)S(1)}, bf16[512,256]{1,0:T(8,128)(2,1)S(1)}, u32[]{:S(2)}, u32[]{:S(2)}) collective-permute-start(bf16[512,256]{1,0:T(8,128)(2,1)S(1)} %add_convert_fusion), channel_id=1, source_target_pairs={{0,16},{8,56},{16,32},{24,8},{32,48},{40,24},{48,0},{56,40},{1,17}... | collective-permute-start | bytes 786440 | tf_op jit(solution)/shard_map/ppermute | solution.py:226
  106.5 12.6 %all-to-all-start.2 = ((f32[8,32,256]{2,1,0:T(8,128)}), f32[8,32,256]{2,1,0:T(8,128)S(1)}, u32[]{:S(2)}, u32[]{:S(2)}) async-start(f32[8,32,256]{2,1,0:T(8,128)} %broadcast_in_dim.5), calls=%async_computation.2 | async-start | bytes 524288 | tf_op jit(solution)/shard_map/all_to_all | solution.py:235
  111.7 7.4 %collective-permute-start.19 = (bf16[128,256]{1,0:T(8,128)(2,1)S(1)}, bf16[128,256]{1,0:T(8,128)(2,1)S(1)}, u32[]{:S(2)}, u32[]{:S(2)}) collective-permute-start(bf16[128,256]{1,0:T(8,128)(2,1)S(1)} %get-tuple-element.25), channel_id=1, source_target_pairs={{0,64},{64,0},{128,192},{192,128},{1,65},{65,1},{129,193},{193,129... | collective-permute-start | bytes 196616 | tf_op jit(solution)/shard_map/ppermute | solution.py:233
  114.2 9.4 %collective-permute-start.20 = (bf16[128,256]{1,0:T(8,128)(2,1)S(1)}, bf16[128,256]{1,0:T(8,128)(2,1)S(1)}, u32[]{:S(2)}, u32[]{:S(2)}) collective-permute-start(bf16[128,256]{1,0:T(8,128)(2,1)S(1)} %get-tuple-element.27), channel_id=1, source_target_pairs={{0,128},{64,192},{128,0},{192,64},{1,129},{65,193},{129,1},{193,65... | collective-permute-start | bytes 196616 | tf_op jit(solution)/shard_map/ppermute | solution.py:233
  116.1 7.5 %collective-permute-start.21 = (bf16[128,256]{1,0:T(8,128)(2,1)S(1)}, bf16[128,256]{1,0:T(8,128)(2,1)S(1)}, u32[]{:S(2)}, u32[]{:S(2)}) collective-permute-start(bf16[128,256]{1,0:T(8,128)(2,1)S(1)} %get-tuple-element.26), channel_id=1, source_target_pairs={{0,192},{64,128},{128,64},{192,0},{1,193},{65,129},{129,65},{193,1... | collective-permute-start | bytes 196616 | tf_op jit(solution)/shard_map/ppermute | solution.py:233

commit v5 on v4

v5 whole, which is shorter than its diff:
```python
import jax
import jax.numpy as jnp
from jax import lax
from jax.experimental import pallas as pl
from jax.experimental.pallas import tpu as pltpu
from jax.sharding import Mesh, PartitionSpec as P

ZH, Y, C, ZL, X = 4, 4, 2, 2, 4
ROWS = ("zh", "y", "c")
REP = ("zl", "x")
ALL = ROWS + REP
TILE = 128
PIECE = 4 * TILE
WROWS = 64
BF16, F32 = jnp.bfloat16, jnp.float32
SMEM = pl.BlockSpec(memory_space=pltpu.SMEM)
WHOLE = pl.BlockSpec(memory_space=pltpu.VMEM)
HBM = pl.BlockSpec(memory_space=pltpu.HBM)


def flat(zh, y, c, zl, x):
    return (((zh * Y + y) * C + c) * ZL + zl) * X + x


def place_of(q, r):
    return (2 * (r % 2) + q // 2 + (q % 2) * (2 * (q // 2) - 1)) % Y


def piece_route():
    pairs = []
    for j in range(ZH * Y * C):
        for k in range(ZL * X):
            r = j // 4
            dx = (k % X - r % X) % X
            if k // X == r // X:
                near, far = 0, 3 if r // X == 0 else 1
            else:
                near, far = 1 if r // X == 0 else 3, 2
            zh = (j // (Y * C) + (far if dx < 2 else near)) % ZH
            pairs.append((j * (ZL * X) + k, flat(zh, place_of(j % 4, r), dx % 2, r // X, r % X)))
    return pairs


def ring_route(back):
    pairs = []
    for y in range(Y):
        for c in range(C):
            step = 1 if (c == 0) != back else -1
            pairs.append((y * C + c, (y + step) % Y * C + c))
    return pairs


def order_of(apart, parity):
    return jnp.where((apart & 1) == 0, 3 * (apart >> 1), 1 + (((3 - apart) >> 1) ^ parity))


def apart_of(q, odd, y):
    high, low = q >> 1, q & 1
    return (2 * odd + high + low * (2 * high - 1) - y) & 3


def down(row):
    square = jnp.transpose(jnp.broadcast_to(row, (TILE, TILE)))
    return jnp.concatenate([square, square], 1)


def call(body, name, outs, scalars, arrays, specs=None, scratch=(), limit=16):
    return pl.pallas_call(
        body,
        out_shape=outs,
        in_specs=[SMEM] * len(scalars) + (specs or [WHOLE] * len(arrays)),
        out_specs=jax.tree.map(lambda _: WHOLE, outs),
        scratch_shapes=list(scratch),
        compiler_params=pltpu.CompilerParams(vmem_limit_bytes=limit << 20),
        name=name,
    )(*scalars, *arrays)


def piece_body(half, degrees, features, out, tiles, sems):
    def copy(k):
        at = pl.ds(pl.multiple_of((2 * k + half[0]) * TILE, TILE), TILE)
        return pltpu.make_async_copy(features.at[at], tiles.at[k], sems.at[k])

    for k in range(4):
        copy(k).start()
    all_rows = degrees[...].astype(F32)
    line = lax.broadcasted_iota(jnp.int32, (16, TILE), 0)
    below = jnp.zeros((16, TILE), F32)
    columns = []
    for k in range(4):
        row = jnp.where(half[0] == 0, all_rows[2 * k : 2 * k + 1], all_rows[2 * k + 1 : 2 * k + 2])
        below = jnp.where(line == k, jnp.broadcast_to(row, (16, TILE)), below)
        columns.append(down(row))
    out[PIECE : PIECE + 16, :] = jnp.concatenate([below, below], 1).astype(BF16)
    for k in range(4):
        copy(k).wait()
        out[k * TILE : (k + 1) * TILE, :] = (columns[k] * tiles[k].astype(F32)).astype(BF16)


def share_body(replica, degrees, features, cotangent, scaled, cot, deg, tile, sems):
    at = pl.ds(pl.multiple_of(replica[0] * TILE, TILE), TILE)
    first = pltpu.make_async_copy(features.at[at], tile, sems.at[0])
    second = pltpu.make_async_copy(cotangent.at[at], cot, sems.at[1])
    first.start()
    second.start()
    line = lax.broadcasted_iota(jnp.int32, (8, TILE), 0)
    row = jnp.sum(jnp.where(line == replica[0], degrees[...].astype(F32), 0.0), 0, keepdims=True)
    column = down(row)
    deg[...] = column
    first.wait()
    scaled[...] = (column * tile[...].astype(F32)).astype(BF16)
    second.wait()


def assemble_body(count, core, y, odd, row, col, vals, own, other, dense, sems, out_sems):
    dense[...] = jnp.zeros_like(dense)
    total = count[0, 0] + count[0, 1] + count[0, 2] + count[0, 3]

    @pl.loop(0, total)
    def _(k):
        at = col[0, k]
        q, sub = at >> 3, at & 7
        parity, pair = sub & 1, sub >> 1
        place = (parity ^ core[0]) * 16 + order_of(apart_of(q, odd[0], y[0]), parity) * 4 + pair
        rows = pl.ds(pl.multiple_of(row[0, k] * TILE, TILE), TILE)
        cols = pl.ds(pl.multiple_of(place * TILE, TILE), TILE)
        pltpu.make_async_copy(vals.at[0, k], dense.at[rows, cols], sems.at[k]).start()

    @pl.loop(0, total)
    def _(k):
        corner = (pl.ds(0, TILE), pl.ds(0, TILE))
        pltpu.make_async_copy(vals.at[0, k], dense.at[corner], sems.at[k]).wait()

    width = own.shape[1]
    halves = [
        pltpu.make_async_copy(dense.at[:, pl.ds(i * width, width)], out, out_sems.at[i])
        for i, out in enumerate((own, other))
    ]
    for half in halves:
        half.start()
    for half in halves:
        half.wait()


def assemble(count, ids, row, col, vals, rows, cols):
    half = jax.ShapeDtypeStruct((rows, cols), BF16)
    return pl.pallas_call(
        assemble_body,
        out_shape=(half, half),
        in_specs=[SMEM] * 6 + [HBM],
        out_specs=(HBM, HBM),
        scratch_shapes=[
            pltpu.VMEM((rows, 2 * cols), BF16),
            pltpu.SemaphoreType.DMA((vals.shape[1],)),
            pltpu.SemaphoreType.DMA((2,)),
        ],
        name="assemble",
    )(count, *ids, row, col, vals)


def middle_body(factor, parts, scaled, cot, deg, weight, activated, both):
    summed = parts[0].astype(F32)
    for s in range(1, ZL * X):
        summed += parts[s].astype(F32)
    column = deg[...]
    propagated = (column * (summed + scaled[...].astype(F32))).astype(BF16)
    preact = jnp.dot(propagated, weight[...], preferred_element_type=F32)
    gate = jax.nn.sigmoid(preact)
    activated[...] = (preact * gate).astype(BF16)
    grad_pre = (cot[...].astype(F32) * gate * (1.0 + preact * (1.0 - gate))).astype(BF16)
    back = lax.dot_general(grad_pre, weight[...], (((1,), (1,)), ((), ())), preferred_element_type=F32)
    back = (column * back).astype(BF16)
    grad = lax.dot_general(propagated, grad_pre, (((0,), (0,)), ((), ())), preferred_element_type=F32)
    grad = (grad * factor).astype(BF16)
    for s in range(ZL * X):
        part = s // X * 2 + s % 2
        both[s, :TILE, :] = back
        both[s, TILE:, :] = grad[part * WROWS : (part + 1) * WROWS]


def regroup(ids, parity, rows, both, outs, others):
    y, odd, owner, q_own = ids
    for i, out in enumerate(outs):
        pair = (y + (0, 3 - 2 * parity, 1 + 2 * parity, 2)[i]) & 3

        def load(q, at):
            place = order_of(apart_of(q, odd, y), parity) * 4 + pair
            part = rows[pl.ds(pl.multiple_of(place * TILE, TILE), TILE), :]
            if others is None:
                return part
            return part + others[pl.ds(pl.multiple_of(i * PIECE + at, TILE), TILE), :].astype(F32)

        for q in range(4):
            out[q * TILE : (q + 1) * TILE, :] = load(q, q * TILE).astype(out.dtype)

        @pl.when(owner != 0)
        def _():
            at = pl.multiple_of(q_own * TILE, TILE)
            mine = load(q_own, at) + both[2 * pair + parity, :TILE, :].astype(F32)
            out[pl.ds(at, TILE), :] = mine.astype(out.dtype)


def slice_sum(both):
    total = both[0, TILE:, :].astype(F32)
    for s in range(1, ZL * X):
        total += both[s, TILE:, :].astype(F32)
    return total.astype(BF16)


def send_body(core, y, odd, owner, q_own, rows, both, out):
    outs = [out.at[i * PIECE : (i + 1) * PIECE] for i in range(4)]
    regroup((y[0], odd[0], owner[0], q_own[0]), 1 - core[0], rows, both, outs, None)
    out[4 * PIECE :, :] = slice_sum(both)


def keep_body(core, y, odd, owner, q_own, rows, both, others, keep, straight, aside, relay, w_own):
    outs = (keep, straight.at[:PIECE], aside, relay.at[:PIECE])
    regroup((y[0], odd[0], owner[0], q_own[0]), core[0], rows, both, outs, others)
    w_rows = (slice_sum(both).astype(F32) + others[4 * PIECE :, :].astype(F32)).astype(BF16)
    straight[PIECE:, :] = w_rows
    relay[PIECE:, :] = w_rows
    w_own[...] = w_rows


def relay_body(aside, came, out):
    out[:PIECE, :] = (aside[...] + came[:PIECE, :].astype(F32)).astype(BF16)
    out[PIECE:, :] = came[PIECE:, :]


def spread_body(zh, keep, direct, relayed, first, w_own, own, out1, out2, out3, w_out):
    w_rows = w_own[...].astype(F32) + first[PIECE:, :].astype(F32)
    w_rows = (w_rows + (direct[PIECE:, :].astype(F32) + relayed[PIECE:, :].astype(F32))).astype(BF16)
    w_out[...] = w_rows
    for m, out in enumerate((own, out1, out2, out3)):
        at = pl.ds(pl.multiple_of((zh[0] ^ m) * TILE, TILE), TILE)
        chunk = keep[at, :] + direct[at, :].astype(F32) + relayed[at, :].astype(F32)
        out[:TILE, :] = chunk.astype(out.dtype)
        if m:
            out[TILE:, :] = w_rows


def last_body(core, y, odd, zh, own, came1, came2, came3, w_rows, p0, p1, p2, p3, grad, w_out):
    order = order_of(apart_of(zh[0], odd[0], y[0]), core[0])
    below = jnp.zeros((16, TILE), F32)
    for i, piece in enumerate((p0, p1, p2, p3)):
        below = jnp.where(order == i, piece[PIECE:, :TILE].astype(F32), below)
    line = lax.broadcasted_iota(jnp.int32, (16, TILE), 0)
    row = jnp.sum(jnp.where(line == y[0], below, 0.0), 0, keepdims=True)
    total = own[...]
    w_sum = w_rows[...].astype(F32)
    for came in (came1, came2, came3):
        total += came[:TILE, :].astype(F32)
        w_sum += came[TILE:, :].astype(F32)
    grad[...] = (down(row) * total).astype(BF16)
    w_out[...] = w_sum


def join_body(zl, xl, mine, over_z, over_x, over_both, out):
    for part, flip_z, flip_x in ((mine, 0, 0), (over_z, 1, 0), (over_x, 0, 1), (over_both, 1, 1)):
        at = ((zl[0] ^ flip_z) * 2 + (xl[0] ^ flip_x)) * WROWS
        out[pl.ds(pl.multiple_of(at, WROWS), WROWS), :] = part[...]


def shards(features, inv_sqrt_degree, weight, tile_vals, tile_row, tile_col, tile_count, cotangent):
    nodes_block, width = features.shape
    zh, y, core, zl, x = (lax.axis_index(a).reshape(1) for a in ALL)
    replica, block = lax.axis_index(REP), lax.axis_index(ROWS)
    nodes = nodes_block * ZH * Y * C
    cols = Y * PIECE
    odd = x & 1
    degrees = inv_sqrt_degree.reshape(nodes_block // TILE, TILE)

    def held(rows, kind=BF16):
        return pltpu.VMEM((rows, width), kind)

    piece = call(
        piece_body, "piece", held(PIECE + 16), [(x + (y >> 1)) & 1], [degrees, features], [WHOLE, HBM],
        [pltpu.VMEM((4, TILE, width), BF16), pltpu.SemaphoreType.DMA((4,))],
    )
    piece = lax.ppermute(piece, ALL, piece_route())
    scaled, cot, deg = call(
        share_body, "share", (held(TILE), held(TILE), held(TILE, F32)), [replica.reshape(1)],
        [degrees, features, cotangent], [WHOLE, HBM, HBM],
        [pltpu.VMEM((TILE, width), BF16), pltpu.SemaphoreType.DMA((2,))],
    )
    own_a, other_a = assemble(tile_count, [core, y, odd], tile_row, tile_col, tile_vals, nodes_block, cols)
    piece, own_a, other_a = lax.optimization_barrier((piece, own_a, other_a))

    swap = [(0, 1), (1, 0)]
    ahead, behind = ring_route(False), ring_route(True)
    first = lax.ppermute(piece, ("y", "c"), ahead)
    second = lax.ppermute(piece, ("y", "c"), behind)
    third = lax.ppermute(first, ("y", "c"), ahead)
    pieces = [piece, first, second, third]
    partial = jnp.zeros((nodes_block, width), F32)
    for i, own_x in enumerate(pieces):
        other_x = lax.ppermute(own_x, "c", swap)
        at = slice(i * PIECE, (i + 1) * PIECE)
        partial = partial + jnp.dot(own_a[:, at], own_x[:PIECE], preferred_element_type=F32)
        partial = partial + jnp.dot(other_a[:, at], other_x[:PIECE], preferred_element_type=F32)
    partial, scaled, cot, deg = lax.optimization_barrier((partial.astype(BF16), scaled, cot, deg))
    parts = lax.all_to_all(partial.reshape(ZL * X, TILE, width), REP, 0, 0)
    activated, both = call(
        lambda *refs: middle_body(float(nodes) ** -0.5, *refs),
        "middle",
        (jax.ShapeDtypeStruct((TILE, width), BF16), pltpu.VMEM((ZL * X, TILE + WROWS, width), BF16)),
        [],
        [parts, scaled, cot, deg, weight],
    )
    both = lax.all_to_all(both, REP, 0, 0)
    back_block = both[:, :TILE].reshape(nodes_block, width)
    ids = [core, y, odd, (replica == block // 4).astype(jnp.int32).reshape(1), (block % 4).reshape(1)]

    def pull(a):
        return lax.dot_general(a, back_block, (((0,), (0,)), ((), ())), preferred_element_type=F32)

    others = call(send_body, "regroup_send", held(cols + WROWS), ids, [pull(other_a), both])
    others = lax.ppermute(others, "c", swap)
    keep, straight, aside, relay, w_own = call(
        keep_body,
        "regroup_keep",
        (held(PIECE, F32), held(PIECE + WROWS), held(PIECE, F32), held(PIECE + WROWS), held(WROWS)),
        ids,
        [pull(own_a), both, others],
    )
    came = lax.ppermute(relay, ("y", "c"), ahead)
    direct = lax.ppermute(straight, ("y", "c"), behind)
    relayed = call(relay_body, "relay", held(PIECE + WROWS), [], [aside, came])
    relayed = lax.ppermute(relayed, ("y", "c"), ahead)
    own, *sent, w_rows = call(
        spread_body,
        "spread",
        (held(TILE, F32), held(TILE + WROWS), held(TILE + WROWS), held(TILE + WROWS), held(WROWS)),
        [zh],
        [keep, direct, relayed, came, w_own],
    )
    got = [lax.ppermute(sent[m - 1], "zh", [(i, i ^ m) for i in range(ZH)]) for m in range(1, 4)]
    feature_grad, w_mine = call(
        last_body,
        "last",
        (jax.ShapeDtypeStruct((TILE, width), BF16), held(WROWS, F32)),
        [core, y, odd, zh],
        [own, *got, w_rows, *pieces],
    )
    flip = [(i, i ^ 1) for i in range(X)]
    over_z = lax.ppermute(w_mine, "zl", swap)
    over_x = lax.ppermute(w_mine, "x", flip)
    over_both = lax.ppermute(over_z, "x", flip)
    weight_grad = call(
        join_body,
        "join",
        jax.ShapeDtypeStruct((width, width), F32),
        [zl, x & 1],
        [w_mine, over_z, over_x, over_both],
    )
    return (activated, weight_grad, feature_grad)


def solution(mesh):
    fine = Mesh(mesh.devices.reshape(ZH, Y, C, ZL, X), ALL)
    placed = (
        P(ROWS, None),
        P(ROWS),
        P(),
        P(ROWS, REP, None, None),
        P(ROWS, REP),
        P(ROWS, REP),
        P(ROWS, REP),
        P(ROWS, None),
    )
    return jax.shard_map(
        shards,
        mesh=fine,
        in_specs=placed,
        out_specs=(P(ALL, None), P(), P(REP + ROWS, None)),
        check_vma=False,
    )
```

time: 126 us -> 126 us (level)
  waiting for transfers between devices: 28.2 us -> 46.8 us
  starting transfers between devices: 52.9 us -> 38.7 us
  other arithmetic: 6.21 us -> 0 us
  Pallas kernels: 8.23 us -> 11.7 us
  matrix products: 12.8 us -> 11.1 us
  blocking collectives: 12.9 us -> 14.2 us
    ppermute x19 -> x15, waiting for transfers between devices: 11.2 us -> 28.7 us  [the longest x1 7.91 us: shards(): relayed = lax.ppermute(relayed, ('y', 'c'), ahead)]
    ppermute x19 -> x15, starting transfers between devices: 39.3 us -> 30 us  [the longest x3 13.4 us: shards(): lax.ppermute(sent[m - 1], 'zh', [(i, i ^ m) for i in range(ZH)])]
    all_to_all x1 -> x0, starting transfers between devices: 5.05 us -> none  [shards(): lax.all_to_all(jnp.broadcast_to(w_sum[None], (reps,) + w_sum.shape), REP,...]
    convert_element_type x10 -> x0, other arithmetic: 5.03 us -> none  [the longest x1 0.93 us: shards(): (deg * lax.dynamic_slice_in_dim(features, start, share, 0).astype(f32)).a...]
    pallas_call x3 -> x10, Pallas kernels: 8.23 us -> 11.7 us  [the longest x1 7.5 us: assemble(): pl.pallas_call(assemble_body, out_shape=(half, half), in_specs=[SMEM] * 6...]
    all_to_all x1, waiting for transfers between devices: 8.34 us -> 10.3 us  [shards(): both = lax.all_to_all(both, REP, 0, 0)]
    dot_general x13 -> x10, matrix products: 12.8 us -> 11.1 us  [the longest x2 5.03 us: pull(): lax.dot_general(a, back_block, (((0,), (0,)), ((), ())), preferred_elemen...]
  transfers between devices with their start and end apart: 24 -> 19, of which waited for: 10 -> 12; matrix products, arithmetic and copies ran while one was open for 9% -> 6% of each run, Pallas kernels for 6% -> 6%
where the time goes in v5:
time: 126 us; the launch traced here: 125 us
  waiting for transfers between devices  46.8 us (37%)
  starting transfers between devices  38.7 us (31%)
  blocking collectives  14.2 us (11%)
  Pallas kernels  11.7 us (9%)
  matrix products  11.1 us (9%)
  local copies, waits for them, and re-layouts  1.78 us (1%)
    all_to_all x1, blocking collectives, shards(): parts = lax.all_to_all(partial.reshape(ZL * X, TILE, width), REP, 0, 0)  14.2 us
    ppermute x3, starting transfers between devices, shards(): lax.ppermute(sent[m - 1], 'zh', [(i, i ^ m) for i in range(ZH)])  13.4 us
    all_to_all x1, waiting for transfers between devices, shards(): both = lax.all_to_all(both, REP, 0, 0)  10.3 us
    ppermute x1, waiting for transfers between devices, shards(): relayed = lax.ppermute(relayed, ('y', 'c'), ahead)  7.91 us
    pallas_call x1, Pallas kernels, assemble(): pl.pallas_call(assemble_body, out_shape=(half, half), in_specs=[SMEM] * 6...  7.5 us
    ppermute x1, waiting for transfers between devices, shards(): came = lax.ppermute(relay, ('y', 'c'), ahead)  7.11 us
    ppermute x3, waiting for transfers between devices, shards(): lax.ppermute(sent[m - 1], 'zh', [(i, i ^ m) for i in range(ZH)])  6.97 us
    ppermute x1, starting transfers between devices, shards(): piece = lax.ppermute(piece, ALL, piece_route())  5.79 us
  transfers between devices with their start and end apart: 19, of which 12 were waited for; matrix products, arithmetic and copies ran while one was open for 6% of the time, Pallas kernels for 6%

profile of v5, /device:TPU:2, one launch (start us, length us, event | category | flops | bytes accessed | tf_op | source)
XLA Modules:
  0.0 125.2 jit_solution(7297039547213494628)
XLA Ops:
  0.6 0.0 copy-start.5
  0.6 0.0 copy-start
  0.7 1.0 copy-done
  1.7 0.7 copy-done.4
  2.4 0.6 piece.1
  3.0 5.8 %collective-permute-start = (bf16[528,256]{1,0:T(8,128)(2,1)S(1)}, bf16[528,256]{1,0:T(8,128)(2,1)S(1)}, u32[]{:S(2)}, u32[]{:S(2)}) collective-permute-start(bf16[528,256]{1,0:T(8,128)(2,1)S(1)} %piece.1), channel_id=1, source_target_pairs={{0,192},{1,200},{2,0},{3,8},{4,128},{5,136},{6,64},{7,72},{8,240},... | collective-permute-start | bytes 811016 | tf_op jit(solution)/shard_map/ppermute | solution.py:280
  8.7 7.5 %assemble.1 = (bf16[1024,2048]{1,0:T(8,128)(2,1)}, bf16[1024,2048]{1,0:T(8,128)(2,1)}) custom-call(s32[1,4]{1,0:T(1,128)} %count.1, s32[1]{0:T(128)} %bitcast.3.core, s32[1]{0:T(128)} %bitcast.1.y, s32[1]{0:T(128)S(6)} %and.23.odd.xl, s32[1,128]{1,0:T(1,128)} %row.1, s32[1,128]{1,0:T(1,128)} %col.1, bf16[1,128,128,128]{3,2,1,0:T(8,128)(2,1)} %vals.1), custom_call_target="tpu_custom_call" | custom-call | tf_op jit(solution)/shard_map/assemble/pallas_call | solution.py:147
  16.3 0.0 collective-permute-done.p0
  16.3 2.2 %collective-permute-start.1 = (bf16[528,256]{1,0:T(8,128)(2,1)S(1)}, bf16[528,256]{1,0:T(8,128)(2,1)S(1)}, u32[]{:S(2)}, u32[]{:S(2)}) collective-permute-start(bf16[528,256]{1,0:T(8,128)(2,1)S(1)} %collective-permute-done.p0), channel_id=1, source_target_pairs={{0,8},{8,0},{1,9},{9,1},{2,10},{10,2},{3,11},{11,3},{4,12},{12,4},... | collective-permute-start | bytes 811016 | tf_op jit(solution)/shard_map/ppermute | solution.py:297
  18.5 0.0 copy-done.5
  18.5 0.3 share.1
  18.8 0.9 collective-permute-start.2
  19.7 2.5 %collective-permute-start.4 = (bf16[528,256]{1,0:T(8,128)(2,1)S(1)}, bf16[528,256]{1,0:T(8,128)(2,1)S(1)}, u32[]{:S(2)}, u32[]{:S(2)}) collective-permute-start(bf16[528,256]{1,0:T(8,128)(2,1)S(1)} %collective-permute-done.p0), channel_id=1, source_target_pairs={{0,48},{8,24},{16,0},{24,40},{32,16},{40,56},{48,32},{56,8},{1,49}... | collective-permute-start | bytes 811016 | tf_op jit(solution)/shard_map/ppermute | solution.py:292
  22.2 0.0 collective-permute-done.1
  22.2 1.7 %fusion.11 = f32[1024,256]{1,0:T(8,128)S(1)} fusion(bf16[1024,2048]{1,0:T(8,128)(2,1)} %get-tuple-element.33, bf16[528,256]{1,0:T(8,128)(2,1)S(1)} %collective-permute-done.1), kind=kOutput, calls=%fused_computation.16 | convolution fusion | flops 268435456 | bytes 2359296 | tf_op jit(solution)/shard_map/dot_general | solution.py:300
  23.8 1.8 %convolution_add_fusion.4 = f32[1024,256]{1,0:T(8,128)S(1)} fusion(f32[1024,256]{1,0:T(8,128)S(1)} %fusion.11, bf16[1024,2048]{1,0:T(8,128)(2,1)} %get-tuple-element.31, bf16[528,256]{1,0:T(8,128)(2,1)S(1)} %collective-permute-done.p0), kind=kOutput, calls=%fused_computation.6 | convolution fusion | flops 268697600 | bytes 3407872 | tf_op jit(solution)/shard_map/dot_general | solution.py:299
  25.6 2.8 %collective-permute-done.2.p1 = bf16[528,256]{1,0:T(8,128)(2,1)S(1)} collective-permute-done((bf16[528,256]{1,0:T(8,128)(2,1)S(1)}, bf16[528,256]{1,0:T(8,128)(2,1)S(1)}, u32[]{:S(2)}, u32[]{:S(2)}) %collective-permute-start.2) | collective-permute-done | bytes 270368 | tf_op jit(solution)/shard_map/ppermute | solution.py:291
  28.5 0.0 collective-permute-start.3
  28.5 0.1 collective-permute-start.6
  28.6 0.4 convolution_add_fusion.3
  29.1 0.0 collective-permute-done.4.p2
  29.1 1.7 %collective-permute-start.5 = (bf16[528,256]{1,0:T(8,128)(2,1)S(1)}, bf16[528,256]{1,0:T(8,128)(2,1)S(1)}, u32[]{:S(2)}, u32[]{:S(2)}) collective-permute-start(bf16[528,256]{1,0:T(8,128)(2,1)S(1)} %collective-permute-done.4.p2), channel_id=1, source_target_pairs={{0,8},{8,0},{1,9},{9,1},{2,10},{10,2},{3,11},{11,3},{4,12},{12,4},... | collective-permute-start | bytes 811016 | tf_op jit(solution)/shard_map/ppermute | solution.py:297
  30.7 0.4 fusion.7
  31.2 5.0 %collective-permute-done.6.p3 = bf16[528,256]{1,0:T(8,128)(2,1)S(1)} collective-permute-done((bf16[528,256]{1,0:T(8,128)(2,1)S(1)}, bf16[528,256]{1,0:T(8,128)(2,1)S(1)}, u32[]{:S(2)}, u32[]{:S(2)}) %collective-permute-start.6) | collective-permute-done | bytes 270368 | tf_op jit(solution)/shard_map/ppermute | solution.py:293
  36.1 0.0 collective-permute-start.7
  36.1 0.0 collective-permute-done.3
  36.1 0.4 fusion.1
  36.6 0.4 fusion.4
  37.0 0.0 copy-start.3
  37.0 0.0 collective-permute-done.5
  37.1 0.4 fusion
  37.5 0.2 collective-permute-done.7
  37.7 0.4 fusion.2
  38.1 14.2 %all_to_all.10.refs_0_ = bf16[8,128,256]{2,1,0:T(8,128)(2,1)S(1)} all-to-all(bf16[8,128,256]{2,1,0:T(8,128)(2,1)S(1)} %bitcast.17), channel_id=1, replica_groups=mesh['zh'=4,'y'=4,'c'=2,'zl'=2,'x'=4] {'zl','x'}, dimensions={0} | all-to-all | bytes 1048576 | tf_op jit(solution)/shard_map/all_to_all | solution.py:302
  52.3 1.3 %middle.1 = (bf16[128,256]{1,0:T(8,128)(2,1)}, bf16[8,192,256]{2,1,0:T(8,128)(2,1)}) custom-call(bf16[8,128,256]{2,1,0:T(8,128)(2,1)S(1)} %all_to_all.10.refs_0_, bf16[128,256]{1,0:T(8,128)(2,1)S(1)} %get-tuple-element.38.refs_1_, bf16[128,256]{1,0:T(8,128)(2,1)S(1)} %get-tuple-element.39.refs_2_, f32[128,256]{1,0:T(8,128)S(1)} %get-tuple-element.40.refs_3_, ...), custom_call_target="tpu_custom_call" | custom-call | tf_op jit(solution)/shard_map/middle/pallas_call | solution.py:68
  53.6 5.2 %all-to-all-start.1 = ((bf16[8,192,256]{2,1,0:T(8,128)(2,1)}), bf16[8,192,256]{2,1,0:T(8,128)(2,1)S(1)}, u32[]{:S(2)}, u32[]{:S(2)}) async-start(bf16[8,192,256]{2,1,0:T(8,128)(2,1)} %get-tuple-element.42), calls=%async_computation.1 | async-start | bytes 1572864 | tf_op jit(solution)/shard_map/all_to_all | solution.py:310
  58.8 10.3 %all-to-all-done.1.both = bf16[8,192,256]{2,1,0:T(8,128)(2,1)S(1)} async-done(((bf16[8,192,256]{2,1,0:T(8,128)(2,1)}), bf16[8,192,256]{2,1,0:T(8,128)(2,1)S(1)}, u32[]{:S(2)}, u32[]{:S(2)}) %all-to-all-start.1) | async-done | bytes 786464 | tf_op jit(solution)/shard_map/all_to_all | solution.py:310
  69.1 3.7 %fusion.23.rows = f32[2048,256]{1,0:T(8,128)S(1)} fusion(bf16[1024,2048]{1,0:T(8,128)(2,1)} %get-tuple-element.33, bf16[1024,256]{1,0:T(8,128)(2,1)S(1)} %bitcast.18), kind=kOutput, calls=%fused_computation.28 | convolution fusion | flops 1073741824 | bytes 6815744 | tf_op jit(solution)/shard_map/dot_general | solution.py:315
  72.8 0.2 regroup_send.1
  73.0 0.3 collective-permute-start.8
  73.3 1.3 %fusion.22.rows = f32[2048,256]{1,0:T(8,128)S(1)} fusion(bf16[1024,2048]{1,0:T(8,128)(2,1)S(1)} %copy-done.8, bf16[1024,256]{1,0:T(8,128)(2,1)S(1)} %bitcast.19), kind=kOutput, calls=%fused_computation.27 | convolution fusion | flops 1073741824 | bytes 6815744 | tf_op jit(solution)/shard_map/dot_general | solution.py:315
  74.6 1.3 %collective-permute-done.8.others = bf16[2112,256]{1,0:T(8,128)(2,1)S(1)} collective-permute-done((bf16[2112,256]{1,0:T(8,128)(2,1)S(1)}, bf16[2112,256]{1,0:T(8,128)(2,1)S(1)}, u32[]{:S(2)}, u32[]{:S(2)}) %collective-permute-start.8) | collective-permute-done | bytes 1081376 | tf_op jit(solution)/shard_map/ppermute | solution.py:318
  76.0 0.3 regroup_keep.1
  76.2 0.1 collective-permute-start.10
  76.3 3.2 %collective-permute-start.9 = (bf16[576,256]{1,0:T(8,128)(2,1)S(1)}, bf16[576,256]{1,0:T(8,128)(2,1)S(1)}, u32[]{:S(2)}, u32[]{:S(2)}) collective-permute-start(bf16[576,256]{1,0:T(8,128)(2,1)S(1)} %get-tuple-element.44), channel_id=1, source_target_pairs={{0,48},{8,24},{16,0},{24,40},{32,16},{40,56},{48,32},{56,8},{1,49}... | collective-permute-start | bytes 884744 | tf_op jit(solution)/shard_map/ppermute | solution.py:327
  79.6 7.1 %collective-permute-done.10.came.first = bf16[576,256]{1,0:T(8,128)(2,1)S(1)} collective-permute-done((bf16[576,256]{1,0:T(8,128)(2,1)S(1)}, bf16[576,256]{1,0:T(8,128)(2,1)S(1)}, u32[]{:S(2)}, u32[]{:S(2)}) %collective-permute-start.10) | collective-permute-done | bytes 294944 | tf_op jit(solution)/shard_map/ppermute | solution.py:326
  86.7 0.1 collective-permute-start.11
  86.8 0.0 collective-permute-done.9.direct
  86.8 7.9 %collective-permute-done.11.relayed = bf16[576,256]{1,0:T(8,128)(2,1)S(1)} collective-permute-done((bf16[576,256]{1,0:T(8,128)(2,1)S(1)}, bf16[576,256]{1,0:T(8,128)(2,1)S(1)}, u32[]{:S(2)}, u32[]{:S(2)}) %collective-permute-start.11) | collective-permute-done | bytes 294944 | tf_op jit(solution)/shard_map/ppermute | solution.py:329
  94.7 0.1 spread.1
  94.8 7.8 %collective-permute-start.12 = (bf16[192,256]{1,0:T(8,128)(2,1)S(1)}, bf16[192,256]{1,0:T(8,128)(2,1)S(1)}, u32[]{:S(2)}, u32[]{:S(2)}) collective-permute-start(bf16[192,256]{1,0:T(8,128)(2,1)S(1)} %get-tuple-element.49), channel_id=1, source_target_pairs={{0,64},{64,0},{128,192},{192,128},{1,65},{65,1},{129,193},{193,129... | collective-permute-start | bytes 294920 | tf_op jit(solution)/shard_map/ppermute | solution.py:337
  102.6 5.1 %collective-permute-start.13 = (bf16[192,256]{1,0:T(8,128)(2,1)S(1)}, bf16[192,256]{1,0:T(8,128)(2,1)S(1)}, u32[]{:S(2)}, u32[]{:S(2)}) collective-permute-start(bf16[192,256]{1,0:T(8,128)(2,1)S(1)} %get-tuple-element.50), channel_id=1, source_target_pairs={{0,128},{64,192},{128,0},{192,64},{1,129},{65,193},{129,1},{193,65... | collective-permute-start | bytes 294920 | tf_op jit(solution)/shard_map/ppermute | solution.py:337
  107.7 0.5 collective-permute-start.14
  108.2 0.0 collective-permute-done.12.came1
  108.2 5.0 %collective-permute-done.13.came2 = bf16[192,256]{1,0:T(8,128)(2,1)S(1)} collective-permute-done((bf16[192,256]{1,0:T(8,128)(2,1)S(1)}, bf16[192,256]{1,0:T(8,128)(2,1)S(1)}, u32[]{:S(2)}, u32[]{:S(2)}) %collective-permute-start.13) | collective-permute-done | bytes 98336 | tf_op jit(solution)/shard_map/ppermute | solution.py:337
  113.2 2.0 %collective-permute-done.14.came3 = bf16[192,256]{1,0:T(8,128)(2,1)S(1)} collective-permute-done((bf16[192,256]{1,0:T(8,128)(2,1)S(1)}, bf16[192,256]{1,0:T(8,128)(2,1)S(1)}, u32[]{:S(2)}, u32[]{:S(2)}) %collective-permute-start.14) | collective-permute-done | bytes 98336 | tf_op jit(solution)/shard_map/ppermute | solution.py:337
  115.2 0.8 last.1
  115.9 1.7 %collective-permute-start.15 = (f32[64,256]{1,0:T(8,128)S(1)}, f32[64,256]{1,0:T(8,128)S(1)}, u32[]{:S(2)}, u32[]{:S(2)}) collective-permute-start(f32[64,256]{1,0:T(8,128)S(1)} %get-tuple-element.53.mine), channel_id=1, source_target_pairs={{0,4},{4,0},{1,5},{5,1},{2,6},{6,2},{3,7},{7,3},{8,12},{12,8},{9,1... | collective-permute-start | bytes 196616 | tf_op jit(solution)/shard_map/ppermute | solution.py:346
  117.6 1.0 collective-permute-start.16
  118.6 1.6 %collective-permute-done.15.over_z = f32[64,256]{1,0:T(8,128)S(1)} collective-permute-done((f32[64,256]{1,0:T(8,128)S(1)}, f32[64,256]{1,0:T(8,128)S(1)}, u32[]{:S(2)}, u32[]{:S(2)}) %collective-permute-start.15) | collective-permute-done | bytes 65568 | tf_op jit(solution)/shard_map/ppermute | solution.py:346
  120.2 0.6 collective-permute-start.17
  120.8 1.0 collective-permute-done.16.over_x
  121.8 2.6 %collective-permute-done.17.over_both = f32[64,256]{1,0:T(8,128)S(1)} collective-permute-done((f32[64,256]{1,0:T(8,128)S(1)}, f32[64,256]{1,0:T(8,128)S(1)}, u32[]{:S(2)}, u32[]{:S(2)}) %collective-permute-start.17) | collective-permute-done | bytes 65568 | tf_op jit(solution)/shard_map/ppermute | solution.py:348
  124.5 0.7 join.1
  (14 shorter events, 0.1 us)
Async XLA Ops:
  0.6 17.9 %copy-start.5 = (bf16[1024]{0:T(1024)(128)(2,1)S(1)}, bf16[1024]{0:T(1024)(128)(2,1)}, u32[]{:S(2)}) copy-start(bf16[1024]{0:T(1024)(128)(2,1)} %param.9) | copy-start | bytes 6148
  0.6 1.0 copy-start
  1.7 0.7 copy-start.4
  2.4 16.1 %copy-start.1 = (bf16[1024,256]{1,0:T(8,128)(2,1)S(1)}, bf16[1024,256]{1,0:T(8,128)(2,1)}, u32[]{:S(2)}) copy-start(bf16[1024,256]{1,0:T(8,128)(2,1)} %features.3) | copy-start | bytes 1572868
  2.4 16.1 %copy-start.2 = (bf16[1024,256]{1,0:T(8,128)(2,1)S(1)}, bf16[1024,256]{1,0:T(8,128)(2,1)}, u32[]{:S(2)}) copy-start(bf16[1024,256]{1,0:T(8,128)(2,1)} %cotangent.1) | copy-start | bytes 1572868
  3.0 13.3 %collective-permute-start = (bf16[528,256]{1,0:T(8,128)(2,1)S(1)}, bf16[528,256]{1,0:T(8,128)(2,1)S(1)}, u32[]{:S(2)}, u32[]{:S(2)}) collective-permute-start(bf16[528,256]{1,0:T(8,128)(2,1)S(1)} %piece.1), channel_id=1, source_target_pairs={{0,192},{1,200},{2,0},{3,8},{4,128},{5,136},{6,64},{7,72},{8,240},... | collective-permute-start | bytes 811016 | tf_op jit(solution)/shard_map/ppermute | solution.py:280
  16.3 5.9 %collective-permute-start.1 = (bf16[528,256]{1,0:T(8,128)(2,1)S(1)}, bf16[528,256]{1,0:T(8,128)(2,1)S(1)}, u32[]{:S(2)}, u32[]{:S(2)}) collective-permute-start(bf16[528,256]{1,0:T(8,128)(2,1)S(1)} %collective-permute-done.p0), channel_id=1, source_target_pairs={{0,8},{8,0},{1,9},{9,1},{2,10},{10,2},{3,11},{11,3},{4,12},{12,4},... | collective-permute-start | bytes 811016 | tf_op jit(solution)/shard_map/ppermute | solution.py:297
  18.5 10.1 %copy-start.7 = (bf16[1024,2048]{1,0:T(8,128)(2,1)S(1)}, bf16[1024,2048]{1,0:T(8,128)(2,1)}, u32[]{:S(2)}) copy-start(bf16[1024,2048]{1,0:T(8,128)(2,1)} %get-tuple-element.31) | copy-start | bytes 12582916
  18.8 9.6 %collective-permute-start.2 = (bf16[528,256]{1,0:T(8,128)(2,1)S(1)}, bf16[528,256]{1,0:T(8,128)(2,1)S(1)}, u32[]{:S(2)}, u32[]{:S(2)}) collective-permute-start(bf16[528,256]{1,0:T(8,128)(2,1)S(1)} %collective-permute-done.p0), channel_id=1, source_target_pairs={{0,16},{8,56},{16,32},{24,8},{32,48},{40,24},{48,0},{56,40},{1,17}... | collective-permute-start | bytes 811016 | tf_op jit(solution)/shard_map/ppermute | solution.py:291
  19.7 9.4 %collective-permute-start.4 = (bf16[528,256]{1,0:T(8,128)(2,1)S(1)}, bf16[528,256]{1,0:T(8,128)(2,1)S(1)}, u32[]{:S(2)}, u32[]{:S(2)}) collective-permute-start(bf16[528,256]{1,0:T(8,128)(2,1)S(1)} %collective-permute-done.p0), channel_id=1, source_target_pairs={{0,48},{8,24},{16,0},{24,40},{32,16},{40,56},{48,32},{56,8},{1,49}... | collective-permute-start | bytes 811016 | tf_op jit(solution)/shard_map/ppermute | solution.py:292
  23.8 12.3 %copy-start.6 = (bf16[1024,2048]{1,0:T(8,128)(2,1)S(1)}, bf16[1024,2048]{1,0:T(8,128)(2,1)}, u32[]{:S(2)}) copy-start(bf16[1024,2048]{1,0:T(8,128)(2,1)} %get-tuple-element.33) | copy-start | bytes 12582916
  28.5 7.7 %collective-permute-start.3 = (bf16[528,256]{1,0:T(8,128)(2,1)S(1)}, bf16[528,256]{1,0:T(8,128)(2,1)S(1)}, u32[]{:S(2)}, u32[]{:S(2)}) collective-permute-start(bf16[528,256]{1,0:T(8,128)(2,1)S(1)} %collective-permute-done.2.p1), channel_id=1, source_target_pairs={{0,8},{8,0},{1,9},{9,1},{2,10},{10,2},{3,11},{11,3},{4,12},{12,4},... | collective-permute-start | bytes 811016 | tf_op jit(solution)/shard_map/ppermute | solution.py:297
  28.5 7.7 %collective-permute-start.6 = (bf16[528,256]{1,0:T(8,128)(2,1)S(1)}, bf16[528,256]{1,0:T(8,128)(2,1)S(1)}, u32[]{:S(2)}, u32[]{:S(2)}) collective-permute-start(bf16[528,256]{1,0:T(8,128)(2,1)S(1)} %collective-permute-done.2.p1), channel_id=1, source_target_pairs={{0,16},{8,56},{16,32},{24,8},{32,48},{40,24},{48,0},{56,40},{1,17}... | collective-permute-start | bytes 811016 | tf_op jit(solution)/shard_map/ppermute | solution.py:293
  29.1 8.0 %collective-permute-start.5 = (bf16[528,256]{1,0:T(8,128)(2,1)S(1)}, bf16[528,256]{1,0:T(8,128)(2,1)S(1)}, u32[]{:S(2)}, u32[]{:S(2)}) collective-permute-start(bf16[528,256]{1,0:T(8,128)(2,1)S(1)} %collective-permute-done.4.p2), channel_id=1, source_target_pairs={{0,8},{8,0},{1,9},{9,1},{2,10},{10,2},{3,11},{11,3},{4,12},{12,4},... | collective-permute-start | bytes 811016 | tf_op jit(solution)/shard_map/ppermute | solution.py:297
  36.1 1.5 %collective-permute-start.7 = (bf16[528,256]{1,0:T(8,128)(2,1)S(1)}, bf16[528,256]{1,0:T(8,128)(2,1)S(1)}, u32[]{:S(2)}, u32[]{:S(2)}) collective-permute-start(bf16[528,256]{1,0:T(8,128)(2,1)S(1)} %collective-permute-done.6.p3), channel_id=1, source_target_pairs={{0,8},{8,0},{1,9},{9,1},{2,10},{10,2},{3,11},{11,3},{4,12},{12,4},... | collective-permute-start | bytes 811016 | tf_op jit(solution)/shard_map/ppermute | solution.py:297
  37.0 15.2 %copy-start.3 = (bf16[256,256]{1,0:T(8,128)(2,1)S(1)}, bf16[256,256]{1,0:T(8,128)(2,1)}, u32[]{:S(2)}) copy-start(bf16[256,256]{1,0:T(8,128)(2,1)} %refs_4_.1) | copy-start | bytes 393220
  53.6 15.5 %all-to-all-start.1 = ((bf16[8,192,256]{2,1,0:T(8,128)(2,1)}), bf16[8,192,256]{2,1,0:T(8,128)(2,1)S(1)}, u32[]{:S(2)}, u32[]{:S(2)}) async-start(bf16[8,192,256]{2,1,0:T(8,128)(2,1)} %get-tuple-element.42), calls=%async_computation.1 | async-start | bytes 1572864 | tf_op jit(solution)/shard_map/all_to_all | solution.py:310
  69.1 4.2 %copy-start.8 = (bf16[1024,2048]{1,0:T(8,128)(2,1)S(1)}, bf16[1024,2048]{1,0:T(8,128)(2,1)}, u32[]{:S(2)}) copy-start(bf16[1024,2048]{1,0:T(8,128)(2,1)} %get-tuple-element.31) | copy-start | bytes 12582916
  73.0 3.0 %collective-permute-start.8 = (bf16[2112,256]{1,0:T(8,128)(2,1)S(1)}, bf16[2112,256]{1,0:T(8,128)(2,1)S(1)}, u32[]{:S(2)}, u32[]{:S(2)}) collective-permute-start(bf16[2112,256]{1,0:T(8,128)(2,1)S(1)} %regroup_send.1), channel_id=1, source_target_pairs={{0,8},{8,0},{1,9},{9,1},{2,10},{10,2},{3,11},{11,3},{4,12},{12,4},... | collective-permute-start | bytes 3244040 | tf_op jit(solution)/shard_map/ppermute | solution.py:318
  76.2 10.4 %collective-permute-start.10 = (bf16[576,256]{1,0:T(8,128)(2,1)S(1)}, bf16[576,256]{1,0:T(8,128)(2,1)S(1)}, u32[]{:S(2)}, u32[]{:S(2)}) collective-permute-start(bf16[576,256]{1,0:T(8,128)(2,1)S(1)} %get-tuple-element.46), channel_id=1, source_target_pairs={{0,16},{8,56},{16,32},{24,8},{32,48},{40,24},{48,0},{56,40},{1,17}... | collective-permute-start | bytes 884744 | tf_op jit(solution)/shard_map/ppermute | solution.py:326
  76.3 10.5 %collective-permute-start.9 = (bf16[576,256]{1,0:T(8,128)(2,1)S(1)}, bf16[576,256]{1,0:T(8,128)(2,1)S(1)}, u32[]{:S(2)}, u32[]{:S(2)}) collective-permute-start(bf16[576,256]{1,0:T(8,128)(2,1)S(1)} %get-tuple-element.44), channel_id=1, source_target_pairs={{0,48},{8,24},{16,0},{24,40},{32,16},{40,56},{48,32},{56,8},{1,49}... | collective-permute-start | bytes 884744 | tf_op jit(solution)/shard_map/ppermute | solution.py:327
  86.7 8.0 %collective-permute-start.11 = (bf16[576,256]{1,0:T(8,128)(2,1)S(1)}, bf16[576,256]{1,0:T(8,128)(2,1)S(1)}, u32[]{:S(2)}, u32[]{:S(2)}) collective-permute-start(bf16[576,256]{1,0:T(8,128)(2,1)S(1)} %relay.1), channel_id=1, source_target_pairs={{0,16},{8,56},{16,32},{24,8},{32,48},{40,24},{48,0},{56,40},{1,17}... | collective-permute-start | bytes 884744 | tf_op jit(solution)/shard_map/ppermute | solution.py:329
  94.8 13.4 %collective-permute-start.12 = (bf16[192,256]{1,0:T(8,128)(2,1)S(1)}, bf16[192,256]{1,0:T(8,128)(2,1)S(1)}, u32[]{:S(2)}, u32[]{:S(2)}) collective-permute-start(bf16[192,256]{1,0:T(8,128)(2,1)S(1)} %get-tuple-element.49), channel_id=1, source_target_pairs={{0,64},{64,0},{128,192},{192,128},{1,65},{65,1},{129,193},{193,129... | collective-permute-start | bytes 294920 | tf_op jit(solution)/shard_map/ppermute | solution.py:337
  102.6 10.6 %collective-permute-start.13 = (bf16[192,256]{1,0:T(8,128)(2,1)S(1)}, bf16[192,256]{1,0:T(8,128)(2,1)S(1)}, u32[]{:S(2)}, u32[]{:S(2)}) collective-permute-start(bf16[192,256]{1,0:T(8,128)(2,1)S(1)} %get-tuple-element.50), channel_id=1, source_target_pairs={{0,128},{64,192},{128,0},{192,64},{1,129},{65,193},{129,1},{193,65... | collective-permute-start | bytes 294920 | tf_op jit(solution)/shard_map/ppermute | solution.py:337
  107.7 7.4 %collective-permute-start.14 = (bf16[192,256]{1,0:T(8,128)(2,1)S(1)}, bf16[192,256]{1,0:T(8,128)(2,1)S(1)}, u32[]{:S(2)}, u32[]{:S(2)}) collective-permute-start(bf16[192,256]{1,0:T(8,128)(2,1)S(1)} %get-tuple-element.51), channel_id=1, source_target_pairs={{0,192},{64,128},{128,64},{192,0},{1,193},{65,129},{129,65},{193,1... | collective-permute-start | bytes 294920 | tf_op jit(solution)/shard_map/ppermute | solution.py:337
  115.9 4.3 %collective-permute-start.15 = (f32[64,256]{1,0:T(8,128)S(1)}, f32[64,256]{1,0:T(8,128)S(1)}, u32[]{:S(2)}, u32[]{:S(2)}) collective-permute-start(f32[64,256]{1,0:T(8,128)S(1)} %get-tuple-element.53.mine), channel_id=1, source_target_pairs={{0,4},{4,0},{1,5},{5,1},{2,6},{6,2},{3,7},{7,3},{8,12},{12,8},{9,1... | collective-permute-start | bytes 196616 | tf_op jit(solution)/shard_map/ppermute | solution.py:346
  117.6 4.3 %collective-permute-start.16 = (f32[64,256]{1,0:T(8,128)S(1)}, f32[64,256]{1,0:T(8,128)S(1)}, u32[]{:S(2)}, u32[]{:S(2)}) collective-permute-start(f32[64,256]{1,0:T(8,128)S(1)} %get-tuple-element.53.mine), channel_id=1, source_target_pairs={{0,1},{1,0},{2,3},{3,2},{4,5},{5,4},{6,7},{7,6},{8,9},{9,8},{10,11... | collective-permute-start | bytes 196616 | tf_op jit(solution)/shard_map/ppermute | solution.py:347
  120.2 4.3 %collective-permute-start.17 = (f32[64,256]{1,0:T(8,128)S(1)}, f32[64,256]{1,0:T(8,128)S(1)}, u32[]{:S(2)}, u32[]{:S(2)}) collective-permute-start(f32[64,256]{1,0:T(8,128)S(1)} %collective-permute-done.15.over_z), channel_id=1, source_target_pairs={{0,1},{1,0},{2,3},{3,2},{4,5},{5,4},{6,7},{7,6},{8,9},{9,8},{10,11... | collective-permute-start | bytes 196616 | tf_op jit(solution)/shard_map/ppermute | solution.py:348

commit v6 on v5

--- a/solution.py
+++ b/solution.py
@@ -11,7 +11,9 @@
 ALL = ROWS + REP
 TILE = 128
 PIECE = 4 * TILE
+HALF = 2 * TILE
 WROWS = 64
+LIMIT = None
 BF16, F32 = jnp.bfloat16, jnp.float32
 SMEM = pl.BlockSpec(memory_space=pltpu.SMEM)
 WHOLE = pl.BlockSpec(memory_space=pltpu.VMEM)
@@ -41,17 +43,12 @@
     return pairs
 
 
-def ring_route(back):
-    pairs = []
-    for y in range(Y):
-        for c in range(C):
-            step = 1 if (c == 0) != back else -1
-            pairs.append((y * C + c, (y + step) % Y * C + c))
-    return pairs
-
-
-def order_of(apart, parity):
-    return jnp.where((apart & 1) == 0, 3 * (apart >> 1), 1 + (((3 - apart) >> 1) ^ parity))
+def ring_route(step):
+    return [(y, (y + step) % Y) for y in range(Y)]
+
+
+def order_of(apart):
+    return jnp.where((apart & 1) == 0, 3 * (apart >> 1), 1 + ((3 - apart) >> 1))
 
 
 def apart_of(q, odd, y):
@@ -64,14 +61,14 @@
     return jnp.concatenate([square, square], 1)
 
 
-def call(body, name, outs, scalars, arrays, specs=None, scratch=(), limit=16):
+def call(body, name, outs, scalars, arrays, specs=None, scratch=(), limit=16 << 20):
     return pl.pallas_call(
         body,
         out_shape=outs,
         in_specs=[SMEM] * len(scalars) + (specs or [WHOLE] * len(arrays)),
         out_specs=jax.tree.map(lambda _: WHOLE, outs),
         scratch_shapes=list(scratch),
-        compiler_params=pltpu.CompilerParams(vmem_limit_bytes=limit << 20),
+        compiler_params=pltpu.CompilerParams(vmem_limit_bytes=limit),
         name=name,
     )(*scalars, *arrays)
 
@@ -121,7 +118,7 @@
         at = col[0, k]
         q, sub = at >> 3, at & 7
         parity, pair = sub & 1, sub >> 1
-        place = (parity ^ core[0]) * 16 + order_of(apart_of(q, odd[0], y[0]), parity) * 4 + pair
+        place = (parity ^ core[0]) * 16 + order_of(apart_of(q, odd[0], y[0])) * 4 + pair
         rows = pl.ds(pl.multiple_of(row[0, k] * TILE, TILE), TILE)
         cols = pl.ds(pl.multiple_of(place * TILE, TILE), TILE)
         pltpu.make_async_copy(vals.at[0, k], dense.at[rows, cols], sems.at[k]).start()
@@ -181,10 +178,10 @@
 def regroup(ids, parity, rows, both, outs, others):
     y, odd, owner, q_own = ids
     for i, out in enumerate(outs):
-        pair = (y + (0, 3 - 2 * parity, 1 + 2 * parity, 2)[i]) & 3
+        pair = (y + (0, 3, 1, 2)[i]) & 3
 
         def load(q, at):
-            place = order_of(apart_of(q, odd, y), parity) * 4 + pair
+            place = order_of(apart_of(q, odd, y)) * 4 + pair
             part = rows[pl.ds(pl.multiple_of(place * TILE, TILE), TILE), :]
             if others is None:
                 return part
@@ -213,46 +210,52 @@
     out[4 * PIECE :, :] = slice_sum(both)
 
 
-def keep_body(core, y, odd, owner, q_own, rows, both, others, keep, straight, aside, relay, w_own):
-    outs = (keep, straight.at[:PIECE], aside, relay.at[:PIECE])
-    regroup((y[0], odd[0], owner[0], q_own[0]), core[0], rows, both, outs, others)
-    w_rows = (slice_sum(both).astype(F32) + others[4 * PIECE :, :].astype(F32)).astype(BF16)
-    straight[PIECE:, :] = w_rows
-    relay[PIECE:, :] = w_rows
-    w_own[...] = w_rows
-
-
-def relay_body(aside, came, out):
-    out[:PIECE, :] = (aside[...] + came[:PIECE, :].astype(F32)).astype(BF16)
-    out[PIECE:, :] = came[PIECE:, :]
-
-
-def spread_body(zh, keep, direct, relayed, first, w_own, own, out1, out2, out3, w_out):
-    w_rows = w_own[...].astype(F32) + first[PIECE:, :].astype(F32)
-    w_rows = (w_rows + (direct[PIECE:, :].astype(F32) + relayed[PIECE:, :].astype(F32))).astype(BF16)
-    w_out[...] = w_rows
+def keep_body(core, y, odd, owner, q_own, rows, both, others, keep, behind, ahead, up, down_, w_own, far):
+    regroup((y[0], odd[0], owner[0], q_own[0]), core[0], rows, both, (keep, behind, ahead, far), others)
+    for i, out in enumerate((up, down_)):
+        out[...] = far[i * HALF : (i + 1) * HALF, :]
+    w_own[...] = (slice_sum(both).astype(F32) + others[4 * PIECE :, :].astype(F32)).astype(BF16)
+
+
+def relay_body(behind, ahead, up, down_, mine, came1, came2, came3, up_out, down_out, w_out):
+    for i, (rows, came, out) in enumerate(((ahead, up, up_out), (behind, down_, down_out))):
+        for k in range(2):
+            part = slice(k * HALF, (k + 1) * HALF)
+            value = rows[part, :]
+            if k == i:
+                value += came[...].astype(F32)
+            out[part, :] = value.astype(BF16)
+    total = mine[...].astype(F32) + came1[...].astype(F32)
+    w_out[...] = total + (came2[...].astype(F32) + came3[...].astype(F32))
+
+
+def spread_body(zh, keep, up2, down2, own, out1, out2, out3):
     for m, out in enumerate((own, out1, out2, out3)):
         at = pl.ds(pl.multiple_of((zh[0] ^ m) * TILE, TILE), TILE)
-        chunk = keep[at, :] + direct[at, :].astype(F32) + relayed[at, :].astype(F32)
-        out[:TILE, :] = chunk.astype(out.dtype)
-        if m:
-            out[TILE:, :] = w_rows
-
-
-def last_body(core, y, odd, zh, own, came1, came2, came3, w_rows, p0, p1, p2, p3, grad, w_out):
-    order = order_of(apart_of(zh[0], odd[0], y[0]), core[0])
+        chunk = keep[at, :] + up2[at, :].astype(F32) + down2[at, :].astype(F32)
+        out[...] = chunk.astype(out.dtype)
+
+
+def pass_body(source, out):
+    out[...] = source[...]
+
+
+def add_body(mine, came1, came2, came3, after, out):
+    total = mine[...].astype(F32) + came1[...].astype(F32)
+    out[...] = total + (came2[...].astype(F32) + came3[...].astype(F32))
+
+
+def last_body(y, odd, zh, own, came1, came2, came3, p0, p1, p2, p3, grad):
+    order = order_of(apart_of(zh[0], odd[0], y[0]))
     below = jnp.zeros((16, TILE), F32)
     for i, piece in enumerate((p0, p1, p2, p3)):
-        below = jnp.where(order == i, piece[PIECE:, :TILE].astype(F32), below)
+        below = jnp.where(order == i, piece[piece.shape[0] - 16 :, :TILE].astype(F32), below)
     line = lax.broadcasted_iota(jnp.int32, (16, TILE), 0)
     row = jnp.sum(jnp.where(line == y[0], below, 0.0), 0, keepdims=True)
     total = own[...]
-    w_sum = w_rows[...].astype(F32)
     for came in (came1, came2, came3):
-        total += came[:TILE, :].astype(F32)
-        w_sum += came[TILE:, :].astype(F32)
+        total += came[...].astype(F32)
     grad[...] = (down(row) * total).astype(BF16)
-    w_out[...] = w_sum
 
 
 def join_body(zl, xl, mine, over_z, over_x, over_both, out):
@@ -275,30 +278,35 @@
 
     piece = call(
         piece_body, "piece", held(PIECE + 16), [(x + (y >> 1)) & 1], [degrees, features], [WHOLE, HBM],
-        [pltpu.VMEM((4, TILE, width), BF16), pltpu.SemaphoreType.DMA((4,))],
+        [pltpu.VMEM((4, TILE, width), BF16), pltpu.SemaphoreType.DMA((4,))], LIMIT,
     )
     piece = lax.ppermute(piece, ALL, piece_route())
     scaled, cot, deg = call(
         share_body, "share", (held(TILE), held(TILE), held(TILE, F32)), [replica.reshape(1)],
         [degrees, features, cotangent], [WHOLE, HBM, HBM],
-        [pltpu.VMEM((TILE, width), BF16), pltpu.SemaphoreType.DMA((2,))],
+        [pltpu.VMEM((TILE, width), BF16), pltpu.SemaphoreType.DMA((2,))], LIMIT,
     )
     own_a, other_a = assemble(tile_count, [core, y, odd], tile_row, tile_col, tile_vals, nodes_block, cols)
     piece, own_a, other_a = lax.optimization_barrier((piece, own_a, other_a))
 
     swap = [(0, 1), (1, 0)]
-    ahead, behind = ring_route(False), ring_route(True)
-    first = lax.ppermute(piece, ("y", "c"), ahead)
-    second = lax.ppermute(piece, ("y", "c"), behind)
-    third = lax.ppermute(first, ("y", "c"), ahead)
-    pieces = [piece, first, second, third]
-    partial = jnp.zeros((nodes_block, width), F32)
-    for i, own_x in enumerate(pieces):
+    ahead, behind = ring_route(1), ring_route(-1)
+    partial = jnp.dot(own_a[:, :PIECE], piece[:PIECE], preferred_element_type=F32)
+    first = lax.ppermute(piece, "y", ahead)
+    second = lax.ppermute(piece, "y", behind)
+    third = lax.ppermute(first[:HALF], "y", ahead)
+    fourth = lax.ppermute(second[HALF:], "y", behind)
+    pieces = [piece, first, second, fourth]
+    at = 0
+    for own_x in (piece, first, second, third, fourth):
         other_x = lax.ppermute(own_x, "c", swap)
-        at = slice(i * PIECE, (i + 1) * PIECE)
-        partial = partial + jnp.dot(own_a[:, at], own_x[:PIECE], preferred_element_type=F32)
-        partial = partial + jnp.dot(other_a[:, at], other_x[:PIECE], preferred_element_type=F32)
-    partial, scaled, cot, deg = lax.optimization_barrier((partial.astype(BF16), scaled, cot, deg))
+        size = own_x.shape[0] // TILE * TILE
+        if at:
+            partial = partial + jnp.dot(own_a[:, at : at + size], own_x[:size], preferred_element_type=F32)
+        partial = partial + jnp.dot(other_a[:, at : at + size], other_x[:size], preferred_element_type=F32)
+        at += size
+    partial = partial.astype(BF16)
+    partial, scaled, cot, deg = lax.optimization_barrier((partial, scaled, cot, deg))
     parts = lax.all_to_all(partial.reshape(ZL * X, TILE, width), REP, 0, 0)
     activated, both = call(
         lambda *refs: middle_body(float(nodes) ** -0.5, *refs),
@@ -316,36 +324,48 @@
 
     others = call(send_body, "regroup_send", held(cols + WROWS), ids, [pull(other_a), both])
     others = lax.ppermute(others, "c", swap)
-    keep, straight, aside, relay, w_own = call(
+    keep, behind_rows, ahead_rows, up, down_, w_own = call(
         keep_body,
         "regroup_keep",
-        (held(PIECE, F32), held(PIECE + WROWS), held(PIECE, F32), held(PIECE + WROWS), held(WROWS)),
+        (held(PIECE, F32), held(PIECE, F32), held(PIECE, F32), held(HALF), held(HALF), held(WROWS)),
         ids,
         [pull(own_a), both, others],
-    )
-    came = lax.ppermute(relay, ("y", "c"), ahead)
-    direct = lax.ppermute(straight, ("y", "c"), behind)
-    relayed = call(relay_body, "relay", held(PIECE + WROWS), [], [aside, came])
-    relayed = lax.ppermute(relayed, ("y", "c"), ahead)
-    own, *sent, w_rows = call(
+        scratch=[held(PIECE)],
+    )
+    up, down_ = lax.ppermute(up, "y", ahead), lax.ppermute(down_, "y", behind)
+    w_rows = call(pass_body, "slices", held(WROWS), [], [w_own])
+    w_y = [lax.ppermute(w_rows, "y", ring_route(m)) for m in range(1, 4)]
+    up2, down2, w_rows = call(
+        relay_body,
+        "relay",
+        (held(PIECE), held(PIECE), held(WROWS, F32)),
+        [],
+        [behind_rows, ahead_rows, up, down_, w_rows, *w_y],
+    )
+    up2, down2 = lax.ppermute(up2, "y", ahead), lax.ppermute(down2, "y", behind)
+    w_rows = call(pass_body, "slices_y", held(WROWS, F32), [], [w_rows])
+    exchange = [[(i, i ^ m) for i in range(ZH)] for m in range(1, 4)]
+    w_z = [lax.ppermute(w_rows, "zh", route) for route in exchange]
+    own, *sent = call(
         spread_body,
         "spread",
-        (held(TILE, F32), held(TILE + WROWS), held(TILE + WROWS), held(TILE + WROWS), held(WROWS)),
+        (held(TILE, F32), held(TILE), held(TILE), held(TILE)),
         [zh],
-        [keep, direct, relayed, came, w_own],
-    )
-    got = [lax.ppermute(sent[m - 1], "zh", [(i, i ^ m) for i in range(ZH)]) for m in range(1, 4)]
-    feature_grad, w_mine = call(
+        [keep, up2, down2],
+    )
+    w_mine = call(add_body, "slices_z", held(WROWS, F32), [], [w_rows, *w_z, sent[0]])
+    got = [lax.ppermute(part, "zh", route) for part, route in zip(sent, exchange)]
+    feature_grad = call(
         last_body,
         "last",
-        (jax.ShapeDtypeStruct((TILE, width), BF16), held(WROWS, F32)),
-        [core, y, odd, zh],
-        [own, *got, w_rows, *pieces],
+        jax.ShapeDtypeStruct((TILE, width), BF16),
+        [y, odd, zh],
+        [own, *got, *pieces],
     )
     flip = [(i, i ^ 1) for i in range(X)]
     over_z = lax.ppermute(w_mine, "zl", swap)
     over_x = lax.ppermute(w_mine, "x", flip)
-    over_both = lax.ppermute(over_z, "x", flip)
+    over_both = lax.ppermute(w_mine, REP, [(i, i ^ 5) for i in range(ZL * X)])
     weight_grad = call(
         join_body,
         "join",

time: 126 us -> 118 us (0.937)
  waiting for transfers between devices: 46.8 us -> 20.7 us
  starting transfers between devices: 38.7 us -> 54.3 us
  Pallas kernels: 11.7 us -> 15.4 us
  local copies, waits for them, and re-layouts: 1.78 us -> 0.07 us
    ppermute x10 -> x18, waiting for transfers between devices: 32.4 us -> 9.62 us  [the longest x3 3.09 us: shards(): w_y = [lax.ppermute(w_rows, 'y', ring_route(m)) for m in range(1, 4)]]
    ppermute x10 -> x18, starting transfers between devices: 20.9 us -> 37.8 us  [the longest x3 12.9 us: shards(): w_z = [lax.ppermute(w_rows, 'zh', route) for route in exchange]]
    pallas_call x9 -> x12, Pallas kernels: 4.25 us -> 6.63 us  [call(): pl.pallas_call(body, out_shape=outs, in_specs=[SMEM] * len(scalars) + (sp...]
    unnamed x18 -> x8, local copies, waits for them, and re-layouts: 1.75 us -> 0.02 us
    ppermute x1, waiting for transfers between devices: 1.6 us -> 0.01 us  [shards(): over_z = lax.ppermute(w_mine, 'zl', swap)]
    pallas_call x1, Pallas kernels: 7.5 us -> 8.82 us  [assemble(): pl.pallas_call(assemble_body, out_shape=(half, half), in_specs=[SMEM] * 6...]
    ppermute x4 -> x5, starting transfers between devices: 3.91 us -> 2.88 us  [shards(): other_x = lax.ppermute(own_x, 'c', swap)]
    dot_general x8 -> x10, matrix products: 6.07 us -> 6.28 us  [the longest x5 3.15 us: shards(): jnp.dot(other_a[:, at:at + size], other_x[:size], preferred_element_type=...]
  transfers between devices with their start and end apart: 19 -> 28, of which waited for: 12 -> 11; matrix products, arithmetic and copies ran while one was open for 6% -> 6% of each run, Pallas kernels for 6% -> 10%
where the time goes in v6:
time: 118 us; the launch traced here: 116 us
  starting transfers between devices  54.3 us (46%)
  waiting for transfers between devices  20.7 us (18%)
  Pallas kernels  15.4 us (13%)
  blocking collectives  13.3 us (11%)
  matrix products  11.3 us (10%)
    all_to_all x1, blocking collectives, shards(): parts = lax.all_to_all(partial.reshape(ZL * X, TILE, width), REP, 0, 0)  13.3 us
    ppermute x3, starting transfers between devices, shards(): w_z = [lax.ppermute(w_rows, 'zh', route) for route in exchange]  12.9 us
    all_to_all x1, waiting for transfers between devices, shards(): both = lax.all_to_all(both, REP, 0, 0)  9.74 us
    pallas_call x1, Pallas kernels, assemble(): pl.pallas_call(assemble_body, out_shape=(half, half), in_specs=[SMEM] * 6...  8.82 us
    pallas_call x12, Pallas kernels, call(): pl.pallas_call(body, out_shape=outs, in_specs=[SMEM] * len(scalars) + (sp...  6.63 us
    ppermute x3, starting transfers between devices, shards(): lax.ppermute(part, 'zh', route)  6.58 us
    ppermute x1, starting transfers between devices, shards(): piece = lax.ppermute(piece, ALL, piece_route())  5.79 us
    all_to_all x1, starting transfers between devices, shards(): both = lax.all_to_all(both, REP, 0, 0)  5.26 us
  transfers between devices with their start and end apart: 28, of which 11 were waited for; matrix products, arithmetic and copies ran while one was open for 6% of the time, Pallas kernels for 10%

profile of v6, /device:TPU:2, one launch (start us, length us, event | category | flops | bytes accessed | tf_op | source)
XLA Modules:
  0.0 116.1 jit_solution(11531897441770632990)
XLA Ops:
  0.6 1.7 %piece.1 = bf16[528,256]{1,0:T(8,128)(2,1)S(1)} custom-call(s32[1]{0:T(128)S(6)} %and.22.half, bf16[8,128]{1,0:T(8,128)(2,1)} %bitcast.20, bf16[1024,256]{1,0:T(8,128)(2,1)} %features.3), custom_call_target="tpu_custom_call" | custom-call | tf_op jit(solution)/shard_map/piece/pallas_call | solution.py:65
  2.3 5.8 %collective-permute-start = (bf16[528,256]{1,0:T(8,128)(2,1)S(1)}, bf16[528,256]{1,0:T(8,128)(2,1)S(1)}, u32[]{:S(2)}, u32[]{:S(2)}) collective-permute-start(bf16[528,256]{1,0:T(8,128)(2,1)S(1)} %piece.1), channel_id=1, source_target_pairs={{0,192},{1,200},{2,0},{3,8},{4,128},{5,136},{6,64},{7,72},{8,240},... | collective-permute-start | bytes 811016 | tf_op jit(solution)/shard_map/ppermute | solution.py:283
  8.1 8.8 %assemble.1 = (bf16[1024,2048]{1,0:T(8,128)(2,1)}, bf16[1024,2048]{1,0:T(8,128)(2,1)}) custom-call(s32[1,4]{1,0:T(1,128)} %count.1, s32[1]{0:T(128)} %bitcast.3.core, s32[1]{0:T(128)} %bitcast.1.y, s32[1]{0:T(128)S(6)} %and.23.odd.xl, s32[1,128]{1,0:T(1,128)} %row.1, s32[1,128]{1,0:T(1,128)} %col.1, bf16[1,128,128,128]{3,2,1,0:T(8,128)(2,1)} %vals.1), custom_call_target="tpu_custom_call" | custom-call | tf_op jit(solution)/shard_map/assemble/pallas_call | solution.py:144
  16.9 1.7 %collective-permute-start.2 = (bf16[528,256]{1,0:T(8,128)(2,1)S(1)}, bf16[528,256]{1,0:T(8,128)(2,1)S(1)}, u32[]{:S(2)}, u32[]{:S(2)}) collective-permute-start(bf16[528,256]{1,0:T(8,128)(2,1)S(1)} %collective-permute-done.p0), channel_id=1, source_target_pairs={{0,16},{16,32},{32,48},{48,0},{1,17},{17,33},{33,49},{49,1},{2,18}... | collective-permute-start | bytes 811016 | tf_op jit(solution)/shard_map/ppermute | solution.py:295
  18.6 2.0 %collective-permute-start.4 = (bf16[528,256]{1,0:T(8,128)(2,1)S(1)}, bf16[528,256]{1,0:T(8,128)(2,1)S(1)}, u32[]{:S(2)}, u32[]{:S(2)}) collective-permute-start(bf16[528,256]{1,0:T(8,128)(2,1)S(1)} %collective-permute-done.p0), channel_id=1, source_target_pairs={{0,48},{16,0},{32,16},{48,32},{1,49},{17,1},{33,17},{49,33},{2,50}... | collective-permute-start | bytes 811016 | tf_op jit(solution)/shard_map/ppermute | solution.py:296
  20.6 1.6 %collective-permute-start.1 = (bf16[528,256]{1,0:T(8,128)(2,1)S(1)}, bf16[528,256]{1,0:T(8,128)(2,1)S(1)}, u32[]{:S(2)}, u32[]{:S(2)}) collective-permute-start(bf16[528,256]{1,0:T(8,128)(2,1)S(1)} %collective-permute-done.p0), channel_id=1, source_target_pairs={{0,8},{8,0},{1,9},{9,1},{2,10},{10,2},{3,11},{11,3},{4,12},{12,4},... | collective-permute-start | bytes 811016 | tf_op jit(solution)/shard_map/ppermute | solution.py:302
  22.3 1.6 %share.1 = (bf16[128,256]{1,0:T(8,128)(2,1)S(1)}, bf16[128,256]{1,0:T(8,128)(2,1)S(1)}, f32[128,256]{1,0:T(8,128)S(1)}) custom-call(s32[1]{0:T(128)} %bitcast.4.replica, bf16[8,128]{1,0:T(8,128)(2,1)} %bitcast.21, bf16[1024,256]{1,0:T(8,128)(2,1)} %features.3, bf16[1024,256]{1,0:T(8,128)(2,1)} %cotangent.1), custom_call_target="tpu_custom_call" | custom-call | tf_op jit(solution)/shard_map/share/pallas_call | solution.py:65
  23.9 2.7 %collective-permute-done.2.p1 = bf16[528,256]{1,0:T(8,128)(2,1)S(1)} collective-permute-done((bf16[528,256]{1,0:T(8,128)(2,1)S(1)}, bf16[528,256]{1,0:T(8,128)(2,1)S(1)}, u32[]{:S(2)}, u32[]{:S(2)}) %collective-permute-start.2) | collective-permute-done | bytes 270368 | tf_op jit(solution)/shard_map/ppermute | solution.py:295
  26.6 1.2 %collective-permute-start.6 = (bf16[256,256]{1,0:T(8,128)(2,1)S(1)}, bf16[256,256]{1,0:T(8,128)(2,1)S(1)}, u32[]{:S(2)}, u32[]{:S(2)}) collective-permute-start(bf16[256,256]{1,0:T(8,128)(2,1)S(1)} %slice.89), channel_id=1, source_target_pairs={{0,16},{16,32},{32,48},{48,0},{1,17},{17,33},{33,49},{49,1},{2,18}... | collective-permute-start | bytes 393224 | tf_op jit(solution)/shard_map/ppermute | solution.py:297
  27.8 0.1 collective-permute-done.4.p2
  27.9 2.5 %collective-permute-start.8 = (bf16[272,256]{1,0:T(8,128)(2,1)S(1)}, bf16[272,256]{1,0:T(8,128)(2,1)S(1)}, u32[]{:S(2)}, u32[]{:S(2)}) collective-permute-start(bf16[272,256]{1,0:T(8,128)(2,1)S(1)} %slice.90), channel_id=1, source_target_pairs={{0,48},{16,0},{32,16},{48,32},{1,49},{17,1},{33,17},{49,33},{2,50}... | collective-permute-start | bytes 417800 | tf_op jit(solution)/shard_map/ppermute | solution.py:298
  30.4 0.0 collective-permute-done.1
  30.4 1.7 %fusion.9 = f32[1024,256]{1,0:T(8,128)S(1)} fusion(bf16[1024,2048]{1,0:T(8,128)(2,1)} %get-tuple-element.34, bf16[528,256]{1,0:T(8,128)(2,1)S(1)} %collective-permute-done.1), kind=kOutput, calls=%fused_computation.15 | convolution fusion | flops 268435456 | bytes 2359296 | tf_op jit(solution)/shard_map/dot_general | solution.py:306
  32.0 1.7 %convolution_add_fusion.5 = f32[1024,256]{1,0:T(8,128)S(1)} fusion(f32[1024,256]{1,0:T(8,128)S(1)} %fusion.9, bf16[1024,2048]{1,0:T(8,128)(2,1)} %get-tuple-element.32, bf16[528,256]{1,0:T(8,128)(2,1)S(1)} %collective-permute-done.p0), kind=kOutput, calls=%fused_computation.8 | convolution fusion | flops 268697600 | bytes 3407872 | tf_op jit(solution)/shard_map/dot_general | solution.py:294
  33.7 0.4 fusion.5
  34.2 0.5 collective-permute-start.3
  34.7 0.1 collective-permute-start.5
  34.8 0.4 convolution_add_fusion.4
  35.3 0.0 collective-permute-done.6
  35.3 0.3 fusion.16
  35.6 0.5 collective-permute-start.7
  36.1 0.1 collective-permute-start.9
  36.2 0.3 fusion.13
  36.5 0.4 fusion.2
  37.0 0.4 fusion.1
  37.4 0.0 copy-start
  37.4 0.3 fusion
  37.8 0.3 fusion.3
  38.1 13.3 %all_to_all.10.refs_0_ = bf16[8,128,256]{2,1,0:T(8,128)(2,1)S(1)} all-to-all(bf16[8,128,256]{2,1,0:T(8,128)(2,1)S(1)} %bitcast.17), channel_id=1, replica_groups=mesh['zh'=4,'y'=4,'c'=2,'zl'=2,'x'=4] {'zl','x'}, dimensions={0} | all-to-all | bytes 1048576 | tf_op jit(solution)/shard_map/all_to_all | solution.py:310
  51.4 1.3 %middle.1 = (bf16[128,256]{1,0:T(8,128)(2,1)}, bf16[8,192,256]{2,1,0:T(8,128)(2,1)}) custom-call(bf16[8,128,256]{2,1,0:T(8,128)(2,1)S(1)} %all_to_all.10.refs_0_, bf16[128,256]{1,0:T(8,128)(2,1)S(1)} %get-tuple-element.39.refs_1_, bf16[128,256]{1,0:T(8,128)(2,1)S(1)} %get-tuple-element.40.refs_2_, f32[128,256]{1,0:T(8,128)S(1)} %get-tuple-element.41.refs_3_, ...), custom_call_target="tpu_custom_call" | custom-call | tf_op jit(solution)/shard_map/middle/pallas_call | solution.py:65
  52.7 5.3 %all-to-all-start.1 = ((bf16[8,192,256]{2,1,0:T(8,128)(2,1)}), bf16[8,192,256]{2,1,0:T(8,128)(2,1)S(1)}, u32[]{:S(2)}, u32[]{:S(2)}) async-start(bf16[8,192,256]{2,1,0:T(8,128)(2,1)} %get-tuple-element.43), calls=%async_computation.1 | async-start | bytes 1572864 | tf_op jit(solution)/shard_map/all_to_all | solution.py:318
  58.0 9.7 %all-to-all-done.1.both = bf16[8,192,256]{2,1,0:T(8,128)(2,1)S(1)} async-done(((bf16[8,192,256]{2,1,0:T(8,128)(2,1)}), bf16[8,192,256]{2,1,0:T(8,128)(2,1)S(1)}, u32[]{:S(2)}, u32[]{:S(2)}) %all-to-all-start.1) | async-done | bytes 786464 | tf_op jit(solution)/shard_map/all_to_all | solution.py:318
  67.8 3.7 %fusion.27.rows = f32[2048,256]{1,0:T(8,128)S(1)} fusion(bf16[1024,2048]{1,0:T(8,128)(2,1)} %get-tuple-element.34, bf16[1024,256]{1,0:T(8,128)(2,1)S(1)} %bitcast.18), kind=kOutput, calls=%fused_computation.33 | convolution fusion | flops 1073741824 | bytes 6815744 | tf_op jit(solution)/shard_map/dot_general | solution.py:323
  71.5 0.2 regroup_send.1
  71.7 0.1 collective-permute-start.10
  71.8 1.3 %fusion.26.rows = f32[2048,256]{1,0:T(8,128)S(1)} fusion(bf16[1024,2048]{1,0:T(8,128)(2,1)S(1)} %copy-done.3, bf16[1024,256]{1,0:T(8,128)(2,1)S(1)} %bitcast.19), kind=kOutput, calls=%fused_computation.32 | convolution fusion | flops 1073741824 | bytes 6815744 | tf_op jit(solution)/shard_map/dot_general | solution.py:323
  73.1 1.3 %collective-permute-done.10.others = bf16[2112,256]{1,0:T(8,128)(2,1)S(1)} collective-permute-done((bf16[2112,256]{1,0:T(8,128)(2,1)S(1)}, bf16[2112,256]{1,0:T(8,128)(2,1)S(1)}, u32[]{:S(2)}, u32[]{:S(2)}) %collective-permute-start.10) | collective-permute-done | bytes 1081376 | tf_op jit(solution)/shard_map/ppermute | solution.py:326
  74.5 0.2 regroup_keep.1
  74.7 0.1 collective-permute-start.11
  74.8 3.2 %collective-permute-start.12 = (bf16[256,256]{1,0:T(8,128)(2,1)S(1)}, bf16[256,256]{1,0:T(8,128)(2,1)S(1)}, u32[]{:S(2)}, u32[]{:S(2)}) collective-permute-start(bf16[256,256]{1,0:T(8,128)(2,1)S(1)} %get-tuple-element.47), channel_id=1, source_target_pairs={{0,48},{16,0},{32,16},{48,32},{1,49},{17,1},{33,17},{49,33},{2,50}... | collective-permute-start | bytes 393224 | tf_op jit(solution)/shard_map/ppermute | solution.py:335
  78.0 2.1 %collective-permute-start.14 = (bf16[64,256]{1,0:T(8,128)(2,1)S(1)}, bf16[64,256]{1,0:T(8,128)(2,1)S(1)}, u32[]{:S(2)}, u32[]{:S(2)}) collective-permute-start(bf16[64,256]{1,0:T(8,128)(2,1)S(1)} %slices.1.mine), channel_id=1, source_target_pairs={{0,32},{16,48},{32,0},{48,16},{1,33},{17,49},{33,1},{49,17},{2,34}... | collective-permute-start | bytes 98312 | tf_op jit(solution)/shard_map/ppermute | solution.py:337
  80.1 1.2 %collective-permute-start.15 = (bf16[64,256]{1,0:T(8,128)(2,1)S(1)}, bf16[64,256]{1,0:T(8,128)(2,1)S(1)}, u32[]{:S(2)}, u32[]{:S(2)}) collective-permute-start(bf16[64,256]{1,0:T(8,128)(2,1)S(1)} %slices.1.mine), channel_id=1, source_target_pairs={{0,48},{16,0},{32,16},{48,32},{1,49},{17,1},{33,17},{49,33},{2,50}... | collective-permute-start | bytes 98312 | tf_op jit(solution)/shard_map/ppermute | solution.py:337
  81.3 1.9 %collective-permute-done.13.came1 = bf16[64,256]{1,0:T(8,128)(2,1)S(1)} collective-permute-done((bf16[64,256]{1,0:T(8,128)(2,1)S(1)}, bf16[64,256]{1,0:T(8,128)(2,1)S(1)}, u32[]{:S(2)}, u32[]{:S(2)}) %collective-permute-start.13) | collective-permute-done | bytes 32800 | tf_op jit(solution)/shard_map/ppermute | solution.py:337
  83.2 0.3 collective-permute-done.14.came2
  83.5 0.9 collective-permute-done.15.came3
  84.4 0.1 relay.1
  84.4 1.8 %collective-permute-start.19 = (bf16[512,256]{1,0:T(8,128)(2,1)S(1)}, bf16[512,256]{1,0:T(8,128)(2,1)S(1)}, u32[]{:S(2)}, u32[]{:S(2)}) collective-permute-start(bf16[512,256]{1,0:T(8,128)(2,1)S(1)} %get-tuple-element.51), channel_id=1, source_target_pairs={{0,16},{16,32},{32,48},{48,0},{1,17},{17,33},{33,49},{49,1},{2,18}... | collective-permute-start | bytes 786440 | tf_op jit(solution)/shard_map/ppermute | solution.py:345
  86.2 1.6 %collective-permute-start.20 = (bf16[512,256]{1,0:T(8,128)(2,1)S(1)}, bf16[512,256]{1,0:T(8,128)(2,1)S(1)}, u32[]{:S(2)}, u32[]{:S(2)}) collective-permute-start(bf16[512,256]{1,0:T(8,128)(2,1)S(1)} %get-tuple-element.52), channel_id=1, source_target_pairs={{0,48},{16,0},{32,16},{48,32},{1,49},{17,1},{33,17},{49,33},{2,50}... | collective-permute-start | bytes 786440 | tf_op jit(solution)/shard_map/ppermute | solution.py:345
  87.8 8.2 %collective-permute-start.16 = (f32[64,256]{1,0:T(8,128)S(1)}, f32[64,256]{1,0:T(8,128)S(1)}, u32[]{:S(2)}, u32[]{:S(2)}) collective-permute-start(f32[64,256]{1,0:T(8,128)S(1)} %slices_y.1.mine), channel_id=1, source_target_pairs={{0,64},{64,0},{128,192},{192,128},{1,65},{65,1},{129,193},{193,129... | collective-permute-start | bytes 196616 | tf_op jit(solution)/shard_map/ppermute | solution.py:348
  96.0 4.2 %collective-permute-start.17 = (f32[64,256]{1,0:T(8,128)S(1)}, f32[64,256]{1,0:T(8,128)S(1)}, u32[]{:S(2)}, u32[]{:S(2)}) collective-permute-start(f32[64,256]{1,0:T(8,128)S(1)} %slices_y.1.mine), channel_id=1, source_target_pairs={{0,128},{64,192},{128,0},{192,64},{1,129},{65,193},{129,1},{193,65... | collective-permute-start | bytes 196616 | tf_op jit(solution)/shard_map/ppermute | solution.py:348
  100.2 0.5 collective-permute-start.18
  100.7 0.1 spread.1
  100.7 2.5 %collective-permute-start.24 = (bf16[128,256]{1,0:T(8,128)(2,1)S(1)}, bf16[128,256]{1,0:T(8,128)(2,1)S(1)}, u32[]{:S(2)}, u32[]{:S(2)}) collective-permute-start(bf16[128,256]{1,0:T(8,128)(2,1)S(1)} %get-tuple-element.53.after), channel_id=1, source_target_pairs={{0,64},{64,0},{128,192},{192,128},{1,65},{65,1},{129,193},{193,129... | collective-permute-start | bytes 196616 | tf_op jit(solution)/shard_map/ppermute | solution.py:357
  103.2 3.7 %collective-permute-start.25 = (bf16[128,256]{1,0:T(8,128)(2,1)S(1)}, bf16[128,256]{1,0:T(8,128)(2,1)S(1)}, u32[]{:S(2)}, u32[]{:S(2)}) collective-permute-start(bf16[128,256]{1,0:T(8,128)(2,1)S(1)} %get-tuple-element.55), channel_id=1, source_target_pairs={{0,128},{64,192},{128,0},{192,64},{1,129},{65,193},{129,1},{193,65... | collective-permute-start | bytes 196616 | tf_op jit(solution)/shard_map/ppermute | solution.py:357
  106.9 0.5 collective-permute-start.26
  107.3 0.4 collective-permute-done.18.came3
  107.7 1.9 %collective-permute-start.21 = (f32[64,256]{1,0:T(8,128)S(1)}, f32[64,256]{1,0:T(8,128)S(1)}, u32[]{:S(2)}, u32[]{:S(2)}) collective-permute-start(f32[64,256]{1,0:T(8,128)S(1)} %slices_z.1.mine), channel_id=1, source_target_pairs={{0,4},{4,0},{1,5},{5,1},{2,6},{6,2},{3,7},{7,3},{8,12},{12,8},{9,1... | collective-permute-start | bytes 196616 | tf_op jit(solution)/shard_map/ppermute | solution.py:366
  109.6 0.6 collective-permute-start.22
  110.2 1.1 collective-permute-start.23
  111.3 1.6 %collective-permute-done.25.came2 = bf16[128,256]{1,0:T(8,128)(2,1)S(1)} collective-permute-done((bf16[128,256]{1,0:T(8,128)(2,1)S(1)}, bf16[128,256]{1,0:T(8,128)(2,1)S(1)}, u32[]{:S(2)}, u32[]{:S(2)}) %collective-permute-start.25) | collective-permute-done | bytes 65568 | tf_op jit(solution)/shard_map/ppermute | solution.py:357
  112.9 0.4 collective-permute-done.26.came3
  113.3 0.7 last.1
  114.1 1.3 %collective-permute-done.23.over_both = f32[64,256]{1,0:T(8,128)S(1)} collective-permute-done((f32[64,256]{1,0:T(8,128)S(1)}, f32[64,256]{1,0:T(8,128)S(1)}, u32[]{:S(2)}, u32[]{:S(2)}) %collective-permute-start.23) | collective-permute-done | bytes 65568 | tf_op jit(solution)/shard_map/ppermute | solution.py:368
  115.4 0.7 join.1
  (29 shorter events, 0.1 us)
Async XLA Ops:
  2.3 14.6 %collective-permute-start = (bf16[528,256]{1,0:T(8,128)(2,1)S(1)}, bf16[528,256]{1,0:T(8,128)(2,1)S(1)}, u32[]{:S(2)}, u32[]{:S(2)}) collective-permute-start(bf16[528,256]{1,0:T(8,128)(2,1)S(1)} %piece.1), channel_id=1, source_target_pairs={{0,192},{1,200},{2,0},{3,8},{4,128},{5,136},{6,64},{7,72},{8,240},... | collective-permute-start | bytes 811016 | tf_op jit(solution)/shard_map/ppermute | solution.py:283
  16.9 9.6 %collective-permute-start.2 = (bf16[528,256]{1,0:T(8,128)(2,1)S(1)}, bf16[528,256]{1,0:T(8,128)(2,1)S(1)}, u32[]{:S(2)}, u32[]{:S(2)}) collective-permute-start(bf16[528,256]{1,0:T(8,128)(2,1)S(1)} %collective-permute-done.p0), channel_id=1, source_target_pairs={{0,16},{16,32},{32,48},{48,0},{1,17},{17,33},{33,49},{49,1},{2,18}... | collective-permute-start | bytes 811016 | tf_op jit(solution)/shard_map/ppermute | solution.py:295
  18.6 9.3 %collective-permute-start.4 = (bf16[528,256]{1,0:T(8,128)(2,1)S(1)}, bf16[528,256]{1,0:T(8,128)(2,1)S(1)}, u32[]{:S(2)}, u32[]{:S(2)}) collective-permute-start(bf16[528,256]{1,0:T(8,128)(2,1)S(1)} %collective-permute-done.p0), channel_id=1, source_target_pairs={{0,48},{16,0},{32,16},{48,32},{1,49},{17,1},{33,17},{49,33},{2,50}... | collective-permute-start | bytes 811016 | tf_op jit(solution)/shard_map/ppermute | solution.py:296
  20.6 9.7 %collective-permute-start.1 = (bf16[528,256]{1,0:T(8,128)(2,1)S(1)}, bf16[528,256]{1,0:T(8,128)(2,1)S(1)}, u32[]{:S(2)}, u32[]{:S(2)}) collective-permute-start(bf16[528,256]{1,0:T(8,128)(2,1)S(1)} %collective-permute-done.p0), channel_id=1, source_target_pairs={{0,8},{8,0},{1,9},{9,1},{2,10},{10,2},{3,11},{11,3},{4,12},{12,4},... | collective-permute-start | bytes 811016 | tf_op jit(solution)/shard_map/ppermute | solution.py:302
  23.8 9.9 %copy-start.2 = (bf16[1024,2048]{1,0:T(8,128)(2,1)S(1)}, bf16[1024,2048]{1,0:T(8,128)(2,1)}, u32[]{:S(2)}) copy-start(bf16[1024,2048]{1,0:T(8,128)(2,1)} %get-tuple-element.32) | copy-start | bytes 12582916
  26.6 8.7 %collective-permute-start.6 = (bf16[256,256]{1,0:T(8,128)(2,1)S(1)}, bf16[256,256]{1,0:T(8,128)(2,1)S(1)}, u32[]{:S(2)}, u32[]{:S(2)}) collective-permute-start(bf16[256,256]{1,0:T(8,128)(2,1)S(1)} %slice.89), channel_id=1, source_target_pairs={{0,16},{16,32},{32,48},{48,0},{1,17},{17,33},{33,49},{49,1},{2,18}... | collective-permute-start | bytes 393224 | tf_op jit(solution)/shard_map/ppermute | solution.py:297
  27.9 8.2 %collective-permute-start.8 = (bf16[272,256]{1,0:T(8,128)(2,1)S(1)}, bf16[272,256]{1,0:T(8,128)(2,1)S(1)}, u32[]{:S(2)}, u32[]{:S(2)}) collective-permute-start(bf16[272,256]{1,0:T(8,128)(2,1)S(1)} %slice.90), channel_id=1, source_target_pairs={{0,48},{16,0},{32,16},{48,32},{1,49},{17,1},{33,17},{49,33},{2,50}... | collective-permute-start | bytes 417800 | tf_op jit(solution)/shard_map/ppermute | solution.py:298
  33.7 2.8 %copy-start.1 = (bf16[1024,2048]{1,0:T(8,128)(2,1)S(1)}, bf16[1024,2048]{1,0:T(8,128)(2,1)}, u32[]{:S(2)}) copy-start(bf16[1024,2048]{1,0:T(8,128)(2,1)} %get-tuple-element.34) | copy-start | bytes 12582916
  34.2 2.3 %collective-permute-start.3 = (bf16[528,256]{1,0:T(8,128)(2,1)S(1)}, bf16[528,256]{1,0:T(8,128)(2,1)S(1)}, u32[]{:S(2)}, u32[]{:S(2)}) collective-permute-start(bf16[528,256]{1,0:T(8,128)(2,1)S(1)} %collective-permute-done.2.p1), channel_id=1, source_target_pairs={{0,8},{8,0},{1,9},{9,1},{2,10},{10,2},{3,11},{11,3},{4,12},{12,4},... | collective-permute-start | bytes 811016 | tf_op jit(solution)/shard_map/ppermute | solution.py:302
  34.7 2.2 %collective-permute-start.5 = (bf16[528,256]{1,0:T(8,128)(2,1)S(1)}, bf16[528,256]{1,0:T(8,128)(2,1)S(1)}, u32[]{:S(2)}, u32[]{:S(2)}) collective-permute-start(bf16[528,256]{1,0:T(8,128)(2,1)S(1)} %collective-permute-done.4.p2), channel_id=1, source_target_pairs={{0,8},{8,0},{1,9},{9,1},{2,10},{10,2},{3,11},{11,3},{4,12},{12,4},... | collective-permute-start | bytes 811016 | tf_op jit(solution)/shard_map/ppermute | solution.py:302
  35.6 1.9 %collective-permute-start.7 = (bf16[256,256]{1,0:T(8,128)(2,1)S(1)}, bf16[256,256]{1,0:T(8,128)(2,1)S(1)}, u32[]{:S(2)}, u32[]{:S(2)}) collective-permute-start(bf16[256,256]{1,0:T(8,128)(2,1)S(1)} %collective-permute-done.6), channel_id=1, source_target_pairs={{0,8},{8,0},{1,9},{9,1},{2,10},{10,2},{3,11},{11,3},{4,12},{12,4},... | collective-permute-start | bytes 393224 | tf_op jit(solution)/shard_map/ppermute | solution.py:302
  36.1 1.7 %collective-permute-start.9 = (bf16[272,256]{1,0:T(8,128)(2,1)S(1)}, bf16[272,256]{1,0:T(8,128)(2,1)S(1)}, u32[]{:S(2)}, u32[]{:S(2)}) collective-permute-start(bf16[272,256]{1,0:T(8,128)(2,1)S(1)} %collective-permute-done.8.p3), channel_id=1, source_target_pairs={{0,8},{8,0},{1,9},{9,1},{2,10},{10,2},{3,11},{11,3},{4,12},{12,4},... | collective-permute-start | bytes 417800 | tf_op jit(solution)/shard_map/ppermute | solution.py:302
  37.4 14.0 %copy-start = (bf16[256,256]{1,0:T(8,128)(2,1)S(1)}, bf16[256,256]{1,0:T(8,128)(2,1)}, u32[]{:S(2)}) copy-start(bf16[256,256]{1,0:T(8,128)(2,1)} %refs_4_.1) | copy-start | bytes 393220
  52.7 15.0 %all-to-all-start.1 = ((bf16[8,192,256]{2,1,0:T(8,128)(2,1)}), bf16[8,192,256]{2,1,0:T(8,128)(2,1)S(1)}, u32[]{:S(2)}, u32[]{:S(2)}) async-start(bf16[8,192,256]{2,1,0:T(8,128)(2,1)} %get-tuple-element.43), calls=%async_computation.1 | async-start | bytes 1572864 | tf_op jit(solution)/shard_map/all_to_all | solution.py:318
  67.8 4.0 %copy-start.3 = (bf16[1024,2048]{1,0:T(8,128)(2,1)S(1)}, bf16[1024,2048]{1,0:T(8,128)(2,1)}, u32[]{:S(2)}) copy-start(bf16[1024,2048]{1,0:T(8,128)(2,1)} %get-tuple-element.32) | copy-start | bytes 12582916
  71.7 2.8 %collective-permute-start.10 = (bf16[2112,256]{1,0:T(8,128)(2,1)S(1)}, bf16[2112,256]{1,0:T(8,128)(2,1)S(1)}, u32[]{:S(2)}, u32[]{:S(2)}) collective-permute-start(bf16[2112,256]{1,0:T(8,128)(2,1)S(1)} %regroup_send.1), channel_id=1, source_target_pairs={{0,8},{8,0},{1,9},{9,1},{2,10},{10,2},{3,11},{11,3},{4,12},{12,4},... | collective-permute-start | bytes 3244040 | tf_op jit(solution)/shard_map/ppermute | solution.py:326
  74.7 9.7 %collective-permute-start.11 = (bf16[256,256]{1,0:T(8,128)(2,1)S(1)}, bf16[256,256]{1,0:T(8,128)(2,1)S(1)}, u32[]{:S(2)}, u32[]{:S(2)}) collective-permute-start(bf16[256,256]{1,0:T(8,128)(2,1)S(1)} %get-tuple-element.46), channel_id=1, source_target_pairs={{0,16},{16,32},{32,48},{48,0},{1,17},{17,33},{33,49},{49,1},{2,18}... | collective-permute-start | bytes 393224 | tf_op jit(solution)/shard_map/ppermute | solution.py:335
  74.8 9.6 %collective-permute-start.12 = (bf16[256,256]{1,0:T(8,128)(2,1)S(1)}, bf16[256,256]{1,0:T(8,128)(2,1)S(1)}, u32[]{:S(2)}, u32[]{:S(2)}) collective-permute-start(bf16[256,256]{1,0:T(8,128)(2,1)S(1)} %get-tuple-element.47), channel_id=1, source_target_pairs={{0,48},{16,0},{32,16},{48,32},{1,49},{17,1},{33,17},{49,33},{2,50}... | collective-permute-start | bytes 393224 | tf_op jit(solution)/shard_map/ppermute | solution.py:335
  78.0 5.1 %collective-permute-start.13 = (bf16[64,256]{1,0:T(8,128)(2,1)S(1)}, bf16[64,256]{1,0:T(8,128)(2,1)S(1)}, u32[]{:S(2)}, u32[]{:S(2)}) collective-permute-start(bf16[64,256]{1,0:T(8,128)(2,1)S(1)} %slices.1.mine), channel_id=1, source_target_pairs={{0,16},{16,32},{32,48},{48,0},{1,17},{17,33},{33,49},{49,1},{2,18}... | collective-permute-start | bytes 98312 | tf_op jit(solution)/shard_map/ppermute | solution.py:337
  78.0 5.5 %collective-permute-start.14 = (bf16[64,256]{1,0:T(8,128)(2,1)S(1)}, bf16[64,256]{1,0:T(8,128)(2,1)S(1)}, u32[]{:S(2)}, u32[]{:S(2)}) collective-permute-start(bf16[64,256]{1,0:T(8,128)(2,1)S(1)} %slices.1.mine), channel_id=1, source_target_pairs={{0,32},{16,48},{32,0},{48,16},{1,33},{17,49},{33,1},{49,17},{2,34}... | collective-permute-start | bytes 98312 | tf_op jit(solution)/shard_map/ppermute | solution.py:337
  80.1 4.3 %collective-permute-start.15 = (bf16[64,256]{1,0:T(8,128)(2,1)S(1)}, bf16[64,256]{1,0:T(8,128)(2,1)S(1)}, u32[]{:S(2)}, u32[]{:S(2)}) collective-permute-start(bf16[64,256]{1,0:T(8,128)(2,1)S(1)} %slices.1.mine), channel_id=1, source_target_pairs={{0,48},{16,0},{32,16},{48,32},{1,49},{17,1},{33,17},{49,33},{2,50}... | collective-permute-start | bytes 98312 | tf_op jit(solution)/shard_map/ppermute | solution.py:337
  84.4 16.2 %collective-permute-start.19 = (bf16[512,256]{1,0:T(8,128)(2,1)S(1)}, bf16[512,256]{1,0:T(8,128)(2,1)S(1)}, u32[]{:S(2)}, u32[]{:S(2)}) collective-permute-start(bf16[512,256]{1,0:T(8,128)(2,1)S(1)} %get-tuple-element.51), channel_id=1, source_target_pairs={{0,16},{16,32},{32,48},{48,0},{1,17},{17,33},{33,49},{49,1},{2,18}... | collective-permute-start | bytes 786440 | tf_op jit(solution)/shard_map/ppermute | solution.py:345
  86.2 14.5 %collective-permute-start.20 = (bf16[512,256]{1,0:T(8,128)(2,1)S(1)}, bf16[512,256]{1,0:T(8,128)(2,1)S(1)}, u32[]{:S(2)}, u32[]{:S(2)}) collective-permute-start(bf16[512,256]{1,0:T(8,128)(2,1)S(1)} %get-tuple-element.52), channel_id=1, source_target_pairs={{0,48},{16,0},{32,16},{48,32},{1,49},{17,1},{33,17},{49,33},{2,50}... | collective-permute-start | bytes 786440 | tf_op jit(solution)/shard_map/ppermute | solution.py:345
  87.8 19.1 %collective-permute-start.16 = (f32[64,256]{1,0:T(8,128)S(1)}, f32[64,256]{1,0:T(8,128)S(1)}, u32[]{:S(2)}, u32[]{:S(2)}) collective-permute-start(f32[64,256]{1,0:T(8,128)S(1)} %slices_y.1.mine), channel_id=1, source_target_pairs={{0,64},{64,0},{128,192},{192,128},{1,65},{65,1},{129,193},{193,129... | collective-permute-start | bytes 196616 | tf_op jit(solution)/shard_map/ppermute | solution.py:348
  96.0 11.3 %collective-permute-start.17 = (f32[64,256]{1,0:T(8,128)S(1)}, f32[64,256]{1,0:T(8,128)S(1)}, u32[]{:S(2)}, u32[]{:S(2)}) collective-permute-start(f32[64,256]{1,0:T(8,128)S(1)} %slices_y.1.mine), channel_id=1, source_target_pairs={{0,128},{64,192},{128,0},{192,64},{1,129},{65,193},{129,1},{193,65... | collective-permute-start | bytes 196616 | tf_op jit(solution)/shard_map/ppermute | solution.py:348
  100.2 7.5 %collective-permute-start.18 = (f32[64,256]{1,0:T(8,128)S(1)}, f32[64,256]{1,0:T(8,128)S(1)}, u32[]{:S(2)}, u32[]{:S(2)}) collective-permute-start(f32[64,256]{1,0:T(8,128)S(1)} %slices_y.1.mine), channel_id=1, source_target_pairs={{0,192},{64,128},{128,64},{192,0},{1,193},{65,129},{129,65},{193,1... | collective-permute-start | bytes 196616 | tf_op jit(solution)/shard_map/ppermute | solution.py:348
  100.7 9.5 %collective-permute-start.24 = (bf16[128,256]{1,0:T(8,128)(2,1)S(1)}, bf16[128,256]{1,0:T(8,128)(2,1)S(1)}, u32[]{:S(2)}, u32[]{:S(2)}) collective-permute-start(bf16[128,256]{1,0:T(8,128)(2,1)S(1)} %get-tuple-element.53.after), channel_id=1, source_target_pairs={{0,64},{64,0},{128,192},{192,128},{1,65},{65,1},{129,193},{193,129... | collective-permute-start | bytes 196616 | tf_op jit(solution)/shard_map/ppermute | solution.py:357
  103.2 9.7 %collective-permute-start.25 = (bf16[128,256]{1,0:T(8,128)(2,1)S(1)}, bf16[128,256]{1,0:T(8,128)(2,1)S(1)}, u32[]{:S(2)}, u32[]{:S(2)}) collective-permute-start(bf16[128,256]{1,0:T(8,128)(2,1)S(1)} %get-tuple-element.55), channel_id=1, source_target_pairs={{0,128},{64,192},{128,0},{192,64},{1,129},{65,193},{129,1},{193,65... | collective-permute-start | bytes 196616 | tf_op jit(solution)/shard_map/ppermute | solution.py:357
  106.9 6.5 %collective-permute-start.26 = (bf16[128,256]{1,0:T(8,128)(2,1)S(1)}, bf16[128,256]{1,0:T(8,128)(2,1)S(1)}, u32[]{:S(2)}, u32[]{:S(2)}) collective-permute-start(bf16[128,256]{1,0:T(8,128)(2,1)S(1)} %get-tuple-element.56), channel_id=1, source_target_pairs={{0,192},{64,128},{128,64},{192,0},{1,193},{65,129},{129,65},{193,1... | collective-permute-start | bytes 196616 | tf_op jit(solution)/shard_map/ppermute | solution.py:357
  107.7 6.4 %collective-permute-start.21 = (f32[64,256]{1,0:T(8,128)S(1)}, f32[64,256]{1,0:T(8,128)S(1)}, u32[]{:S(2)}, u32[]{:S(2)}) collective-permute-start(f32[64,256]{1,0:T(8,128)S(1)} %slices_z.1.mine), channel_id=1, source_target_pairs={{0,4},{4,0},{1,5},{5,1},{2,6},{6,2},{3,7},{7,3},{8,12},{12,8},{9,1... | collective-permute-start | bytes 196616 | tf_op jit(solution)/shard_map/ppermute | solution.py:366
  109.6 4.5 %collective-permute-start.22 = (f32[64,256]{1,0:T(8,128)S(1)}, f32[64,256]{1,0:T(8,128)S(1)}, u32[]{:S(2)}, u32[]{:S(2)}) collective-permute-start(f32[64,256]{1,0:T(8,128)S(1)} %slices_z.1.mine), channel_id=1, source_target_pairs={{0,1},{1,0},{2,3},{3,2},{4,5},{5,4},{6,7},{7,6},{8,9},{9,8},{10,11... | collective-permute-start | bytes 196616 | tf_op jit(solution)/shard_map/ppermute | solution.py:367
  110.2 5.2 %collective-permute-start.23 = (f32[64,256]{1,0:T(8,128)S(1)}, f32[64,256]{1,0:T(8,128)S(1)}, u32[]{:S(2)}, u32[]{:S(2)}) collective-permute-start(f32[64,256]{1,0:T(8,128)S(1)} %slices_z.1.mine), channel_id=1, source_target_pairs={{0,5},{1,4},{2,7},{3,6},{4,1},{5,0},{6,3},{7,2},{8,13},{9,12},{10,... | collective-permute-start | bytes 196616 | tf_op jit(solution)/shard_map/ppermute | solution.py:368

commit v7 on v6

--- a/solution.py
+++ b/solution.py
@@ -306,7 +306,10 @@
         partial = partial + jnp.dot(other_a[:, at : at + size], other_x[:size], preferred_element_type=F32)
         at += size
     partial = partial.astype(BF16)
-    partial, scaled, cot, deg = lax.optimization_barrier((partial, scaled, cot, deg))
+    owner, q_own = (replica == block // 4).astype(jnp.int32).reshape(1), (block % 4).reshape(1)
+    partial, scaled, cot, deg, owner, q_own = lax.optimization_barrier(
+        (partial, scaled, cot, deg, owner, q_own)
+    )
     parts = lax.all_to_all(partial.reshape(ZL * X, TILE, width), REP, 0, 0)
     activated, both = call(
         lambda *refs: middle_body(float(nodes) ** -0.5, *refs),
@@ -317,7 +320,7 @@
     )
     both = lax.all_to_all(both, REP, 0, 0)
     back_block = both[:, :TILE].reshape(nodes_block, width)
-    ids = [core, y, odd, (replica == block // 4).astype(jnp.int32).reshape(1), (block % 4).reshape(1)]
+    ids = [core, y, odd, owner, q_own]
 
     def pull(a):
         return lax.dot_general(a, back_block, (((0,), (0,)), ((), ())), preferred_element_type=F32)

time: 118 us -> 115 us (0.975); the launches traced: 116 us -> 115 us
  blocking collectives: 13.3 us -> 28.2 us
  waiting for transfers between devices: 20.7 us -> 13 us
  starting transfers between devices: 54.3 us -> 49.4 us
  matrix products: 11.3 us -> 9.13 us
  Pallas kernels: 15.4 us -> 14.1 us
    all_to_all x0 -> x1, blocking collectives: none -> 15 us  [shards(): both = lax.all_to_all(both, REP, 0, 0)]
    all_to_all x1 -> x0, waiting for transfers between devices: 9.74 us -> none  [shards(): both = lax.all_to_all(both, REP, 0, 0)]
    all_to_all x1 -> x0, starting transfers between devices: 5.26 us -> none  [shards(): both = lax.all_to_all(both, REP, 0, 0)]
    dot_general x2, matrix products: 5.03 us -> 2.7 us  [pull(): lax.dot_general(a, back_block, (((0,), (0,)), ((), ())), preferred_elemen...]
    ppermute x1, starting transfers between devices: 0.59 us -> 2.14 us  [shards(): over_x = lax.ppermute(w_mine, 'x', flip)]
    ppermute x1, waiting for transfers between devices: 1.3 us -> 2.7 us  [shards(): over_both = lax.ppermute(w_mine, REP, [(i, i ^ 5) for i in range(ZL * X)])]
  transfers between devices with their start and end apart: 28 -> 27, of which waited for: 11 -> 9; matrix products, arithmetic and copies ran while one was open for 6% -> 7% of each run, Pallas kernels for 10% -> 9%
where the time goes in v7:
time: 115 us
  starting transfers between devices  49.4 us (43%)
  blocking collectives  28.2 us (25%)
  Pallas kernels  14.1 us (12%)
  waiting for transfers between devices  13 us (11%)
  matrix products  9.13 us (8%)
    all_to_all x1, blocking collectives, shards(): both = lax.all_to_all(both, REP, 0, 0)  15 us
    all_to_all x1, blocking collectives, shards(): parts = lax.all_to_all(partial.reshape(ZL * X, TILE, width), REP, 0, 0)  13.3 us
    ppermute x3, starting transfers between devices, shards(): w_z = [lax.ppermute(w_rows, 'zh', route) for route in exchange]  12.8 us
    pallas_call x1, Pallas kernels, assemble(): pl.pallas_call(assemble_body, out_shape=(half, half), in_specs=[SMEM] * 6...  7.99 us
    ppermute x3, starting transfers between devices, shards(): lax.ppermute(part, 'zh', route)  6.58 us
    pallas_call x12, Pallas kernels, call(): pl.pallas_call(body, out_shape=outs, in_specs=[SMEM] * len(scalars) + (sp...  6.15 us
    ppermute x1, starting transfers between devices, shards(): piece = lax.ppermute(piece, ALL, piece_route())  5.79 us
    ppermute x1, waiting for transfers between devices, shards(): first = lax.ppermute(piece, 'y', ahead)  3.68 us
  transfers between devices with their start and end apart: 27, of which 9 were waited for; matrix products, arithmetic and copies ran while one was open for 7% of the time, Pallas kernels for 9%

profile of v7, /device:TPU:2, one launch (start us, length us, event | category | flops | bytes accessed | tf_op | source)
XLA Modules:
  0.0 114.9 jit_solution(15588228314504127484)
XLA Ops:
  0.6 1.7 %piece.1 = bf16[528,256]{1,0:T(8,128)(2,1)S(1)} custom-call(s32[1]{0:T(128)S(6)} %and.22.half, bf16[8,128]{1,0:T(8,128)(2,1)} %bitcast.20, bf16[1024,256]{1,0:T(8,128)(2,1)} %features.3), custom_call_target="tpu_custom_call" | custom-call | tf_op jit(solution)/shard_map/piece/pallas_call | solution.py:65
  2.3 5.8 %collective-permute-start = (bf16[528,256]{1,0:T(8,128)(2,1)S(1)}, bf16[528,256]{1,0:T(8,128)(2,1)S(1)}, u32[]{:S(2)}, u32[]{:S(2)}) collective-permute-start(bf16[528,256]{1,0:T(8,128)(2,1)S(1)} %piece.1), channel_id=1, source_target_pairs={{0,192},{1,200},{2,0},{3,8},{4,128},{5,136},{6,64},{7,72},{8,240},... | collective-permute-start | bytes 811016 | tf_op jit(solution)/shard_map/ppermute | solution.py:283
  8.1 8.0 %assemble.1 = (bf16[1024,2048]{1,0:T(8,128)(2,1)}, bf16[1024,2048]{1,0:T(8,128)(2,1)}) custom-call(s32[1,4]{1,0:T(1,128)} %count.1, s32[1]{0:T(128)} %bitcast.3.core, s32[1]{0:T(128)} %bitcast.1.y, s32[1]{0:T(128)S(6)} %and.23.odd.xl, s32[1,128]{1,0:T(1,128)} %row.1, s32[1,128]{1,0:T(1,128)} %col.1, bf16[1,128,128,128]{3,2,1,0:T(8,128)(2,1)} %vals.1), custom_call_target="tpu_custom_call" | custom-call | tf_op jit(solution)/shard_map/assemble/pallas_call | solution.py:144
  16.1 0.0 collective-permute-done.p0
  16.1 1.9 %collective-permute-start.2 = (bf16[528,256]{1,0:T(8,128)(2,1)S(1)}, bf16[528,256]{1,0:T(8,128)(2,1)S(1)}, u32[]{:S(2)}, u32[]{:S(2)}) collective-permute-start(bf16[528,256]{1,0:T(8,128)(2,1)S(1)} %collective-permute-done.p0), channel_id=1, source_target_pairs={{0,16},{16,32},{32,48},{48,0},{1,17},{17,33},{33,49},{49,1},{2,18}... | collective-permute-start | bytes 811016 | tf_op jit(solution)/shard_map/ppermute | solution.py:295
  18.0 2.3 %collective-permute-start.4 = (bf16[528,256]{1,0:T(8,128)(2,1)S(1)}, bf16[528,256]{1,0:T(8,128)(2,1)S(1)}, u32[]{:S(2)}, u32[]{:S(2)}) collective-permute-start(bf16[528,256]{1,0:T(8,128)(2,1)S(1)} %collective-permute-done.p0), channel_id=1, source_target_pairs={{0,48},{16,0},{32,16},{48,32},{1,49},{17,1},{33,17},{49,33},{2,50}... | collective-permute-start | bytes 811016 | tf_op jit(solution)/shard_map/ppermute | solution.py:296
  20.3 1.2 %collective-permute-start.1 = (bf16[528,256]{1,0:T(8,128)(2,1)S(1)}, bf16[528,256]{1,0:T(8,128)(2,1)S(1)}, u32[]{:S(2)}, u32[]{:S(2)}) collective-permute-start(bf16[528,256]{1,0:T(8,128)(2,1)S(1)} %collective-permute-done.p0), channel_id=1, source_target_pairs={{0,8},{8,0},{1,9},{9,1},{2,10},{10,2},{3,11},{11,3},{4,12},{12,4},... | collective-permute-start | bytes 811016 | tf_op jit(solution)/shard_map/ppermute | solution.py:302
  21.5 1.6 %share.1 = (bf16[128,256]{1,0:T(8,128)(2,1)S(1)}, bf16[128,256]{1,0:T(8,128)(2,1)S(1)}, f32[128,256]{1,0:T(8,128)S(1)}) custom-call(s32[1]{0:T(128)} %bitcast.4.replica, bf16[8,128]{1,0:T(8,128)(2,1)} %bitcast.21, bf16[1024,256]{1,0:T(8,128)(2,1)} %features.3, bf16[1024,256]{1,0:T(8,128)(2,1)} %cotangent.1), custom_call_target="tpu_custom_call" | custom-call | tf_op jit(solution)/shard_map/share/pallas_call | solution.py:65
  23.1 3.7 %collective-permute-done.2.p1 = bf16[528,256]{1,0:T(8,128)(2,1)S(1)} collective-permute-done((bf16[528,256]{1,0:T(8,128)(2,1)S(1)}, bf16[528,256]{1,0:T(8,128)(2,1)S(1)}, u32[]{:S(2)}, u32[]{:S(2)}) %collective-permute-start.2) | collective-permute-done | bytes 270368 | tf_op jit(solution)/shard_map/ppermute | solution.py:295
  26.8 0.6 collective-permute-start.6
  27.3 0.0 collective-permute-done.4.p2
  27.3 3.2 %collective-permute-start.8 = (bf16[272,256]{1,0:T(8,128)(2,1)S(1)}, bf16[272,256]{1,0:T(8,128)(2,1)S(1)}, u32[]{:S(2)}, u32[]{:S(2)}) collective-permute-start(bf16[272,256]{1,0:T(8,128)(2,1)S(1)} %slice.90), channel_id=1, source_target_pairs={{0,48},{16,0},{32,16},{48,32},{1,49},{17,1},{33,17},{49,33},{2,50}... | collective-permute-start | bytes 417800 | tf_op jit(solution)/shard_map/ppermute | solution.py:298
  30.6 1.7 %fusion.9 = f32[1024,256]{1,0:T(8,128)S(1)} fusion(bf16[1024,2048]{1,0:T(8,128)(2,1)} %get-tuple-element.36, bf16[528,256]{1,0:T(8,128)(2,1)S(1)} %collective-permute-done.1), kind=kOutput, calls=%fused_computation.15 | convolution fusion | flops 268435456 | bytes 2359296 | tf_op jit(solution)/shard_map/dot_general | solution.py:306
  32.2 1.7 %convolution_add_fusion.5 = f32[1024,256]{1,0:T(8,128)S(1)} fusion(f32[1024,256]{1,0:T(8,128)S(1)} %fusion.9, bf16[1024,2048]{1,0:T(8,128)(2,1)} %get-tuple-element.34, bf16[528,256]{1,0:T(8,128)(2,1)S(1)} %collective-permute-done.p0), kind=kOutput, calls=%fused_computation.8 | convolution fusion | flops 268697600 | bytes 3407872 | tf_op jit(solution)/shard_map/dot_general | solution.py:294
  33.9 0.4 fusion.5
  34.4 0.1 collective-permute-start.3
  34.5 0.5 collective-permute-start.5
  35.0 0.4 convolution_add_fusion.4
  35.4 0.3 fusion.16
  35.8 0.2 collective-permute-start.7
  35.9 0.4 collective-permute-start.9
  36.4 0.3 fusion.13
  36.7 0.5 fusion.2
  37.1 0.0 collective-permute-done.5
  37.2 0.5 fusion.1
  37.6 0.0 copy-start
  37.6 0.0 collective-permute-done.7
  37.7 0.4 fusion
  38.0 0.0 collective-permute-done.9
  38.1 0.3 fusion.3
  38.4 13.3 %all_to_all.10.refs_0_ = bf16[8,128,256]{2,1,0:T(8,128)(2,1)S(1)} all-to-all(bf16[8,128,256]{2,1,0:T(8,128)(2,1)S(1)} %bitcast.17), channel_id=1, replica_groups=mesh['zh'=4,'y'=4,'c'=2,'zl'=2,'x'=4] {'zl','x'}, dimensions={0} | all-to-all | bytes 1048576 | tf_op jit(solution)/shard_map/all_to_all | solution.py:313
  51.6 0.8 middle.1
  52.5 15.0 %all_to_all.11.both = bf16[8,192,256]{2,1,0:T(8,128)(2,1)S(1)} all-to-all(bf16[8,192,256]{2,1,0:T(8,128)(2,1)S(1)} %get-tuple-element.47), channel_id=1, replica_groups=mesh['zh'=4,'y'=4,'c'=2,'zl'=2,'x'=4] {'zl','x'}, dimensions={0} | all-to-all | bytes 1572864 | tf_op jit(solution)/shard_map/all_to_all | solution.py:321
  67.5 1.4 %fusion.27.rows = f32[2048,256]{1,0:T(8,128)S(1)} fusion(bf16[1024,2048]{1,0:T(8,128)(2,1)S(1)} %copy-done.1, bf16[1024,256]{1,0:T(8,128)(2,1)S(1)} %bitcast.18), kind=kOutput, calls=%fused_computation.33 | convolution fusion | flops 1073741824 | bytes 6815744 | tf_op jit(solution)/shard_map/dot_general | solution.py:326
  68.9 0.2 regroup_send.1
  69.0 0.1 collective-permute-start.10
  69.1 1.3 %fusion.26.rows = f32[2048,256]{1,0:T(8,128)S(1)} fusion(bf16[1024,2048]{1,0:T(8,128)(2,1)S(1)} %copy-done.2, bf16[1024,256]{1,0:T(8,128)(2,1)S(1)} %bitcast.19), kind=kOutput, calls=%fused_computation.32 | convolution fusion | flops 1073741824 | bytes 6815744 | tf_op jit(solution)/shard_map/dot_general | solution.py:326
  70.5 1.3 %collective-permute-done.10.others = bf16[2112,256]{1,0:T(8,128)(2,1)S(1)} collective-permute-done((bf16[2112,256]{1,0:T(8,128)(2,1)S(1)}, bf16[2112,256]{1,0:T(8,128)(2,1)S(1)}, u32[]{:S(2)}, u32[]{:S(2)}) %collective-permute-start.10) | collective-permute-done | bytes 1081376 | tf_op jit(solution)/shard_map/ppermute | solution.py:329
  71.8 0.2 regroup_keep.1
  72.1 0.1 collective-permute-start.11
  72.2 3.2 %collective-permute-start.12 = (bf16[256,256]{1,0:T(8,128)(2,1)S(1)}, bf16[256,256]{1,0:T(8,128)(2,1)S(1)}, u32[]{:S(2)}, u32[]{:S(2)}) collective-permute-start(bf16[256,256]{1,0:T(8,128)(2,1)S(1)} %get-tuple-element.51), channel_id=1, source_target_pairs={{0,48},{16,0},{32,16},{48,32},{1,49},{17,1},{33,17},{49,33},{2,50}... | collective-permute-start | bytes 393224 | tf_op jit(solution)/shard_map/ppermute | solution.py:338
  75.4 2.3 %collective-permute-start.14 = (bf16[64,256]{1,0:T(8,128)(2,1)S(1)}, bf16[64,256]{1,0:T(8,128)(2,1)S(1)}, u32[]{:S(2)}, u32[]{:S(2)}) collective-permute-start(bf16[64,256]{1,0:T(8,128)(2,1)S(1)} %slices.1.mine), channel_id=1, source_target_pairs={{0,32},{16,48},{32,0},{48,16},{1,33},{17,49},{33,1},{49,17},{2,34}... | collective-permute-start | bytes 98312 | tf_op jit(solution)/shard_map/ppermute | solution.py:340
  77.7 0.9 collective-permute-start.15
  78.6 1.9 %collective-permute-done.13.came1 = bf16[64,256]{1,0:T(8,128)(2,1)S(1)} collective-permute-done((bf16[64,256]{1,0:T(8,128)(2,1)S(1)}, bf16[64,256]{1,0:T(8,128)(2,1)S(1)}, u32[]{:S(2)}, u32[]{:S(2)}) %collective-permute-start.13) | collective-permute-done | bytes 32800 | tf_op jit(solution)/shard_map/ppermute | solution.py:340
  80.5 0.3 collective-permute-done.14.came2
  80.9 0.9 collective-permute-done.15.came3
  81.7 0.1 relay.1
  81.8 1.8 %collective-permute-start.19 = (bf16[512,256]{1,0:T(8,128)(2,1)S(1)}, bf16[512,256]{1,0:T(8,128)(2,1)S(1)}, u32[]{:S(2)}, u32[]{:S(2)}) collective-permute-start(bf16[512,256]{1,0:T(8,128)(2,1)S(1)} %get-tuple-element.55), channel_id=1, source_target_pairs={{0,16},{16,32},{32,48},{48,0},{1,17},{17,33},{33,49},{49,1},{2,18}... | collective-permute-start | bytes 786440 | tf_op jit(solution)/shard_map/ppermute | solution.py:348
  83.6 1.6 %collective-permute-start.20 = (bf16[512,256]{1,0:T(8,128)(2,1)S(1)}, bf16[512,256]{1,0:T(8,128)(2,1)S(1)}, u32[]{:S(2)}, u32[]{:S(2)}) collective-permute-start(bf16[512,256]{1,0:T(8,128)(2,1)S(1)} %get-tuple-element.56), channel_id=1, source_target_pairs={{0,48},{16,0},{32,16},{48,32},{1,49},{17,1},{33,17},{49,33},{2,50}... | collective-permute-start | bytes 786440 | tf_op jit(solution)/shard_map/ppermute | solution.py:348
  85.1 8.2 %collective-permute-start.16 = (f32[64,256]{1,0:T(8,128)S(1)}, f32[64,256]{1,0:T(8,128)S(1)}, u32[]{:S(2)}, u32[]{:S(2)}) collective-permute-start(f32[64,256]{1,0:T(8,128)S(1)} %slices_y.1.mine), channel_id=1, source_target_pairs={{0,64},{64,0},{128,192},{192,128},{1,65},{65,1},{129,193},{193,129... | collective-permute-start | bytes 196616 | tf_op jit(solution)/shard_map/ppermute | solution.py:351
  93.3 4.2 %collective-permute-start.17 = (f32[64,256]{1,0:T(8,128)S(1)}, f32[64,256]{1,0:T(8,128)S(1)}, u32[]{:S(2)}, u32[]{:S(2)}) collective-permute-start(f32[64,256]{1,0:T(8,128)S(1)} %slices_y.1.mine), channel_id=1, source_target_pairs={{0,128},{64,192},{128,0},{192,64},{1,129},{65,193},{129,1},{193,65... | collective-permute-start | bytes 196616 | tf_op jit(solution)/shard_map/ppermute | solution.py:351
  97.5 0.5 collective-permute-start.18
  98.0 0.1 spread.1
  98.0 2.5 %collective-permute-start.24 = (bf16[128,256]{1,0:T(8,128)(2,1)S(1)}, bf16[128,256]{1,0:T(8,128)(2,1)S(1)}, u32[]{:S(2)}, u32[]{:S(2)}) collective-permute-start(bf16[128,256]{1,0:T(8,128)(2,1)S(1)} %get-tuple-element.57.after), channel_id=1, source_target_pairs={{0,64},{64,0},{128,192},{192,128},{1,65},{65,1},{129,193},{193,129... | collective-permute-start | bytes 196616 | tf_op jit(solution)/shard_map/ppermute | solution.py:360
  100.5 3.7 %collective-permute-start.25 = (bf16[128,256]{1,0:T(8,128)(2,1)S(1)}, bf16[128,256]{1,0:T(8,128)(2,1)S(1)}, u32[]{:S(2)}, u32[]{:S(2)}) collective-permute-start(bf16[128,256]{1,0:T(8,128)(2,1)S(1)} %get-tuple-element.59), channel_id=1, source_target_pairs={{0,128},{64,192},{128,0},{192,64},{1,129},{65,193},{129,1},{193,65... | collective-permute-start | bytes 196616 | tf_op jit(solution)/shard_map/ppermute | solution.py:360
  104.2 0.5 collective-permute-start.26
  104.6 0.5 collective-permute-done.18.came3
  105.1 1.7 %collective-permute-start.21 = (f32[64,256]{1,0:T(8,128)S(1)}, f32[64,256]{1,0:T(8,128)S(1)}, u32[]{:S(2)}, u32[]{:S(2)}) collective-permute-start(f32[64,256]{1,0:T(8,128)S(1)} %slices_z.1.mine), channel_id=1, source_target_pairs={{0,4},{4,0},{1,5},{5,1},{2,6},{6,2},{3,7},{7,3},{8,12},{12,8},{9,1... | collective-permute-start | bytes 196616 | tf_op jit(solution)/shard_map/ppermute | solution.py:369
  106.8 2.1 %collective-permute-start.22 = (f32[64,256]{1,0:T(8,128)S(1)}, f32[64,256]{1,0:T(8,128)S(1)}, u32[]{:S(2)}, u32[]{:S(2)}) collective-permute-start(f32[64,256]{1,0:T(8,128)S(1)} %slices_z.1.mine), channel_id=1, source_target_pairs={{0,1},{1,0},{2,3},{3,2},{4,5},{5,4},{6,7},{7,6},{8,9},{9,8},{10,11... | collective-permute-start | bytes 196616 | tf_op jit(solution)/shard_map/ppermute | solution.py:370
  109.0 1.2 %collective-permute-done.25.came2 = bf16[128,256]{1,0:T(8,128)(2,1)S(1)} collective-permute-done((bf16[128,256]{1,0:T(8,128)(2,1)S(1)}, bf16[128,256]{1,0:T(8,128)(2,1)S(1)}, u32[]{:S(2)}, u32[]{:S(2)}) %collective-permute-start.25) | collective-permute-done | bytes 65568 | tf_op jit(solution)/shard_map/ppermute | solution.py:360
  110.1 0.5 collective-permute-done.26.came3
  110.7 0.7 last.1
  111.4 2.7 %collective-permute-done.23.over_both = f32[64,256]{1,0:T(8,128)S(1)} collective-permute-done((f32[64,256]{1,0:T(8,128)S(1)}, f32[64,256]{1,0:T(8,128)S(1)}, u32[]{:S(2)}, u32[]{:S(2)}) %collective-permute-start.23) | collective-permute-done | bytes 65568 | tf_op jit(solution)/shard_map/ppermute | solution.py:371
  114.2 0.7 join.1
  (26 shorter events, 0.1 us)
Async XLA Ops:
  2.3 13.8 %collective-permute-start = (bf16[528,256]{1,0:T(8,128)(2,1)S(1)}, bf16[528,256]{1,0:T(8,128)(2,1)S(1)}, u32[]{:S(2)}, u32[]{:S(2)}) collective-permute-start(bf16[528,256]{1,0:T(8,128)(2,1)S(1)} %piece.1), channel_id=1, source_target_pairs={{0,192},{1,200},{2,0},{3,8},{4,128},{5,136},{6,64},{7,72},{8,240},... | collective-permute-start | bytes 811016 | tf_op jit(solution)/shard_map/ppermute | solution.py:283
  16.1 10.6 %collective-permute-start.2 = (bf16[528,256]{1,0:T(8,128)(2,1)S(1)}, bf16[528,256]{1,0:T(8,128)(2,1)S(1)}, u32[]{:S(2)}, u32[]{:S(2)}) collective-permute-start(bf16[528,256]{1,0:T(8,128)(2,1)S(1)} %collective-permute-done.p0), channel_id=1, source_target_pairs={{0,16},{16,32},{32,48},{48,0},{1,17},{17,33},{33,49},{49,1},{2,18}... | collective-permute-start | bytes 811016 | tf_op jit(solution)/shard_map/ppermute | solution.py:295
  18.0 9.3 %collective-permute-start.4 = (bf16[528,256]{1,0:T(8,128)(2,1)S(1)}, bf16[528,256]{1,0:T(8,128)(2,1)S(1)}, u32[]{:S(2)}, u32[]{:S(2)}) collective-permute-start(bf16[528,256]{1,0:T(8,128)(2,1)S(1)} %collective-permute-done.p0), channel_id=1, source_target_pairs={{0,48},{16,0},{32,16},{48,32},{1,49},{17,1},{33,17},{49,33},{2,50}... | collective-permute-start | bytes 811016 | tf_op jit(solution)/shard_map/ppermute | solution.py:296
  20.3 10.3 %collective-permute-start.1 = (bf16[528,256]{1,0:T(8,128)(2,1)S(1)}, bf16[528,256]{1,0:T(8,128)(2,1)S(1)}, u32[]{:S(2)}, u32[]{:S(2)}) collective-permute-start(bf16[528,256]{1,0:T(8,128)(2,1)S(1)} %collective-permute-done.p0), channel_id=1, source_target_pairs={{0,8},{8,0},{1,9},{9,1},{2,10},{10,2},{3,11},{11,3},{4,12},{12,4},... | collective-permute-start | bytes 811016 | tf_op jit(solution)/shard_map/ppermute | solution.py:302
  23.1 10.9 %copy-start.2 = (bf16[1024,2048]{1,0:T(8,128)(2,1)S(1)}, bf16[1024,2048]{1,0:T(8,128)(2,1)}, u32[]{:S(2)}) copy-start(bf16[1024,2048]{1,0:T(8,128)(2,1)} %get-tuple-element.34) | copy-start | bytes 12582916
  26.8 8.7 %collective-permute-start.6 = (bf16[256,256]{1,0:T(8,128)(2,1)S(1)}, bf16[256,256]{1,0:T(8,128)(2,1)S(1)}, u32[]{:S(2)}, u32[]{:S(2)}) collective-permute-start(bf16[256,256]{1,0:T(8,128)(2,1)S(1)} %slice.89), channel_id=1, source_target_pairs={{0,16},{16,32},{32,48},{48,0},{1,17},{17,33},{33,49},{49,1},{2,18}... | collective-permute-start | bytes 393224 | tf_op jit(solution)/shard_map/ppermute | solution.py:297
  27.3 8.6 %collective-permute-start.8 = (bf16[272,256]{1,0:T(8,128)(2,1)S(1)}, bf16[272,256]{1,0:T(8,128)(2,1)S(1)}, u32[]{:S(2)}, u32[]{:S(2)}) collective-permute-start(bf16[272,256]{1,0:T(8,128)(2,1)S(1)} %slice.90), channel_id=1, source_target_pairs={{0,48},{16,0},{32,16},{48,32},{1,49},{17,1},{33,17},{49,33},{2,50}... | collective-permute-start | bytes 417800 | tf_op jit(solution)/shard_map/ppermute | solution.py:298
  33.9 2.8 %copy-start.1 = (bf16[1024,2048]{1,0:T(8,128)(2,1)S(1)}, bf16[1024,2048]{1,0:T(8,128)(2,1)}, u32[]{:S(2)}) copy-start(bf16[1024,2048]{1,0:T(8,128)(2,1)} %get-tuple-element.36) | copy-start | bytes 12582916
  34.4 2.3 %collective-permute-start.3 = (bf16[528,256]{1,0:T(8,128)(2,1)S(1)}, bf16[528,256]{1,0:T(8,128)(2,1)S(1)}, u32[]{:S(2)}, u32[]{:S(2)}) collective-permute-start(bf16[528,256]{1,0:T(8,128)(2,1)S(1)} %collective-permute-done.2.p1), channel_id=1, source_target_pairs={{0,8},{8,0},{1,9},{9,1},{2,10},{10,2},{3,11},{11,3},{4,12},{12,4},... | collective-permute-start | bytes 811016 | tf_op jit(solution)/shard_map/ppermute | solution.py:302
  34.5 2.7 %collective-permute-start.5 = (bf16[528,256]{1,0:T(8,128)(2,1)S(1)}, bf16[528,256]{1,0:T(8,128)(2,1)S(1)}, u32[]{:S(2)}, u32[]{:S(2)}) collective-permute-start(bf16[528,256]{1,0:T(8,128)(2,1)S(1)} %collective-permute-done.4.p2), channel_id=1, source_target_pairs={{0,8},{8,0},{1,9},{9,1},{2,10},{10,2},{3,11},{11,3},{4,12},{12,4},... | collective-permute-start | bytes 811016 | tf_op jit(solution)/shard_map/ppermute | solution.py:302
  35.8 1.9 %collective-permute-start.7 = (bf16[256,256]{1,0:T(8,128)(2,1)S(1)}, bf16[256,256]{1,0:T(8,128)(2,1)S(1)}, u32[]{:S(2)}, u32[]{:S(2)}) collective-permute-start(bf16[256,256]{1,0:T(8,128)(2,1)S(1)} %collective-permute-done.6), channel_id=1, source_target_pairs={{0,8},{8,0},{1,9},{9,1},{2,10},{10,2},{3,11},{11,3},{4,12},{12,4},... | collective-permute-start | bytes 393224 | tf_op jit(solution)/shard_map/ppermute | solution.py:302
  35.9 2.1 %collective-permute-start.9 = (bf16[272,256]{1,0:T(8,128)(2,1)S(1)}, bf16[272,256]{1,0:T(8,128)(2,1)S(1)}, u32[]{:S(2)}, u32[]{:S(2)}) collective-permute-start(bf16[272,256]{1,0:T(8,128)(2,1)S(1)} %collective-permute-done.8.p3), channel_id=1, source_target_pairs={{0,8},{8,0},{1,9},{9,1},{2,10},{10,2},{3,11},{11,3},{4,12},{12,4},... | collective-permute-start | bytes 417800 | tf_op jit(solution)/shard_map/ppermute | solution.py:302
  37.6 14.0 %copy-start = (bf16[256,256]{1,0:T(8,128)(2,1)S(1)}, bf16[256,256]{1,0:T(8,128)(2,1)}, u32[]{:S(2)}) copy-start(bf16[256,256]{1,0:T(8,128)(2,1)} %refs_4_.1) | copy-start | bytes 393220
  69.0 2.8 %collective-permute-start.10 = (bf16[2112,256]{1,0:T(8,128)(2,1)S(1)}, bf16[2112,256]{1,0:T(8,128)(2,1)S(1)}, u32[]{:S(2)}, u32[]{:S(2)}) collective-permute-start(bf16[2112,256]{1,0:T(8,128)(2,1)S(1)} %regroup_send.1), channel_id=1, source_target_pairs={{0,8},{8,0},{1,9},{9,1},{2,10},{10,2},{3,11},{11,3},{4,12},{12,4},... | collective-permute-start | bytes 3244040 | tf_op jit(solution)/shard_map/ppermute | solution.py:329
  72.1 9.7 %collective-permute-start.11 = (bf16[256,256]{1,0:T(8,128)(2,1)S(1)}, bf16[256,256]{1,0:T(8,128)(2,1)S(1)}, u32[]{:S(2)}, u32[]{:S(2)}) collective-permute-start(bf16[256,256]{1,0:T(8,128)(2,1)S(1)} %get-tuple-element.50), channel_id=1, source_target_pairs={{0,16},{16,32},{32,48},{48,0},{1,17},{17,33},{33,49},{49,1},{2,18}... | collective-permute-start | bytes 393224 | tf_op jit(solution)/shard_map/ppermute | solution.py:338
  72.2 9.6 %collective-permute-start.12 = (bf16[256,256]{1,0:T(8,128)(2,1)S(1)}, bf16[256,256]{1,0:T(8,128)(2,1)S(1)}, u32[]{:S(2)}, u32[]{:S(2)}) collective-permute-start(bf16[256,256]{1,0:T(8,128)(2,1)S(1)} %get-tuple-element.51), channel_id=1, source_target_pairs={{0,48},{16,0},{32,16},{48,32},{1,49},{17,1},{33,17},{49,33},{2,50}... | collective-permute-start | bytes 393224 | tf_op jit(solution)/shard_map/ppermute | solution.py:338
  75.4 5.1 %collective-permute-start.13 = (bf16[64,256]{1,0:T(8,128)(2,1)S(1)}, bf16[64,256]{1,0:T(8,128)(2,1)S(1)}, u32[]{:S(2)}, u32[]{:S(2)}) collective-permute-start(bf16[64,256]{1,0:T(8,128)(2,1)S(1)} %slices.1.mine), channel_id=1, source_target_pairs={{0,16},{16,32},{32,48},{48,0},{1,17},{17,33},{33,49},{49,1},{2,18}... | collective-permute-start | bytes 98312 | tf_op jit(solution)/shard_map/ppermute | solution.py:340
  75.4 5.5 %collective-permute-start.14 = (bf16[64,256]{1,0:T(8,128)(2,1)S(1)}, bf16[64,256]{1,0:T(8,128)(2,1)S(1)}, u32[]{:S(2)}, u32[]{:S(2)}) collective-permute-start(bf16[64,256]{1,0:T(8,128)(2,1)S(1)} %slices.1.mine), channel_id=1, source_target_pairs={{0,32},{16,48},{32,0},{48,16},{1,33},{17,49},{33,1},{49,17},{2,34}... | collective-permute-start | bytes 98312 | tf_op jit(solution)/shard_map/ppermute | solution.py:340
  77.7 4.0 %collective-permute-start.15 = (bf16[64,256]{1,0:T(8,128)(2,1)S(1)}, bf16[64,256]{1,0:T(8,128)(2,1)S(1)}, u32[]{:S(2)}, u32[]{:S(2)}) collective-permute-start(bf16[64,256]{1,0:T(8,128)(2,1)S(1)} %slices.1.mine), channel_id=1, source_target_pairs={{0,48},{16,0},{32,16},{48,32},{1,49},{17,1},{33,17},{49,33},{2,50}... | collective-permute-start | bytes 98312 | tf_op jit(solution)/shard_map/ppermute | solution.py:340
  81.8 16.1 %collective-permute-start.19 = (bf16[512,256]{1,0:T(8,128)(2,1)S(1)}, bf16[512,256]{1,0:T(8,128)(2,1)S(1)}, u32[]{:S(2)}, u32[]{:S(2)}) collective-permute-start(bf16[512,256]{1,0:T(8,128)(2,1)S(1)} %get-tuple-element.55), channel_id=1, source_target_pairs={{0,16},{16,32},{32,48},{48,0},{1,17},{17,33},{33,49},{49,1},{2,18}... | collective-permute-start | bytes 786440 | tf_op jit(solution)/shard_map/ppermute | solution.py:348
  83.6 14.4 %collective-permute-start.20 = (bf16[512,256]{1,0:T(8,128)(2,1)S(1)}, bf16[512,256]{1,0:T(8,128)(2,1)S(1)}, u32[]{:S(2)}, u32[]{:S(2)}) collective-permute-start(bf16[512,256]{1,0:T(8,128)(2,1)S(1)} %get-tuple-element.56), channel_id=1, source_target_pairs={{0,48},{16,0},{32,16},{48,32},{1,49},{17,1},{33,17},{49,33},{2,50}... | collective-permute-start | bytes 786440 | tf_op jit(solution)/shard_map/ppermute | solution.py:348
  85.1 19.0 %collective-permute-start.16 = (f32[64,256]{1,0:T(8,128)S(1)}, f32[64,256]{1,0:T(8,128)S(1)}, u32[]{:S(2)}, u32[]{:S(2)}) collective-permute-start(f32[64,256]{1,0:T(8,128)S(1)} %slices_y.1.mine), channel_id=1, source_target_pairs={{0,64},{64,0},{128,192},{192,128},{1,65},{65,1},{129,193},{193,129... | collective-permute-start | bytes 196616 | tf_op jit(solution)/shard_map/ppermute | solution.py:351
  93.3 11.3 %collective-permute-start.17 = (f32[64,256]{1,0:T(8,128)S(1)}, f32[64,256]{1,0:T(8,128)S(1)}, u32[]{:S(2)}, u32[]{:S(2)}) collective-permute-start(f32[64,256]{1,0:T(8,128)S(1)} %slices_y.1.mine), channel_id=1, source_target_pairs={{0,128},{64,192},{128,0},{192,64},{1,129},{65,193},{129,1},{193,65... | collective-permute-start | bytes 196616 | tf_op jit(solution)/shard_map/ppermute | solution.py:351
  97.5 7.6 %collective-permute-start.18 = (f32[64,256]{1,0:T(8,128)S(1)}, f32[64,256]{1,0:T(8,128)S(1)}, u32[]{:S(2)}, u32[]{:S(2)}) collective-permute-start(f32[64,256]{1,0:T(8,128)S(1)} %slices_y.1.mine), channel_id=1, source_target_pairs={{0,192},{64,128},{128,64},{192,0},{1,193},{65,129},{129,65},{193,1... | collective-permute-start | bytes 196616 | tf_op jit(solution)/shard_map/ppermute | solution.py:351
  98.0 10.9 %collective-permute-start.24 = (bf16[128,256]{1,0:T(8,128)(2,1)S(1)}, bf16[128,256]{1,0:T(8,128)(2,1)S(1)}, u32[]{:S(2)}, u32[]{:S(2)}) collective-permute-start(bf16[128,256]{1,0:T(8,128)(2,1)S(1)} %get-tuple-element.57.after), channel_id=1, source_target_pairs={{0,64},{64,0},{128,192},{192,128},{1,65},{65,1},{129,193},{193,129... | collective-permute-start | bytes 196616 | tf_op jit(solution)/shard_map/ppermute | solution.py:360
  100.5 9.6 %collective-permute-start.25 = (bf16[128,256]{1,0:T(8,128)(2,1)S(1)}, bf16[128,256]{1,0:T(8,128)(2,1)S(1)}, u32[]{:S(2)}, u32[]{:S(2)}) collective-permute-start(bf16[128,256]{1,0:T(8,128)(2,1)S(1)} %get-tuple-element.59), channel_id=1, source_target_pairs={{0,128},{64,192},{128,0},{192,64},{1,129},{65,193},{129,1},{193,65... | collective-permute-start | bytes 196616 | tf_op jit(solution)/shard_map/ppermute | solution.py:360
  104.2 6.5 %collective-permute-start.26 = (bf16[128,256]{1,0:T(8,128)(2,1)S(1)}, bf16[128,256]{1,0:T(8,128)(2,1)S(1)}, u32[]{:S(2)}, u32[]{:S(2)}) collective-permute-start(bf16[128,256]{1,0:T(8,128)(2,1)S(1)} %get-tuple-element.60), channel_id=1, source_target_pairs={{0,192},{64,128},{128,64},{192,0},{1,193},{65,129},{129,65},{193,1... | collective-permute-start | bytes 196616 | tf_op jit(solution)/shard_map/ppermute | solution.py:360
  105.1 6.3 %collective-permute-start.21 = (f32[64,256]{1,0:T(8,128)S(1)}, f32[64,256]{1,0:T(8,128)S(1)}, u32[]{:S(2)}, u32[]{:S(2)}) collective-permute-start(f32[64,256]{1,0:T(8,128)S(1)} %slices_z.1.mine), channel_id=1, source_target_pairs={{0,4},{4,0},{1,5},{5,1},{2,6},{6,2},{3,7},{7,3},{8,12},{12,8},{9,1... | collective-permute-start | bytes 196616 | tf_op jit(solution)/shard_map/ppermute | solution.py:369
  106.8 4.6 %collective-permute-start.22 = (f32[64,256]{1,0:T(8,128)S(1)}, f32[64,256]{1,0:T(8,128)S(1)}, u32[]{:S(2)}, u32[]{:S(2)}) collective-permute-start(f32[64,256]{1,0:T(8,128)S(1)} %slices_z.1.mine), channel_id=1, source_target_pairs={{0,1},{1,0},{2,3},{3,2},{4,5},{5,4},{6,7},{7,6},{8,9},{9,8},{10,11... | collective-permute-start | bytes 196616 | tf_op jit(solution)/shard_map/ppermute | solution.py:370
  109.0 5.2 %collective-permute-start.23 = (f32[64,256]{1,0:T(8,128)S(1)}, f32[64,256]{1,0:T(8,128)S(1)}, u32[]{:S(2)}, u32[]{:S(2)}) collective-permute-start(f32[64,256]{1,0:T(8,128)S(1)} %slices_z.1.mine), channel_id=1, source_target_pairs={{0,5},{1,4},{2,7},{3,6},{4,1},{5,0},{6,3},{7,2},{8,13},{9,12},{10,... | collective-permute-start | bytes 196616 | tf_op jit(solution)/shard_map/ppermute | solution.py:371

commit v8 on v7

--- a/solution.py
+++ b/solution.py
@@ -73,14 +73,17 @@
     )(*scalars, *arrays)
 
 
-def piece_body(half, degrees, features, out, tiles, sems):
+def piece_body(half, degrees, features, out, tiles, near, sems):
     def copy(k):
         at = pl.ds(pl.multiple_of((2 * k + half[0]) * TILE, TILE), TILE)
         return pltpu.make_async_copy(features.at[at], tiles.at[k], sems.at[k])
 
+    fetch = pltpu.make_async_copy(degrees, near, sems.at[4])
+    fetch.start()
     for k in range(4):
         copy(k).start()
-    all_rows = degrees[...].astype(F32)
+    fetch.wait()
+    all_rows = near[...].astype(F32)
     line = lax.broadcasted_iota(jnp.int32, (16, TILE), 0)
     below = jnp.zeros((16, TILE), F32)
     columns = []
@@ -277,8 +280,13 @@
         return pltpu.VMEM((rows, width), kind)
 
     piece = call(
-        piece_body, "piece", held(PIECE + 16), [(x + (y >> 1)) & 1], [degrees, features], [WHOLE, HBM],
-        [pltpu.VMEM((4, TILE, width), BF16), pltpu.SemaphoreType.DMA((4,))], LIMIT,
+        piece_body, "piece", held(PIECE + 16), [(x + (y >> 1)) & 1], [degrees, features], [HBM, HBM],
+        [
+            pltpu.VMEM((4, TILE, width), BF16),
+            pltpu.VMEM(degrees.shape, BF16),
+            pltpu.SemaphoreType.DMA((5,)),
+        ],
+        LIMIT,
     )
     piece = lax.ppermute(piece, ALL, piece_route())
     scaled, cot, deg = call(

time: 115 us -> 115 us (level)
  starting transfers between devices: 49.4 us -> 47.1 us
  waiting for transfers between devices: 13 us -> 14.9 us
    ppermute x1, waiting for transfers between devices: 3.68 us -> 5.33 us  [shards(): first = lax.ppermute(piece, 'y', ahead)]
    ppermute x1, starting transfers between devices: 1.89 us -> 0.38 us  [shards(): first = lax.ppermute(piece, 'y', ahead)]
  transfers between devices with their start and end apart: 27 -> 27, of which waited for: 9 -> 10; matrix products, arithmetic and copies ran while one was open for 7% -> 7% of each run, Pallas kernels for 9% -> 10%
where the time goes in v8:
time: 115 us; the launch traced here: 114 us
  starting transfers between devices  47.1 us (41%)
  blocking collectives  27.8 us (24%)
  waiting for transfers between devices  14.9 us (13%)
  Pallas kernels  14.3 us (12%)
  matrix products  9.13 us (8%)
    all_to_all x1, blocking collectives, shards(): both = lax.all_to_all(both, REP, 0, 0)  15 us
    ppermute x3, starting transfers between devices, shards(): w_z = [lax.ppermute(w_rows, 'zh', route) for route in exchange]  12.9 us
    all_to_all x1, blocking collectives, shards(): parts = lax.all_to_all(partial.reshape(ZL * X, TILE, width), REP, 0, 0)  12.8 us
    pallas_call x1, Pallas kernels, assemble(): pl.pallas_call(assemble_body, out_shape=(half, half), in_specs=[SMEM] * 6...  8.8 us
    ppermute x3, starting transfers between devices, shards(): lax.ppermute(part, 'zh', route)  6.58 us
    ppermute x1, starting transfers between devices, shards(): piece = lax.ppermute(piece, ALL, piece_route())  5.79 us
    pallas_call x12, Pallas kernels, call(): pl.pallas_call(body, out_shape=outs, in_specs=[SMEM] * len(scalars) + (sp...  5.49 us
    ppermute x1, waiting for transfers between devices, shards(): first = lax.ppermute(piece, 'y', ahead)  5.33 us
  transfers between devices with their start and end apart: 27, of which 10 were waited for; matrix products, arithmetic and copies ran while one was open for 7% of the time, Pallas kernels for 10%

profile of v8, /device:TPU:2, one launch (start us, length us, event | category | flops | bytes accessed | tf_op | source)
XLA Modules:
  0.0 114.2 jit_solution(104671299458500876)
XLA Ops:
  0.6 1.0 piece.1
  1.7 5.8 %collective-permute-start = (bf16[528,256]{1,0:T(8,128)(2,1)S(1)}, bf16[528,256]{1,0:T(8,128)(2,1)S(1)}, u32[]{:S(2)}, u32[]{:S(2)}) collective-permute-start(bf16[528,256]{1,0:T(8,128)(2,1)S(1)} %piece.1), channel_id=1, source_target_pairs={{0,192},{1,200},{2,0},{3,8},{4,128},{5,136},{6,64},{7,72},{8,240},... | collective-permute-start | bytes 811016 | tf_op jit(solution)/shard_map/ppermute | solution.py:291
  7.4 8.8 %assemble.1 = (bf16[1024,2048]{1,0:T(8,128)(2,1)}, bf16[1024,2048]{1,0:T(8,128)(2,1)}) custom-call(s32[1,4]{1,0:T(1,128)} %count.1, s32[1]{0:T(128)} %bitcast.3.core, s32[1]{0:T(128)} %bitcast.1.y, s32[1]{0:T(128)S(6)} %and.23.odd.xl, s32[1,128]{1,0:T(1,128)} %row.1, s32[1,128]{1,0:T(1,128)} %col.1, bf16[1,128,128,128]{3,2,1,0:T(8,128)(2,1)} %vals.1), custom_call_target="tpu_custom_call" | custom-call | tf_op jit(solution)/shard_map/assemble/pallas_call | solution.py:147
  16.3 0.4 collective-permute-start.2
  16.6 2.9 %collective-permute-start.4 = (bf16[528,256]{1,0:T(8,128)(2,1)S(1)}, bf16[528,256]{1,0:T(8,128)(2,1)S(1)}, u32[]{:S(2)}, u32[]{:S(2)}) collective-permute-start(bf16[528,256]{1,0:T(8,128)(2,1)S(1)} %collective-permute-done.p0), channel_id=1, source_target_pairs={{0,48},{16,0},{32,16},{48,32},{1,49},{17,1},{33,17},{49,33},{2,50}... | collective-permute-start | bytes 811016 | tf_op jit(solution)/shard_map/ppermute | solution.py:304
  19.6 0.3 collective-permute-start.1
  19.9 1.6 %share.1 = (bf16[128,256]{1,0:T(8,128)(2,1)S(1)}, bf16[128,256]{1,0:T(8,128)(2,1)S(1)}, f32[128,256]{1,0:T(8,128)S(1)}) custom-call(s32[1]{0:T(128)} %bitcast.4.replica, bf16[8,128]{1,0:T(8,128)(2,1)} %bitcast.21, bf16[1024,256]{1,0:T(8,128)(2,1)} %features.3, bf16[1024,256]{1,0:T(8,128)(2,1)} %cotangent.1), custom_call_target="tpu_custom_call" | custom-call | tf_op jit(solution)/shard_map/share/pallas_call | solution.py:65
  21.5 5.3 %collective-permute-done.2.p1 = bf16[528,256]{1,0:T(8,128)(2,1)S(1)} collective-permute-done((bf16[528,256]{1,0:T(8,128)(2,1)S(1)}, bf16[528,256]{1,0:T(8,128)(2,1)S(1)}, u32[]{:S(2)}, u32[]{:S(2)}) %collective-permute-start.2) | collective-permute-done | bytes 270368 | tf_op jit(solution)/shard_map/ppermute | solution.py:303
  26.9 0.1 collective-permute-start.6
  26.9 0.2 collective-permute-done.4.p2
  27.2 3.1 %collective-permute-start.8 = (bf16[272,256]{1,0:T(8,128)(2,1)S(1)}, bf16[272,256]{1,0:T(8,128)(2,1)S(1)}, u32[]{:S(2)}, u32[]{:S(2)}) collective-permute-start(bf16[272,256]{1,0:T(8,128)(2,1)S(1)} %slice.90), channel_id=1, source_target_pairs={{0,48},{16,0},{32,16},{48,32},{1,49},{17,1},{33,17},{49,33},{2,50}... | collective-permute-start | bytes 417800 | tf_op jit(solution)/shard_map/ppermute | solution.py:306
  30.3 1.7 %fusion.9 = f32[1024,256]{1,0:T(8,128)S(1)} fusion(bf16[1024,2048]{1,0:T(8,128)(2,1)} %get-tuple-element.36, bf16[528,256]{1,0:T(8,128)(2,1)S(1)} %collective-permute-done.1), kind=kOutput, calls=%fused_computation.15 | convolution fusion | flops 268435456 | bytes 2359296 | tf_op jit(solution)/shard_map/dot_general | solution.py:314
  31.9 1.7 %convolution_add_fusion.5 = f32[1024,256]{1,0:T(8,128)S(1)} fusion(f32[1024,256]{1,0:T(8,128)S(1)} %fusion.9, bf16[1024,2048]{1,0:T(8,128)(2,1)} %get-tuple-element.34, bf16[528,256]{1,0:T(8,128)(2,1)S(1)} %collective-permute-done.p0), kind=kOutput, calls=%fused_computation.8 | convolution fusion | flops 268697600 | bytes 3407872 | tf_op jit(solution)/shard_map/dot_general | solution.py:302
  33.6 0.4 fusion.5
  34.1 0.1 collective-permute-start.3
  34.2 0.5 collective-permute-start.5
  34.7 0.4 convolution_add_fusion.4
  35.1 0.3 fusion.16
  35.4 0.2 collective-permute-start.7
  35.6 0.4 collective-permute-start.9
  36.0 0.3 fusion.13
  36.4 0.5 fusion.2
  36.8 0.0 collective-permute-done.5
  36.8 0.5 fusion.1
  37.3 0.0 copy-start
  37.3 0.0 collective-permute-done.7
  37.3 0.4 fusion
  37.7 0.0 collective-permute-done.9
  37.7 0.3 fusion.3
  38.0 12.8 %all_to_all.10.refs_0_ = bf16[8,128,256]{2,1,0:T(8,128)(2,1)S(1)} all-to-all(bf16[8,128,256]{2,1,0:T(8,128)(2,1)S(1)} %bitcast.17), channel_id=1, replica_groups=mesh['zh'=4,'y'=4,'c'=2,'zl'=2,'x'=4] {'zl','x'}, dimensions={0} | all-to-all | bytes 1048576 | tf_op jit(solution)/shard_map/all_to_all | solution.py:321
  50.9 0.8 middle.1
  51.7 15.0 %all_to_all.11.both = bf16[8,192,256]{2,1,0:T(8,128)(2,1)S(1)} all-to-all(bf16[8,192,256]{2,1,0:T(8,128)(2,1)S(1)} %get-tuple-element.47), channel_id=1, replica_groups=mesh['zh'=4,'y'=4,'c'=2,'zl'=2,'x'=4] {'zl','x'}, dimensions={0} | all-to-all | bytes 1572864 | tf_op jit(solution)/shard_map/all_to_all | solution.py:329
  66.8 1.3 %fusion.27.rows = f32[2048,256]{1,0:T(8,128)S(1)} fusion(bf16[1024,2048]{1,0:T(8,128)(2,1)S(1)} %copy-done.1, bf16[1024,256]{1,0:T(8,128)(2,1)S(1)} %bitcast.18), kind=kOutput, calls=%fused_computation.33 | convolution fusion | flops 1073741824 | bytes 6815744 | tf_op jit(solution)/shard_map/dot_general | solution.py:334
  68.1 0.2 regroup_send.1
  68.3 0.1 collective-permute-start.10
  68.4 1.3 %fusion.26.rows = f32[2048,256]{1,0:T(8,128)S(1)} fusion(bf16[1024,2048]{1,0:T(8,128)(2,1)S(1)} %copy-done.2, bf16[1024,256]{1,0:T(8,128)(2,1)S(1)} %bitcast.19), kind=kOutput, calls=%fused_computation.32 | convolution fusion | flops 1073741824 | bytes 6815744 | tf_op jit(solution)/shard_map/dot_general | solution.py:334
  69.8 1.3 %collective-permute-done.10.others = bf16[2112,256]{1,0:T(8,128)(2,1)S(1)} collective-permute-done((bf16[2112,256]{1,0:T(8,128)(2,1)S(1)}, bf16[2112,256]{1,0:T(8,128)(2,1)S(1)}, u32[]{:S(2)}, u32[]{:S(2)}) %collective-permute-start.10) | collective-permute-done | bytes 1081376 | tf_op jit(solution)/shard_map/ppermute | solution.py:337
  71.1 0.2 regroup_keep.1
  71.3 0.1 collective-permute-start.11
  71.4 3.2 %collective-permute-start.12 = (bf16[256,256]{1,0:T(8,128)(2,1)S(1)}, bf16[256,256]{1,0:T(8,128)(2,1)S(1)}, u32[]{:S(2)}, u32[]{:S(2)}) collective-permute-start(bf16[256,256]{1,0:T(8,128)(2,1)S(1)} %get-tuple-element.51), channel_id=1, source_target_pairs={{0,48},{16,0},{32,16},{48,32},{1,49},{17,1},{33,17},{49,33},{2,50}... | collective-permute-start | bytes 393224 | tf_op jit(solution)/shard_map/ppermute | solution.py:346
  74.7 2.0 %collective-permute-start.14 = (bf16[64,256]{1,0:T(8,128)(2,1)S(1)}, bf16[64,256]{1,0:T(8,128)(2,1)S(1)}, u32[]{:S(2)}, u32[]{:S(2)}) collective-permute-start(bf16[64,256]{1,0:T(8,128)(2,1)S(1)} %slices.1.mine), channel_id=1, source_target_pairs={{0,32},{16,48},{32,0},{48,16},{1,33},{17,49},{33,1},{49,17},{2,34}... | collective-permute-start | bytes 98312 | tf_op jit(solution)/shard_map/ppermute | solution.py:348
  76.6 1.3 %collective-permute-start.15 = (bf16[64,256]{1,0:T(8,128)(2,1)S(1)}, bf16[64,256]{1,0:T(8,128)(2,1)S(1)}, u32[]{:S(2)}, u32[]{:S(2)}) collective-permute-start(bf16[64,256]{1,0:T(8,128)(2,1)S(1)} %slices.1.mine), channel_id=1, source_target_pairs={{0,48},{16,0},{32,16},{48,32},{1,49},{17,1},{33,17},{49,33},{2,50}... | collective-permute-start | bytes 98312 | tf_op jit(solution)/shard_map/ppermute | solution.py:348
  77.9 1.9 %collective-permute-done.13.came1 = bf16[64,256]{1,0:T(8,128)(2,1)S(1)} collective-permute-done((bf16[64,256]{1,0:T(8,128)(2,1)S(1)}, bf16[64,256]{1,0:T(8,128)(2,1)S(1)}, u32[]{:S(2)}, u32[]{:S(2)}) %collective-permute-start.13) | collective-permute-done | bytes 32800 | tf_op jit(solution)/shard_map/ppermute | solution.py:348
  79.8 0.3 collective-permute-done.14.came2
  80.1 0.9 collective-permute-done.15.came3
  81.0 0.1 relay.1
  81.1 1.8 %collective-permute-start.19 = (bf16[512,256]{1,0:T(8,128)(2,1)S(1)}, bf16[512,256]{1,0:T(8,128)(2,1)S(1)}, u32[]{:S(2)}, u32[]{:S(2)}) collective-permute-start(bf16[512,256]{1,0:T(8,128)(2,1)S(1)} %get-tuple-element.55), channel_id=1, source_target_pairs={{0,16},{16,32},{32,48},{48,0},{1,17},{17,33},{33,49},{49,1},{2,18}... | collective-permute-start | bytes 786440 | tf_op jit(solution)/shard_map/ppermute | solution.py:356
  82.8 1.6 %collective-permute-start.20 = (bf16[512,256]{1,0:T(8,128)(2,1)S(1)}, bf16[512,256]{1,0:T(8,128)(2,1)S(1)}, u32[]{:S(2)}, u32[]{:S(2)}) collective-permute-start(bf16[512,256]{1,0:T(8,128)(2,1)S(1)} %get-tuple-element.56), channel_id=1, source_target_pairs={{0,48},{16,0},{32,16},{48,32},{1,49},{17,1},{33,17},{49,33},{2,50}... | collective-permute-start | bytes 786440 | tf_op jit(solution)/shard_map/ppermute | solution.py:356
  84.4 8.2 %collective-permute-start.16 = (f32[64,256]{1,0:T(8,128)S(1)}, f32[64,256]{1,0:T(8,128)S(1)}, u32[]{:S(2)}, u32[]{:S(2)}) collective-permute-start(f32[64,256]{1,0:T(8,128)S(1)} %slices_y.1.mine), channel_id=1, source_target_pairs={{0,64},{64,0},{128,192},{192,128},{1,65},{65,1},{129,193},{193,129... | collective-permute-start | bytes 196616 | tf_op jit(solution)/shard_map/ppermute | solution.py:359
  92.6 4.2 %collective-permute-start.17 = (f32[64,256]{1,0:T(8,128)S(1)}, f32[64,256]{1,0:T(8,128)S(1)}, u32[]{:S(2)}, u32[]{:S(2)}) collective-permute-start(f32[64,256]{1,0:T(8,128)S(1)} %slices_y.1.mine), channel_id=1, source_target_pairs={{0,128},{64,192},{128,0},{192,64},{1,129},{65,193},{129,1},{193,65... | collective-permute-start | bytes 196616 | tf_op jit(solution)/shard_map/ppermute | solution.py:359
  96.8 0.5 collective-permute-start.18
  97.3 0.1 spread.1
  97.4 2.5 %collective-permute-start.24 = (bf16[128,256]{1,0:T(8,128)(2,1)S(1)}, bf16[128,256]{1,0:T(8,128)(2,1)S(1)}, u32[]{:S(2)}, u32[]{:S(2)}) collective-permute-start(bf16[128,256]{1,0:T(8,128)(2,1)S(1)} %get-tuple-element.57.after), channel_id=1, source_target_pairs={{0,64},{64,0},{128,192},{192,128},{1,65},{65,1},{129,193},{193,129... | collective-permute-start | bytes 196616 | tf_op jit(solution)/shard_map/ppermute | solution.py:368
  99.8 3.7 %collective-permute-start.25 = (bf16[128,256]{1,0:T(8,128)(2,1)S(1)}, bf16[128,256]{1,0:T(8,128)(2,1)S(1)}, u32[]{:S(2)}, u32[]{:S(2)}) collective-permute-start(bf16[128,256]{1,0:T(8,128)(2,1)S(1)} %get-tuple-element.59), channel_id=1, source_target_pairs={{0,128},{64,192},{128,0},{192,64},{1,129},{65,193},{129,1},{193,65... | collective-permute-start | bytes 196616 | tf_op jit(solution)/shard_map/ppermute | solution.py:368
  103.5 0.0 collective-permute-done.16.came1
  103.5 0.5 collective-permute-start.26
  104.0 0.5 collective-permute-done.18.came3
  104.4 1.7 %collective-permute-start.21 = (f32[64,256]{1,0:T(8,128)S(1)}, f32[64,256]{1,0:T(8,128)S(1)}, u32[]{:S(2)}, u32[]{:S(2)}) collective-permute-start(f32[64,256]{1,0:T(8,128)S(1)} %slices_z.1.mine), channel_id=1, source_target_pairs={{0,4},{4,0},{1,5},{5,1},{2,6},{6,2},{3,7},{7,3},{8,12},{12,8},{9,1... | collective-permute-start | bytes 196616 | tf_op jit(solution)/shard_map/ppermute | solution.py:377
  106.2 2.1 %collective-permute-start.22 = (f32[64,256]{1,0:T(8,128)S(1)}, f32[64,256]{1,0:T(8,128)S(1)}, u32[]{:S(2)}, u32[]{:S(2)}) collective-permute-start(f32[64,256]{1,0:T(8,128)S(1)} %slices_z.1.mine), channel_id=1, source_target_pairs={{0,1},{1,0},{2,3},{3,2},{4,5},{5,4},{6,7},{7,6},{8,9},{9,8},{10,11... | collective-permute-start | bytes 196616 | tf_op jit(solution)/shard_map/ppermute | solution.py:378
  108.3 1.1 %collective-permute-done.25.came2 = bf16[128,256]{1,0:T(8,128)(2,1)S(1)} collective-permute-done((bf16[128,256]{1,0:T(8,128)(2,1)S(1)}, bf16[128,256]{1,0:T(8,128)(2,1)S(1)}, u32[]{:S(2)}, u32[]{:S(2)}) %collective-permute-start.25) | collective-permute-done | bytes 65568 | tf_op jit(solution)/shard_map/ppermute | solution.py:368
  109.5 0.6 collective-permute-done.26.came3
  110.0 0.7 last.1
  110.8 2.7 %collective-permute-done.23.over_both = f32[64,256]{1,0:T(8,128)S(1)} collective-permute-done((f32[64,256]{1,0:T(8,128)S(1)}, f32[64,256]{1,0:T(8,128)S(1)}, u32[]{:S(2)}, u32[]{:S(2)}) %collective-permute-start.23) | collective-permute-done | bytes 65568 | tf_op jit(solution)/shard_map/ppermute | solution.py:379
  113.5 0.7 join.1
  (26 shorter events, 0.1 us)
Async XLA Ops:
  1.7 14.6 %collective-permute-start = (bf16[528,256]{1,0:T(8,128)(2,1)S(1)}, bf16[528,256]{1,0:T(8,128)(2,1)S(1)}, u32[]{:S(2)}, u32[]{:S(2)}) collective-permute-start(bf16[528,256]{1,0:T(8,128)(2,1)S(1)} %piece.1), channel_id=1, source_target_pairs={{0,192},{1,200},{2,0},{3,8},{4,128},{5,136},{6,64},{7,72},{8,240},... | collective-permute-start | bytes 811016 | tf_op jit(solution)/shard_map/ppermute | solution.py:291
  16.3 10.6 %collective-permute-start.2 = (bf16[528,256]{1,0:T(8,128)(2,1)S(1)}, bf16[528,256]{1,0:T(8,128)(2,1)S(1)}, u32[]{:S(2)}, u32[]{:S(2)}) collective-permute-start(bf16[528,256]{1,0:T(8,128)(2,1)S(1)} %collective-permute-done.p0), channel_id=1, source_target_pairs={{0,16},{16,32},{32,48},{48,0},{1,17},{17,33},{33,49},{49,1},{2,18}... | collective-permute-start | bytes 811016 | tf_op jit(solution)/shard_map/ppermute | solution.py:303
  16.6 10.5 %collective-permute-start.4 = (bf16[528,256]{1,0:T(8,128)(2,1)S(1)}, bf16[528,256]{1,0:T(8,128)(2,1)S(1)}, u32[]{:S(2)}, u32[]{:S(2)}) collective-permute-start(bf16[528,256]{1,0:T(8,128)(2,1)S(1)} %collective-permute-done.p0), channel_id=1, source_target_pairs={{0,48},{16,0},{32,16},{48,32},{1,49},{17,1},{33,17},{49,33},{2,50}... | collective-permute-start | bytes 811016 | tf_op jit(solution)/shard_map/ppermute | solution.py:304
  19.6 10.7 %collective-permute-start.1 = (bf16[528,256]{1,0:T(8,128)(2,1)S(1)}, bf16[528,256]{1,0:T(8,128)(2,1)S(1)}, u32[]{:S(2)}, u32[]{:S(2)}) collective-permute-start(bf16[528,256]{1,0:T(8,128)(2,1)S(1)} %collective-permute-done.p0), channel_id=1, source_target_pairs={{0,8},{8,0},{1,9},{9,1},{2,10},{10,2},{3,11},{11,3},{4,12},{12,4},... | collective-permute-start | bytes 811016 | tf_op jit(solution)/shard_map/ppermute | solution.py:310
  21.5 12.1 %copy-start.2 = (bf16[1024,2048]{1,0:T(8,128)(2,1)S(1)}, bf16[1024,2048]{1,0:T(8,128)(2,1)}, u32[]{:S(2)}) copy-start(bf16[1024,2048]{1,0:T(8,128)(2,1)} %get-tuple-element.34) | copy-start | bytes 12582916
  26.9 8.3 %collective-permute-start.6 = (bf16[256,256]{1,0:T(8,128)(2,1)S(1)}, bf16[256,256]{1,0:T(8,128)(2,1)S(1)}, u32[]{:S(2)}, u32[]{:S(2)}) collective-permute-start(bf16[256,256]{1,0:T(8,128)(2,1)S(1)} %slice.89), channel_id=1, source_target_pairs={{0,16},{16,32},{32,48},{48,0},{1,17},{17,33},{33,49},{49,1},{2,18}... | collective-permute-start | bytes 393224 | tf_op jit(solution)/shard_map/ppermute | solution.py:305
  27.2 8.4 %collective-permute-start.8 = (bf16[272,256]{1,0:T(8,128)(2,1)S(1)}, bf16[272,256]{1,0:T(8,128)(2,1)S(1)}, u32[]{:S(2)}, u32[]{:S(2)}) collective-permute-start(bf16[272,256]{1,0:T(8,128)(2,1)S(1)} %slice.90), channel_id=1, source_target_pairs={{0,48},{16,0},{32,16},{48,32},{1,49},{17,1},{33,17},{49,33},{2,50}... | collective-permute-start | bytes 417800 | tf_op jit(solution)/shard_map/ppermute | solution.py:306
  33.6 2.8 %copy-start.1 = (bf16[1024,2048]{1,0:T(8,128)(2,1)S(1)}, bf16[1024,2048]{1,0:T(8,128)(2,1)}, u32[]{:S(2)}) copy-start(bf16[1024,2048]{1,0:T(8,128)(2,1)} %get-tuple-element.36) | copy-start | bytes 12582916
  34.1 2.3 %collective-permute-start.3 = (bf16[528,256]{1,0:T(8,128)(2,1)S(1)}, bf16[528,256]{1,0:T(8,128)(2,1)S(1)}, u32[]{:S(2)}, u32[]{:S(2)}) collective-permute-start(bf16[528,256]{1,0:T(8,128)(2,1)S(1)} %collective-permute-done.2.p1), channel_id=1, source_target_pairs={{0,8},{8,0},{1,9},{9,1},{2,10},{10,2},{3,11},{11,3},{4,12},{12,4},... | collective-permute-start | bytes 811016 | tf_op jit(solution)/shard_map/ppermute | solution.py:310
  34.2 2.7 %collective-permute-start.5 = (bf16[528,256]{1,0:T(8,128)(2,1)S(1)}, bf16[528,256]{1,0:T(8,128)(2,1)S(1)}, u32[]{:S(2)}, u32[]{:S(2)}) collective-permute-start(bf16[528,256]{1,0:T(8,128)(2,1)S(1)} %collective-permute-done.4.p2), channel_id=1, source_target_pairs={{0,8},{8,0},{1,9},{9,1},{2,10},{10,2},{3,11},{11,3},{4,12},{12,4},... | collective-permute-start | bytes 811016 | tf_op jit(solution)/shard_map/ppermute | solution.py:310
  35.4 1.9 %collective-permute-start.7 = (bf16[256,256]{1,0:T(8,128)(2,1)S(1)}, bf16[256,256]{1,0:T(8,128)(2,1)S(1)}, u32[]{:S(2)}, u32[]{:S(2)}) collective-permute-start(bf16[256,256]{1,0:T(8,128)(2,1)S(1)} %collective-permute-done.6), channel_id=1, source_target_pairs={{0,8},{8,0},{1,9},{9,1},{2,10},{10,2},{3,11},{11,3},{4,12},{12,4},... | collective-permute-start | bytes 393224 | tf_op jit(solution)/shard_map/ppermute | solution.py:310
  35.6 2.1 %collective-permute-start.9 = (bf16[272,256]{1,0:T(8,128)(2,1)S(1)}, bf16[272,256]{1,0:T(8,128)(2,1)S(1)}, u32[]{:S(2)}, u32[]{:S(2)}) collective-permute-start(bf16[272,256]{1,0:T(8,128)(2,1)S(1)} %collective-permute-done.8.p3), channel_id=1, source_target_pairs={{0,8},{8,0},{1,9},{9,1},{2,10},{10,2},{3,11},{11,3},{4,12},{12,4},... | collective-permute-start | bytes 417800 | tf_op jit(solution)/shard_map/ppermute | solution.py:310
  37.3 13.6 %copy-start = (bf16[256,256]{1,0:T(8,128)(2,1)S(1)}, bf16[256,256]{1,0:T(8,128)(2,1)}, u32[]{:S(2)}) copy-start(bf16[256,256]{1,0:T(8,128)(2,1)} %refs_4_.1) | copy-start | bytes 393220
  68.3 2.8 %collective-permute-start.10 = (bf16[2112,256]{1,0:T(8,128)(2,1)S(1)}, bf16[2112,256]{1,0:T(8,128)(2,1)S(1)}, u32[]{:S(2)}, u32[]{:S(2)}) collective-permute-start(bf16[2112,256]{1,0:T(8,128)(2,1)S(1)} %regroup_send.1), channel_id=1, source_target_pairs={{0,8},{8,0},{1,9},{9,1},{2,10},{10,2},{3,11},{11,3},{4,12},{12,4},... | collective-permute-start | bytes 3244040 | tf_op jit(solution)/shard_map/ppermute | solution.py:337
  71.3 9.7 %collective-permute-start.11 = (bf16[256,256]{1,0:T(8,128)(2,1)S(1)}, bf16[256,256]{1,0:T(8,128)(2,1)S(1)}, u32[]{:S(2)}, u32[]{:S(2)}) collective-permute-start(bf16[256,256]{1,0:T(8,128)(2,1)S(1)} %get-tuple-element.50), channel_id=1, source_target_pairs={{0,16},{16,32},{32,48},{48,0},{1,17},{17,33},{33,49},{49,1},{2,18}... | collective-permute-start | bytes 393224 | tf_op jit(solution)/shard_map/ppermute | solution.py:346
  71.4 9.6 %collective-permute-start.12 = (bf16[256,256]{1,0:T(8,128)(2,1)S(1)}, bf16[256,256]{1,0:T(8,128)(2,1)S(1)}, u32[]{:S(2)}, u32[]{:S(2)}) collective-permute-start(bf16[256,256]{1,0:T(8,128)(2,1)S(1)} %get-tuple-element.51), channel_id=1, source_target_pairs={{0,48},{16,0},{32,16},{48,32},{1,49},{17,1},{33,17},{49,33},{2,50}... | collective-permute-start | bytes 393224 | tf_op jit(solution)/shard_map/ppermute | solution.py:346
  74.7 5.1 %collective-permute-start.13 = (bf16[64,256]{1,0:T(8,128)(2,1)S(1)}, bf16[64,256]{1,0:T(8,128)(2,1)S(1)}, u32[]{:S(2)}, u32[]{:S(2)}) collective-permute-start(bf16[64,256]{1,0:T(8,128)(2,1)S(1)} %slices.1.mine), channel_id=1, source_target_pairs={{0,16},{16,32},{32,48},{48,0},{1,17},{17,33},{33,49},{49,1},{2,18}... | collective-permute-start | bytes 98312 | tf_op jit(solution)/shard_map/ppermute | solution.py:348
  74.7 5.5 %collective-permute-start.14 = (bf16[64,256]{1,0:T(8,128)(2,1)S(1)}, bf16[64,256]{1,0:T(8,128)(2,1)S(1)}, u32[]{:S(2)}, u32[]{:S(2)}) collective-permute-start(bf16[64,256]{1,0:T(8,128)(2,1)S(1)} %slices.1.mine), channel_id=1, source_target_pairs={{0,32},{16,48},{32,0},{48,16},{1,33},{17,49},{33,1},{49,17},{2,34}... | collective-permute-start | bytes 98312 | tf_op jit(solution)/shard_map/ppermute | solution.py:348
  76.6 4.4 %collective-permute-start.15 = (bf16[64,256]{1,0:T(8,128)(2,1)S(1)}, bf16[64,256]{1,0:T(8,128)(2,1)S(1)}, u32[]{:S(2)}, u32[]{:S(2)}) collective-permute-start(bf16[64,256]{1,0:T(8,128)(2,1)S(1)} %slices.1.mine), channel_id=1, source_target_pairs={{0,48},{16,0},{32,16},{48,32},{1,49},{17,1},{33,17},{49,33},{2,50}... | collective-permute-start | bytes 98312 | tf_op jit(solution)/shard_map/ppermute | solution.py:348
  81.1 16.2 %collective-permute-start.19 = (bf16[512,256]{1,0:T(8,128)(2,1)S(1)}, bf16[512,256]{1,0:T(8,128)(2,1)S(1)}, u32[]{:S(2)}, u32[]{:S(2)}) collective-permute-start(bf16[512,256]{1,0:T(8,128)(2,1)S(1)} %get-tuple-element.55), channel_id=1, source_target_pairs={{0,16},{16,32},{32,48},{48,0},{1,17},{17,33},{33,49},{49,1},{2,18}... | collective-permute-start | bytes 786440 | tf_op jit(solution)/shard_map/ppermute | solution.py:356
  82.8 14.5 %collective-permute-start.20 = (bf16[512,256]{1,0:T(8,128)(2,1)S(1)}, bf16[512,256]{1,0:T(8,128)(2,1)S(1)}, u32[]{:S(2)}, u32[]{:S(2)}) collective-permute-start(bf16[512,256]{1,0:T(8,128)(2,1)S(1)} %get-tuple-element.56), channel_id=1, source_target_pairs={{0,48},{16,0},{32,16},{48,32},{1,49},{17,1},{33,17},{49,33},{2,50}... | collective-permute-start | bytes 786440 | tf_op jit(solution)/shard_map/ppermute | solution.py:356
  84.4 19.1 %collective-permute-start.16 = (f32[64,256]{1,0:T(8,128)S(1)}, f32[64,256]{1,0:T(8,128)S(1)}, u32[]{:S(2)}, u32[]{:S(2)}) collective-permute-start(f32[64,256]{1,0:T(8,128)S(1)} %slices_y.1.mine), channel_id=1, source_target_pairs={{0,64},{64,0},{128,192},{192,128},{1,65},{65,1},{129,193},{193,129... | collective-permute-start | bytes 196616 | tf_op jit(solution)/shard_map/ppermute | solution.py:359
  92.6 11.3 %collective-permute-start.17 = (f32[64,256]{1,0:T(8,128)S(1)}, f32[64,256]{1,0:T(8,128)S(1)}, u32[]{:S(2)}, u32[]{:S(2)}) collective-permute-start(f32[64,256]{1,0:T(8,128)S(1)} %slices_y.1.mine), channel_id=1, source_target_pairs={{0,128},{64,192},{128,0},{192,64},{1,129},{65,193},{129,1},{193,65... | collective-permute-start | bytes 196616 | tf_op jit(solution)/shard_map/ppermute | solution.py:359
  96.8 7.6 %collective-permute-start.18 = (f32[64,256]{1,0:T(8,128)S(1)}, f32[64,256]{1,0:T(8,128)S(1)}, u32[]{:S(2)}, u32[]{:S(2)}) collective-permute-start(f32[64,256]{1,0:T(8,128)S(1)} %slices_y.1.mine), channel_id=1, source_target_pairs={{0,192},{64,128},{128,64},{192,0},{1,193},{65,129},{129,65},{193,1... | collective-permute-start | bytes 196616 | tf_op jit(solution)/shard_map/ppermute | solution.py:359
  97.4 10.9 %collective-permute-start.24 = (bf16[128,256]{1,0:T(8,128)(2,1)S(1)}, bf16[128,256]{1,0:T(8,128)(2,1)S(1)}, u32[]{:S(2)}, u32[]{:S(2)}) collective-permute-start(bf16[128,256]{1,0:T(8,128)(2,1)S(1)} %get-tuple-element.57.after), channel_id=1, source_target_pairs={{0,64},{64,0},{128,192},{192,128},{1,65},{65,1},{129,193},{193,129... | collective-permute-start | bytes 196616 | tf_op jit(solution)/shard_map/ppermute | solution.py:368
  99.8 9.6 %collective-permute-start.25 = (bf16[128,256]{1,0:T(8,128)(2,1)S(1)}, bf16[128,256]{1,0:T(8,128)(2,1)S(1)}, u32[]{:S(2)}, u32[]{:S(2)}) collective-permute-start(bf16[128,256]{1,0:T(8,128)(2,1)S(1)} %get-tuple-element.59), channel_id=1, source_target_pairs={{0,128},{64,192},{128,0},{192,64},{1,129},{65,193},{129,1},{193,65... | collective-permute-start | bytes 196616 | tf_op jit(solution)/shard_map/ppermute | solution.py:368
  103.5 6.5 %collective-permute-start.26 = (bf16[128,256]{1,0:T(8,128)(2,1)S(1)}, bf16[128,256]{1,0:T(8,128)(2,1)S(1)}, u32[]{:S(2)}, u32[]{:S(2)}) collective-permute-start(bf16[128,256]{1,0:T(8,128)(2,1)S(1)} %get-tuple-element.60), channel_id=1, source_target_pairs={{0,192},{64,128},{128,64},{192,0},{1,193},{65,129},{129,65},{193,1... | collective-permute-start | bytes 196616 | tf_op jit(solution)/shard_map/ppermute | solution.py:368
  104.4 6.3 %collective-permute-start.21 = (f32[64,256]{1,0:T(8,128)S(1)}, f32[64,256]{1,0:T(8,128)S(1)}, u32[]{:S(2)}, u32[]{:S(2)}) collective-permute-start(f32[64,256]{1,0:T(8,128)S(1)} %slices_z.1.mine), channel_id=1, source_target_pairs={{0,4},{4,0},{1,5},{5,1},{2,6},{6,2},{3,7},{7,3},{8,12},{12,8},{9,1... | collective-permute-start | bytes 196616 | tf_op jit(solution)/shard_map/ppermute | solution.py:377
  106.2 4.6 %collective-permute-start.22 = (f32[64,256]{1,0:T(8,128)S(1)}, f32[64,256]{1,0:T(8,128)S(1)}, u32[]{:S(2)}, u32[]{:S(2)}) collective-permute-start(f32[64,256]{1,0:T(8,128)S(1)} %slices_z.1.mine), channel_id=1, source_target_pairs={{0,1},{1,0},{2,3},{3,2},{4,5},{5,4},{6,7},{7,6},{8,9},{9,8},{10,11... | collective-permute-start | bytes 196616 | tf_op jit(solution)/shard_map/ppermute | solution.py:378
  108.3 5.2 %collective-permute-start.23 = (f32[64,256]{1,0:T(8,128)S(1)}, f32[64,256]{1,0:T(8,128)S(1)}, u32[]{:S(2)}, u32[]{:S(2)}) collective-permute-start(f32[64,256]{1,0:T(8,128)S(1)} %slices_z.1.mine), channel_id=1, source_target_pairs={{0,5},{1,4},{2,7},{3,6},{4,1},{5,0},{6,3},{7,2},{8,13},{9,12},{10,... | collective-permute-start | bytes 196616 | tf_op jit(solution)/shard_map/ppermute | solution.py:379

commit v9 on v8

--- a/solution.py
+++ b/solution.py
@@ -345,7 +345,7 @@
     )
     up, down_ = lax.ppermute(up, "y", ahead), lax.ppermute(down_, "y", behind)
     w_rows = call(pass_body, "slices", held(WROWS), [], [w_own])
-    w_y = [lax.ppermute(w_rows, "y", ring_route(m)) for m in range(1, 4)]
+    w_y = [lax.ppermute(w_rows, "y", ring_route(m)) for m in (2, 1, 3)]
     up2, down2, w_rows = call(
         relay_body,
         "relay",

time: 115 us -> 113 us (0.983)
  starting transfers between devices: 47.1 us -> 51.3 us
  waiting for transfers between devices: 14.9 us -> 11 us
  Pallas kernels: 14.3 us -> 12.4 us
    ppermute x1, waiting for transfers between devices: 5.33 us -> 2.86 us  [shards(): first = lax.ppermute(piece, 'y', ahead)]
    ppermute x1, starting transfers between devices: 0.38 us -> 2.54 us  [shards(): first = lax.ppermute(piece, 'y', ahead)]
    pallas_call x1, Pallas kernels: 8.8 us -> 6.89 us  [assemble(): pl.pallas_call(assemble_body, out_shape=(half, half), in_specs=[SMEM] * 6...]
    ppermute x5, starting transfers between devices: 1.53 us -> 2.74 us  [shards(): other_x = lax.ppermute(own_x, 'c', swap)]
  transfers between devices with their start and end apart: 27 -> 27, of which waited for: 10 -> 8; matrix products, arithmetic and copies ran while one was open for 7% -> 7% of each run, Pallas kernels for 10% -> 8%
where the time goes in v9:
time: 113 us
  starting transfers between devices  51.3 us (45%)
  blocking collectives  28.2 us (25%)
  Pallas kernels  12.4 us (11%)
  waiting for transfers between devices  11 us (10%)
  matrix products  9.12 us (8%)
    all_to_all x1, blocking collectives, shards(): both = lax.all_to_all(both, REP, 0, 0)  15 us
    all_to_all x1, blocking collectives, shards(): parts = lax.all_to_all(partial.reshape(ZL * X, TILE, width), REP, 0, 0)  13.2 us
    ppermute x3, starting transfers between devices, shards(): w_z = [lax.ppermute(w_rows, 'zh', route) for route in exchange]  12.6 us
    pallas_call x1, Pallas kernels, assemble(): pl.pallas_call(assemble_body, out_shape=(half, half), in_specs=[SMEM] * 6...  6.89 us
    ppermute x3, starting transfers between devices, shards(): lax.ppermute(part, 'zh', route)  6.58 us
    ppermute x1, starting transfers between devices, shards(): piece = lax.ppermute(piece, ALL, piece_route())  5.79 us
    pallas_call x12, Pallas kernels, call(): pl.pallas_call(body, out_shape=outs, in_specs=[SMEM] * len(scalars) + (sp...  5.5 us
    ppermute x1, starting transfers between devices, shards(): fourth = lax.ppermute(second[HALF:], 'y', behind)  3.69 us
  transfers between devices with their start and end apart: 27, of which 8 were waited for; matrix products, arithmetic and copies ran while one was open for 7% of the time, Pallas kernels for 8%

profile of v9, /device:TPU:2, one launch (start us, length us, event | category | flops | bytes accessed | tf_op | source)
XLA Modules:
  0.0 113.0 jit_solution(11687316494518839914)
XLA Ops:
  0.6 1.0 piece.1
  1.7 5.8 %collective-permute-start = (bf16[528,256]{1,0:T(8,128)(2,1)S(1)}, bf16[528,256]{1,0:T(8,128)(2,1)S(1)}, u32[]{:S(2)}, u32[]{:S(2)}) collective-permute-start(bf16[528,256]{1,0:T(8,128)(2,1)S(1)} %piece.1), channel_id=1, source_target_pairs={{0,192},{1,200},{2,0},{3,8},{4,128},{5,136},{6,64},{7,72},{8,240},... | collective-permute-start | bytes 811016 | tf_op jit(solution)/shard_map/ppermute | solution.py:291
  7.4 6.9 %assemble.1 = (bf16[1024,2048]{1,0:T(8,128)(2,1)}, bf16[1024,2048]{1,0:T(8,128)(2,1)}) custom-call(s32[1,4]{1,0:T(1,128)} %count.1, s32[1]{0:T(128)} %bitcast.3.core, s32[1]{0:T(128)} %bitcast.1.y, s32[1]{0:T(128)S(6)} %and.23.odd.xl, s32[1,128]{1,0:T(1,128)} %row.1, s32[1,128]{1,0:T(1,128)} %col.1, bf16[1,128,128,128]{3,2,1,0:T(8,128)(2,1)} %vals.1), custom_call_target="tpu_custom_call" | custom-call | tf_op jit(solution)/shard_map/assemble/pallas_call | solution.py:147
  14.4 2.5 %collective-permute-start.2 = (bf16[528,256]{1,0:T(8,128)(2,1)S(1)}, bf16[528,256]{1,0:T(8,128)(2,1)S(1)}, u32[]{:S(2)}, u32[]{:S(2)}) collective-permute-start(bf16[528,256]{1,0:T(8,128)(2,1)S(1)} %collective-permute-done.p0), channel_id=1, source_target_pairs={{0,16},{16,32},{32,48},{48,0},{1,17},{17,33},{33,49},{49,1},{2,18}... | collective-permute-start | bytes 811016 | tf_op jit(solution)/shard_map/ppermute | solution.py:303
  16.9 3.2 %collective-permute-start.4 = (bf16[528,256]{1,0:T(8,128)(2,1)S(1)}, bf16[528,256]{1,0:T(8,128)(2,1)S(1)}, u32[]{:S(2)}, u32[]{:S(2)}) collective-permute-start(bf16[528,256]{1,0:T(8,128)(2,1)S(1)} %collective-permute-done.p0), channel_id=1, source_target_pairs={{0,48},{16,0},{32,16},{48,32},{1,49},{17,1},{33,17},{49,33},{2,50}... | collective-permute-start | bytes 811016 | tf_op jit(solution)/shard_map/ppermute | solution.py:304
  20.1 1.5 %collective-permute-start.1 = (bf16[528,256]{1,0:T(8,128)(2,1)S(1)}, bf16[528,256]{1,0:T(8,128)(2,1)S(1)}, u32[]{:S(2)}, u32[]{:S(2)}) collective-permute-start(bf16[528,256]{1,0:T(8,128)(2,1)S(1)} %collective-permute-done.p0), channel_id=1, source_target_pairs={{0,8},{8,0},{1,9},{9,1},{2,10},{10,2},{3,11},{11,3},{4,12},{12,4},... | collective-permute-start | bytes 811016 | tf_op jit(solution)/shard_map/ppermute | solution.py:310
  21.6 1.6 %share.1 = (bf16[128,256]{1,0:T(8,128)(2,1)S(1)}, bf16[128,256]{1,0:T(8,128)(2,1)S(1)}, f32[128,256]{1,0:T(8,128)S(1)}) custom-call(s32[1]{0:T(128)} %bitcast.4.replica, bf16[8,128]{1,0:T(8,128)(2,1)} %bitcast.21, bf16[1024,256]{1,0:T(8,128)(2,1)} %features.3, bf16[1024,256]{1,0:T(8,128)(2,1)} %cotangent.1), custom_call_target="tpu_custom_call" | custom-call | tf_op jit(solution)/shard_map/share/pallas_call | solution.py:65
  23.2 2.9 %collective-permute-done.2.p1 = bf16[528,256]{1,0:T(8,128)(2,1)S(1)} collective-permute-done((bf16[528,256]{1,0:T(8,128)(2,1)S(1)}, bf16[528,256]{1,0:T(8,128)(2,1)S(1)}, u32[]{:S(2)}, u32[]{:S(2)}) %collective-permute-start.2) | collective-permute-done | bytes 270368 | tf_op jit(solution)/shard_map/ppermute | solution.py:303
  26.1 0.1 collective-permute-start.6
  26.1 0.0 collective-permute-done.4.p2
  26.2 3.7 %collective-permute-start.8 = (bf16[272,256]{1,0:T(8,128)(2,1)S(1)}, bf16[272,256]{1,0:T(8,128)(2,1)S(1)}, u32[]{:S(2)}, u32[]{:S(2)}) collective-permute-start(bf16[272,256]{1,0:T(8,128)(2,1)S(1)} %slice.90), channel_id=1, source_target_pairs={{0,48},{16,0},{32,16},{48,32},{1,49},{17,1},{33,17},{49,33},{2,50}... | collective-permute-start | bytes 417800 | tf_op jit(solution)/shard_map/ppermute | solution.py:306
  29.9 0.0 collective-permute-done.1
  29.9 1.6 %fusion.9 = f32[1024,256]{1,0:T(8,128)S(1)} fusion(bf16[1024,2048]{1,0:T(8,128)(2,1)} %get-tuple-element.36, bf16[528,256]{1,0:T(8,128)(2,1)S(1)} %collective-permute-done.1), kind=kOutput, calls=%fused_computation.15 | convolution fusion | flops 268435456 | bytes 2359296 | tf_op jit(solution)/shard_map/dot_general | solution.py:314
  31.5 1.7 %convolution_add_fusion.5 = f32[1024,256]{1,0:T(8,128)S(1)} fusion(f32[1024,256]{1,0:T(8,128)S(1)} %fusion.9, bf16[1024,2048]{1,0:T(8,128)(2,1)} %get-tuple-element.34, bf16[528,256]{1,0:T(8,128)(2,1)S(1)} %collective-permute-done.p0), kind=kOutput, calls=%fused_computation.8 | convolution fusion | flops 268697600 | bytes 3407872 | tf_op jit(solution)/shard_map/dot_general | solution.py:302
  33.2 0.4 fusion.5
  33.7 0.5 collective-permute-start.3
  34.1 0.1 collective-permute-start.5
  34.3 0.4 convolution_add_fusion.4
  34.7 0.3 fusion.16
  35.0 0.5 collective-permute-start.7
  35.5 0.0 collective-permute-done.8.p3
  35.5 0.1 collective-permute-start.9
  35.6 0.3 fusion.13
  36.0 0.5 fusion.2
  36.4 0.0 collective-permute-done.5
  36.4 0.5 fusion.1
  36.9 0.0 copy-start
  36.9 0.0 collective-permute-done.7
  36.9 0.4 fusion
  37.3 0.3 fusion.3
  37.6 13.2 %all_to_all.10.refs_0_ = bf16[8,128,256]{2,1,0:T(8,128)(2,1)S(1)} all-to-all(bf16[8,128,256]{2,1,0:T(8,128)(2,1)S(1)} %bitcast.17), channel_id=1, replica_groups=mesh['zh'=4,'y'=4,'c'=2,'zl'=2,'x'=4] {'zl','x'}, dimensions={0} | all-to-all | bytes 1048576 | tf_op jit(solution)/shard_map/all_to_all | solution.py:321
  50.9 0.8 middle.1
  51.7 15.0 %all_to_all.11.both = bf16[8,192,256]{2,1,0:T(8,128)(2,1)S(1)} all-to-all(bf16[8,192,256]{2,1,0:T(8,128)(2,1)S(1)} %get-tuple-element.47), channel_id=1, replica_groups=mesh['zh'=4,'y'=4,'c'=2,'zl'=2,'x'=4] {'zl','x'}, dimensions={0} | all-to-all | bytes 1572864 | tf_op jit(solution)/shard_map/all_to_all | solution.py:329
  66.8 1.3 %fusion.27.rows = f32[2048,256]{1,0:T(8,128)S(1)} fusion(bf16[1024,2048]{1,0:T(8,128)(2,1)S(1)} %copy-done.1, bf16[1024,256]{1,0:T(8,128)(2,1)S(1)} %bitcast.18), kind=kOutput, calls=%fused_computation.33 | convolution fusion | flops 1073741824 | bytes 6815744 | tf_op jit(solution)/shard_map/dot_general | solution.py:334
  68.1 0.2 regroup_send.1
  68.3 0.1 collective-permute-start.10
  68.4 1.3 %fusion.26.rows = f32[2048,256]{1,0:T(8,128)S(1)} fusion(bf16[1024,2048]{1,0:T(8,128)(2,1)S(1)} %copy-done.2, bf16[1024,256]{1,0:T(8,128)(2,1)S(1)} %bitcast.19), kind=kOutput, calls=%fused_computation.32 | convolution fusion | flops 1073741824 | bytes 6815744 | tf_op jit(solution)/shard_map/dot_general | solution.py:334
  69.8 1.3 %collective-permute-done.10.others = bf16[2112,256]{1,0:T(8,128)(2,1)S(1)} collective-permute-done((bf16[2112,256]{1,0:T(8,128)(2,1)S(1)}, bf16[2112,256]{1,0:T(8,128)(2,1)S(1)}, u32[]{:S(2)}, u32[]{:S(2)}) %collective-permute-start.10) | collective-permute-done | bytes 1081376 | tf_op jit(solution)/shard_map/ppermute | solution.py:337
  71.1 0.2 regroup_keep.1
  71.3 0.1 collective-permute-start.11
  71.4 3.2 %collective-permute-start.12 = (bf16[256,256]{1,0:T(8,128)(2,1)S(1)}, bf16[256,256]{1,0:T(8,128)(2,1)S(1)}, u32[]{:S(2)}, u32[]{:S(2)}) collective-permute-start(bf16[256,256]{1,0:T(8,128)(2,1)S(1)} %get-tuple-element.51), channel_id=1, source_target_pairs={{0,48},{16,0},{32,16},{48,32},{1,49},{17,1},{33,17},{49,33},{2,50}... | collective-permute-start | bytes 393224 | tf_op jit(solution)/shard_map/ppermute | solution.py:346
  74.7 0.4 collective-permute-start.13
  75.0 1.4 %collective-permute-start.14 = (bf16[64,256]{1,0:T(8,128)(2,1)S(1)}, bf16[64,256]{1,0:T(8,128)(2,1)S(1)}, u32[]{:S(2)}, u32[]{:S(2)}) collective-permute-start(bf16[64,256]{1,0:T(8,128)(2,1)S(1)} %slices.1.mine), channel_id=1, source_target_pairs={{0,16},{16,32},{32,48},{48,0},{1,17},{17,33},{33,49},{49,1},{2,18}... | collective-permute-start | bytes 98312 | tf_op jit(solution)/shard_map/ppermute | solution.py:348
  76.4 1.8 %collective-permute-start.15 = (bf16[64,256]{1,0:T(8,128)(2,1)S(1)}, bf16[64,256]{1,0:T(8,128)(2,1)S(1)}, u32[]{:S(2)}, u32[]{:S(2)}) collective-permute-start(bf16[64,256]{1,0:T(8,128)(2,1)S(1)} %slices.1.mine), channel_id=1, source_target_pairs={{0,48},{16,0},{32,16},{48,32},{1,49},{17,1},{33,17},{49,33},{2,50}... | collective-permute-start | bytes 98312 | tf_op jit(solution)/shard_map/ppermute | solution.py:348
  78.3 1.8 %collective-permute-done.13.came1 = bf16[64,256]{1,0:T(8,128)(2,1)S(1)} collective-permute-done((bf16[64,256]{1,0:T(8,128)(2,1)S(1)}, bf16[64,256]{1,0:T(8,128)(2,1)S(1)}, u32[]{:S(2)}, u32[]{:S(2)}) %collective-permute-start.13) | collective-permute-done | bytes 32800 | tf_op jit(solution)/shard_map/ppermute | solution.py:348
  80.1 0.3 collective-permute-done.14.came2
  80.4 0.1 relay.1
  80.5 1.7 %collective-permute-start.19 = (bf16[512,256]{1,0:T(8,128)(2,1)S(1)}, bf16[512,256]{1,0:T(8,128)(2,1)S(1)}, u32[]{:S(2)}, u32[]{:S(2)}) collective-permute-start(bf16[512,256]{1,0:T(8,128)(2,1)S(1)} %get-tuple-element.55), channel_id=1, source_target_pairs={{0,16},{16,32},{32,48},{48,0},{1,17},{17,33},{33,49},{49,1},{2,18}... | collective-permute-start | bytes 786440 | tf_op jit(solution)/shard_map/ppermute | solution.py:356
  82.2 1.6 %collective-permute-start.20 = (bf16[512,256]{1,0:T(8,128)(2,1)S(1)}, bf16[512,256]{1,0:T(8,128)(2,1)S(1)}, u32[]{:S(2)}, u32[]{:S(2)}) collective-permute-start(bf16[512,256]{1,0:T(8,128)(2,1)S(1)} %get-tuple-element.56), channel_id=1, source_target_pairs={{0,48},{16,0},{32,16},{48,32},{1,49},{17,1},{33,17},{49,33},{2,50}... | collective-permute-start | bytes 786440 | tf_op jit(solution)/shard_map/ppermute | solution.py:356
  83.8 8.0 %collective-permute-start.16 = (f32[64,256]{1,0:T(8,128)S(1)}, f32[64,256]{1,0:T(8,128)S(1)}, u32[]{:S(2)}, u32[]{:S(2)}) collective-permute-start(f32[64,256]{1,0:T(8,128)S(1)} %slices_y.1.mine), channel_id=1, source_target_pairs={{0,64},{64,0},{128,192},{192,128},{1,65},{65,1},{129,193},{193,129... | collective-permute-start | bytes 196616 | tf_op jit(solution)/shard_map/ppermute | solution.py:359
  91.8 4.2 %collective-permute-start.17 = (f32[64,256]{1,0:T(8,128)S(1)}, f32[64,256]{1,0:T(8,128)S(1)}, u32[]{:S(2)}, u32[]{:S(2)}) collective-permute-start(f32[64,256]{1,0:T(8,128)S(1)} %slices_y.1.mine), channel_id=1, source_target_pairs={{0,128},{64,192},{128,0},{192,64},{1,129},{65,193},{129,1},{193,65... | collective-permute-start | bytes 196616 | tf_op jit(solution)/shard_map/ppermute | solution.py:359
  96.0 0.5 collective-permute-start.18
  96.4 0.1 spread.1
  96.5 2.5 %collective-permute-start.24 = (bf16[128,256]{1,0:T(8,128)(2,1)S(1)}, bf16[128,256]{1,0:T(8,128)(2,1)S(1)}, u32[]{:S(2)}, u32[]{:S(2)}) collective-permute-start(bf16[128,256]{1,0:T(8,128)(2,1)S(1)} %get-tuple-element.57.after), channel_id=1, source_target_pairs={{0,64},{64,0},{128,192},{192,128},{1,65},{65,1},{129,193},{193,129... | collective-permute-start | bytes 196616 | tf_op jit(solution)/shard_map/ppermute | solution.py:368
  99.0 3.7 %collective-permute-start.25 = (bf16[128,256]{1,0:T(8,128)(2,1)S(1)}, bf16[128,256]{1,0:T(8,128)(2,1)S(1)}, u32[]{:S(2)}, u32[]{:S(2)}) collective-permute-start(bf16[128,256]{1,0:T(8,128)(2,1)S(1)} %get-tuple-element.59), channel_id=1, source_target_pairs={{0,128},{64,192},{128,0},{192,64},{1,129},{65,193},{129,1},{193,65... | collective-permute-start | bytes 196616 | tf_op jit(solution)/shard_map/ppermute | solution.py:368
  102.7 0.5 collective-permute-start.26
  103.1 0.2 collective-permute-done.18.came3
  103.3 1.8 %collective-permute-start.21 = (f32[64,256]{1,0:T(8,128)S(1)}, f32[64,256]{1,0:T(8,128)S(1)}, u32[]{:S(2)}, u32[]{:S(2)}) collective-permute-start(f32[64,256]{1,0:T(8,128)S(1)} %slices_z.1.mine), channel_id=1, source_target_pairs={{0,4},{4,0},{1,5},{5,1},{2,6},{6,2},{3,7},{7,3},{8,12},{12,8},{9,1... | collective-permute-start | bytes 196616 | tf_op jit(solution)/shard_map/ppermute | solution.py:377
  105.1 2.0 %collective-permute-start.22 = (f32[64,256]{1,0:T(8,128)S(1)}, f32[64,256]{1,0:T(8,128)S(1)}, u32[]{:S(2)}, u32[]{:S(2)}) collective-permute-start(f32[64,256]{1,0:T(8,128)S(1)} %slices_z.1.mine), channel_id=1, source_target_pairs={{0,1},{1,0},{2,3},{3,2},{4,5},{5,4},{6,7},{7,6},{8,9},{9,8},{10,11... | collective-permute-start | bytes 196616 | tf_op jit(solution)/shard_map/ppermute | solution.py:378
  107.1 1.4 %collective-permute-done.25.came2 = bf16[128,256]{1,0:T(8,128)(2,1)S(1)} collective-permute-done((bf16[128,256]{1,0:T(8,128)(2,1)S(1)}, bf16[128,256]{1,0:T(8,128)(2,1)S(1)}, u32[]{:S(2)}, u32[]{:S(2)}) %collective-permute-start.25) | collective-permute-done | bytes 65568 | tf_op jit(solution)/shard_map/ppermute | solution.py:368
  108.5 1.3 %collective-permute-done.26.came3 = bf16[128,256]{1,0:T(8,128)(2,1)S(1)} collective-permute-done((bf16[128,256]{1,0:T(8,128)(2,1)S(1)}, bf16[128,256]{1,0:T(8,128)(2,1)S(1)}, u32[]{:S(2)}, u32[]{:S(2)}) %collective-permute-start.26) | collective-permute-done | bytes 65568 | tf_op jit(solution)/shard_map/ppermute | solution.py:368
  109.7 0.7 last.1
  110.5 1.8 %collective-permute-done.23.over_both = f32[64,256]{1,0:T(8,128)S(1)} collective-permute-done((f32[64,256]{1,0:T(8,128)S(1)}, f32[64,256]{1,0:T(8,128)S(1)}, u32[]{:S(2)}, u32[]{:S(2)}) %collective-permute-start.23) | collective-permute-done | bytes 65568 | tf_op jit(solution)/shard_map/ppermute | solution.py:379
  112.3 0.7 join.1
  (26 shorter events, 0.1 us)
Async XLA Ops:
  1.7 12.7 %collective-permute-start = (bf16[528,256]{1,0:T(8,128)(2,1)S(1)}, bf16[528,256]{1,0:T(8,128)(2,1)S(1)}, u32[]{:S(2)}, u32[]{:S(2)}) collective-permute-start(bf16[528,256]{1,0:T(8,128)(2,1)S(1)} %piece.1), channel_id=1, source_target_pairs={{0,192},{1,200},{2,0},{3,8},{4,128},{5,136},{6,64},{7,72},{8,240},... | collective-permute-start | bytes 811016 | tf_op jit(solution)/shard_map/ppermute | solution.py:291
  14.4 11.7 %collective-permute-start.2 = (bf16[528,256]{1,0:T(8,128)(2,1)S(1)}, bf16[528,256]{1,0:T(8,128)(2,1)S(1)}, u32[]{:S(2)}, u32[]{:S(2)}) collective-permute-start(bf16[528,256]{1,0:T(8,128)(2,1)S(1)} %collective-permute-done.p0), channel_id=1, source_target_pairs={{0,16},{16,32},{32,48},{48,0},{1,17},{17,33},{33,49},{49,1},{2,18}... | collective-permute-start | bytes 811016 | tf_op jit(solution)/shard_map/ppermute | solution.py:303
  16.9 9.3 %collective-permute-start.4 = (bf16[528,256]{1,0:T(8,128)(2,1)S(1)}, bf16[528,256]{1,0:T(8,128)(2,1)S(1)}, u32[]{:S(2)}, u32[]{:S(2)}) collective-permute-start(bf16[528,256]{1,0:T(8,128)(2,1)S(1)} %collective-permute-done.p0), channel_id=1, source_target_pairs={{0,48},{16,0},{32,16},{48,32},{1,49},{17,1},{33,17},{49,33},{2,50}... | collective-permute-start | bytes 811016 | tf_op jit(solution)/shard_map/ppermute | solution.py:304
  20.1 9.8 %collective-permute-start.1 = (bf16[528,256]{1,0:T(8,128)(2,1)S(1)}, bf16[528,256]{1,0:T(8,128)(2,1)S(1)}, u32[]{:S(2)}, u32[]{:S(2)}) collective-permute-start(bf16[528,256]{1,0:T(8,128)(2,1)S(1)} %collective-permute-done.p0), channel_id=1, source_target_pairs={{0,8},{8,0},{1,9},{9,1},{2,10},{10,2},{3,11},{11,3},{4,12},{12,4},... | collective-permute-start | bytes 811016 | tf_op jit(solution)/shard_map/ppermute | solution.py:310
  23.2 10.0 %copy-start.2 = (bf16[1024,2048]{1,0:T(8,128)(2,1)S(1)}, bf16[1024,2048]{1,0:T(8,128)(2,1)}, u32[]{:S(2)}) copy-start(bf16[1024,2048]{1,0:T(8,128)(2,1)} %get-tuple-element.34) | copy-start | bytes 12582916
  26.1 8.7 %collective-permute-start.6 = (bf16[256,256]{1,0:T(8,128)(2,1)S(1)}, bf16[256,256]{1,0:T(8,128)(2,1)S(1)}, u32[]{:S(2)}, u32[]{:S(2)}) collective-permute-start(bf16[256,256]{1,0:T(8,128)(2,1)S(1)} %slice.89), channel_id=1, source_target_pairs={{0,16},{16,32},{32,48},{48,0},{1,17},{17,33},{33,49},{49,1},{2,18}... | collective-permute-start | bytes 393224 | tf_op jit(solution)/shard_map/ppermute | solution.py:305
  26.2 9.3 %collective-permute-start.8 = (bf16[272,256]{1,0:T(8,128)(2,1)S(1)}, bf16[272,256]{1,0:T(8,128)(2,1)S(1)}, u32[]{:S(2)}, u32[]{:S(2)}) collective-permute-start(bf16[272,256]{1,0:T(8,128)(2,1)S(1)} %slice.90), channel_id=1, source_target_pairs={{0,48},{16,0},{32,16},{48,32},{1,49},{17,1},{33,17},{49,33},{2,50}... | collective-permute-start | bytes 417800 | tf_op jit(solution)/shard_map/ppermute | solution.py:306
  33.2 2.8 %copy-start.1 = (bf16[1024,2048]{1,0:T(8,128)(2,1)S(1)}, bf16[1024,2048]{1,0:T(8,128)(2,1)}, u32[]{:S(2)}) copy-start(bf16[1024,2048]{1,0:T(8,128)(2,1)} %get-tuple-element.36) | copy-start | bytes 12582916
  33.7 2.3 %collective-permute-start.3 = (bf16[528,256]{1,0:T(8,128)(2,1)S(1)}, bf16[528,256]{1,0:T(8,128)(2,1)S(1)}, u32[]{:S(2)}, u32[]{:S(2)}) collective-permute-start(bf16[528,256]{1,0:T(8,128)(2,1)S(1)} %collective-permute-done.2.p1), channel_id=1, source_target_pairs={{0,8},{8,0},{1,9},{9,1},{2,10},{10,2},{3,11},{11,3},{4,12},{12,4},... | collective-permute-start | bytes 811016 | tf_op jit(solution)/shard_map/ppermute | solution.py:310
  34.1 2.3 %collective-permute-start.5 = (bf16[528,256]{1,0:T(8,128)(2,1)S(1)}, bf16[528,256]{1,0:T(8,128)(2,1)S(1)}, u32[]{:S(2)}, u32[]{:S(2)}) collective-permute-start(bf16[528,256]{1,0:T(8,128)(2,1)S(1)} %collective-permute-done.4.p2), channel_id=1, source_target_pairs={{0,8},{8,0},{1,9},{9,1},{2,10},{10,2},{3,11},{11,3},{4,12},{12,4},... | collective-permute-start | bytes 811016 | tf_op jit(solution)/shard_map/ppermute | solution.py:310
  35.0 1.9 %collective-permute-start.7 = (bf16[256,256]{1,0:T(8,128)(2,1)S(1)}, bf16[256,256]{1,0:T(8,128)(2,1)S(1)}, u32[]{:S(2)}, u32[]{:S(2)}) collective-permute-start(bf16[256,256]{1,0:T(8,128)(2,1)S(1)} %collective-permute-done.6), channel_id=1, source_target_pairs={{0,8},{8,0},{1,9},{9,1},{2,10},{10,2},{3,11},{11,3},{4,12},{12,4},... | collective-permute-start | bytes 393224 | tf_op jit(solution)/shard_map/ppermute | solution.py:310
  35.5 1.8 %collective-permute-start.9 = (bf16[272,256]{1,0:T(8,128)(2,1)S(1)}, bf16[272,256]{1,0:T(8,128)(2,1)S(1)}, u32[]{:S(2)}, u32[]{:S(2)}) collective-permute-start(bf16[272,256]{1,0:T(8,128)(2,1)S(1)} %collective-permute-done.8.p3), channel_id=1, source_target_pairs={{0,8},{8,0},{1,9},{9,1},{2,10},{10,2},{3,11},{11,3},{4,12},{12,4},... | collective-permute-start | bytes 417800 | tf_op jit(solution)/shard_map/ppermute | solution.py:310
  36.9 14.0 %copy-start = (bf16[256,256]{1,0:T(8,128)(2,1)S(1)}, bf16[256,256]{1,0:T(8,128)(2,1)}, u32[]{:S(2)}) copy-start(bf16[256,256]{1,0:T(8,128)(2,1)} %refs_4_.1) | copy-start | bytes 393220
  68.3 2.8 %collective-permute-start.10 = (bf16[2112,256]{1,0:T(8,128)(2,1)S(1)}, bf16[2112,256]{1,0:T(8,128)(2,1)S(1)}, u32[]{:S(2)}, u32[]{:S(2)}) collective-permute-start(bf16[2112,256]{1,0:T(8,128)(2,1)S(1)} %regroup_send.1), channel_id=1, source_target_pairs={{0,8},{8,0},{1,9},{9,1},{2,10},{10,2},{3,11},{11,3},{4,12},{12,4},... | collective-permute-start | bytes 3244040 | tf_op jit(solution)/shard_map/ppermute | solution.py:337
  71.3 9.1 %collective-permute-start.11 = (bf16[256,256]{1,0:T(8,128)(2,1)S(1)}, bf16[256,256]{1,0:T(8,128)(2,1)S(1)}, u32[]{:S(2)}, u32[]{:S(2)}) collective-permute-start(bf16[256,256]{1,0:T(8,128)(2,1)S(1)} %get-tuple-element.50), channel_id=1, source_target_pairs={{0,16},{16,32},{32,48},{48,0},{1,17},{17,33},{33,49},{49,1},{2,18}... | collective-permute-start | bytes 393224 | tf_op jit(solution)/shard_map/ppermute | solution.py:346
  71.4 9.0 %collective-permute-start.12 = (bf16[256,256]{1,0:T(8,128)(2,1)S(1)}, bf16[256,256]{1,0:T(8,128)(2,1)S(1)}, u32[]{:S(2)}, u32[]{:S(2)}) collective-permute-start(bf16[256,256]{1,0:T(8,128)(2,1)S(1)} %get-tuple-element.51), channel_id=1, source_target_pairs={{0,48},{16,0},{32,16},{48,32},{1,49},{17,1},{33,17},{49,33},{2,50}... | collective-permute-start | bytes 393224 | tf_op jit(solution)/shard_map/ppermute | solution.py:346
  74.7 5.4 %collective-permute-start.13 = (bf16[64,256]{1,0:T(8,128)(2,1)S(1)}, bf16[64,256]{1,0:T(8,128)(2,1)S(1)}, u32[]{:S(2)}, u32[]{:S(2)}) collective-permute-start(bf16[64,256]{1,0:T(8,128)(2,1)S(1)} %slices.1.mine), channel_id=1, source_target_pairs={{0,32},{16,48},{32,0},{48,16},{1,33},{17,49},{33,1},{49,17},{2,34}... | collective-permute-start | bytes 98312 | tf_op jit(solution)/shard_map/ppermute | solution.py:348
  75.0 5.4 %collective-permute-start.14 = (bf16[64,256]{1,0:T(8,128)(2,1)S(1)}, bf16[64,256]{1,0:T(8,128)(2,1)S(1)}, u32[]{:S(2)}, u32[]{:S(2)}) collective-permute-start(bf16[64,256]{1,0:T(8,128)(2,1)S(1)} %slices.1.mine), channel_id=1, source_target_pairs={{0,16},{16,32},{32,48},{48,0},{1,17},{17,33},{33,49},{49,1},{2,18}... | collective-permute-start | bytes 98312 | tf_op jit(solution)/shard_map/ppermute | solution.py:348
  76.4 4.0 %collective-permute-start.15 = (bf16[64,256]{1,0:T(8,128)(2,1)S(1)}, bf16[64,256]{1,0:T(8,128)(2,1)S(1)}, u32[]{:S(2)}, u32[]{:S(2)}) collective-permute-start(bf16[64,256]{1,0:T(8,128)(2,1)S(1)} %slices.1.mine), channel_id=1, source_target_pairs={{0,48},{16,0},{32,16},{48,32},{1,49},{17,1},{33,17},{49,33},{2,50}... | collective-permute-start | bytes 98312 | tf_op jit(solution)/shard_map/ppermute | solution.py:348
  80.5 15.9 %collective-permute-start.19 = (bf16[512,256]{1,0:T(8,128)(2,1)S(1)}, bf16[512,256]{1,0:T(8,128)(2,1)S(1)}, u32[]{:S(2)}, u32[]{:S(2)}) collective-permute-start(bf16[512,256]{1,0:T(8,128)(2,1)S(1)} %get-tuple-element.55), channel_id=1, source_target_pairs={{0,16},{16,32},{32,48},{48,0},{1,17},{17,33},{33,49},{49,1},{2,18}... | collective-permute-start | bytes 786440 | tf_op jit(solution)/shard_map/ppermute | solution.py:356
  82.2 14.2 %collective-permute-start.20 = (bf16[512,256]{1,0:T(8,128)(2,1)S(1)}, bf16[512,256]{1,0:T(8,128)(2,1)S(1)}, u32[]{:S(2)}, u32[]{:S(2)}) collective-permute-start(bf16[512,256]{1,0:T(8,128)(2,1)S(1)} %get-tuple-element.56), channel_id=1, source_target_pairs={{0,48},{16,0},{32,16},{48,32},{1,49},{17,1},{33,17},{49,33},{2,50}... | collective-permute-start | bytes 786440 | tf_op jit(solution)/shard_map/ppermute | solution.py:356
  83.8 18.8 %collective-permute-start.16 = (f32[64,256]{1,0:T(8,128)S(1)}, f32[64,256]{1,0:T(8,128)S(1)}, u32[]{:S(2)}, u32[]{:S(2)}) collective-permute-start(f32[64,256]{1,0:T(8,128)S(1)} %slices_y.1.mine), channel_id=1, source_target_pairs={{0,64},{64,0},{128,192},{192,128},{1,65},{65,1},{129,193},{193,129... | collective-permute-start | bytes 196616 | tf_op jit(solution)/shard_map/ppermute | solution.py:359
  91.8 11.3 %collective-permute-start.17 = (f32[64,256]{1,0:T(8,128)S(1)}, f32[64,256]{1,0:T(8,128)S(1)}, u32[]{:S(2)}, u32[]{:S(2)}) collective-permute-start(f32[64,256]{1,0:T(8,128)S(1)} %slices_y.1.mine), channel_id=1, source_target_pairs={{0,128},{64,192},{128,0},{192,64},{1,129},{65,193},{129,1},{193,65... | collective-permute-start | bytes 196616 | tf_op jit(solution)/shard_map/ppermute | solution.py:359
  96.0 7.3 %collective-permute-start.18 = (f32[64,256]{1,0:T(8,128)S(1)}, f32[64,256]{1,0:T(8,128)S(1)}, u32[]{:S(2)}, u32[]{:S(2)}) collective-permute-start(f32[64,256]{1,0:T(8,128)S(1)} %slices_y.1.mine), channel_id=1, source_target_pairs={{0,192},{64,128},{128,64},{192,0},{1,193},{65,129},{129,65},{193,1... | collective-permute-start | bytes 196616 | tf_op jit(solution)/shard_map/ppermute | solution.py:359
  96.5 10.6 %collective-permute-start.24 = (bf16[128,256]{1,0:T(8,128)(2,1)S(1)}, bf16[128,256]{1,0:T(8,128)(2,1)S(1)}, u32[]{:S(2)}, u32[]{:S(2)}) collective-permute-start(bf16[128,256]{1,0:T(8,128)(2,1)S(1)} %get-tuple-element.57.after), channel_id=1, source_target_pairs={{0,64},{64,0},{128,192},{192,128},{1,65},{65,1},{129,193},{193,129... | collective-permute-start | bytes 196616 | tf_op jit(solution)/shard_map/ppermute | solution.py:368
  99.0 9.5 %collective-permute-start.25 = (bf16[128,256]{1,0:T(8,128)(2,1)S(1)}, bf16[128,256]{1,0:T(8,128)(2,1)S(1)}, u32[]{:S(2)}, u32[]{:S(2)}) collective-permute-start(bf16[128,256]{1,0:T(8,128)(2,1)S(1)} %get-tuple-element.59), channel_id=1, source_target_pairs={{0,128},{64,192},{128,0},{192,64},{1,129},{65,193},{129,1},{193,65... | collective-permute-start | bytes 196616 | tf_op jit(solution)/shard_map/ppermute | solution.py:368
  102.7 7.1 %collective-permute-start.26 = (bf16[128,256]{1,0:T(8,128)(2,1)S(1)}, bf16[128,256]{1,0:T(8,128)(2,1)S(1)}, u32[]{:S(2)}, u32[]{:S(2)}) collective-permute-start(bf16[128,256]{1,0:T(8,128)(2,1)S(1)} %get-tuple-element.60), channel_id=1, source_target_pairs={{0,192},{64,128},{128,64},{192,0},{1,193},{65,129},{129,65},{193,1... | collective-permute-start | bytes 196616 | tf_op jit(solution)/shard_map/ppermute | solution.py:368
  103.3 7.2 %collective-permute-start.21 = (f32[64,256]{1,0:T(8,128)S(1)}, f32[64,256]{1,0:T(8,128)S(1)}, u32[]{:S(2)}, u32[]{:S(2)}) collective-permute-start(f32[64,256]{1,0:T(8,128)S(1)} %slices_z.1.mine), channel_id=1, source_target_pairs={{0,4},{4,0},{1,5},{5,1},{2,6},{6,2},{3,7},{7,3},{8,12},{12,8},{9,1... | collective-permute-start | bytes 196616 | tf_op jit(solution)/shard_map/ppermute | solution.py:377
  105.1 5.4 %collective-permute-start.22 = (f32[64,256]{1,0:T(8,128)S(1)}, f32[64,256]{1,0:T(8,128)S(1)}, u32[]{:S(2)}, u32[]{:S(2)}) collective-permute-start(f32[64,256]{1,0:T(8,128)S(1)} %slices_z.1.mine), channel_id=1, source_target_pairs={{0,1},{1,0},{2,3},{3,2},{4,5},{5,4},{6,7},{7,6},{8,9},{9,8},{10,11... | collective-permute-start | bytes 196616 | tf_op jit(solution)/shard_map/ppermute | solution.py:378
  107.1 5.2 %collective-permute-start.23 = (f32[64,256]{1,0:T(8,128)S(1)}, f32[64,256]{1,0:T(8,128)S(1)}, u32[]{:S(2)}, u32[]{:S(2)}) collective-permute-start(f32[64,256]{1,0:T(8,128)S(1)} %slices_z.1.mine), channel_id=1, source_target_pairs={{0,5},{1,4},{2,7},{3,6},{4,1},{5,0},{6,3},{7,2},{8,13},{9,12},{10,... | collective-permute-start | bytes 196616 | tf_op jit(solution)/shard_map/ppermute | solution.py:379
